TPU v7x, 128 devices: a whole 4x4x4 slice. The times are simulated.
128 devices in a mesh: node: 8 (over y, core), tm: 16 (over x, z).
Axes of the slice: x: 4, y: 4, z: 4, core: 2. Of those that a mesh axis runs over, the one named last changes fastest.
Arguments:
- memory: bfloat16 [131072, 1024], P(('node', 'tm')), may hold values from -6 to 6
- ends_owner: int32 [32768, 2], P(('node', 'tm')), may hold values from 0 to 127, all different within a row; in each aligned block of 256 rows (0 to 255, 256 to 511, ...) at most 5 rows name the same one
- ends_row: int32 [32768, 2], P(('node', 'tm')), may hold values from 0 to 1023
- event_mask: int32 [32768], P(('node', 'tm')), may hold values 0 or 1
- edge_feat: bfloat16 [32768, 128], P(('node', 'tm')), may hold values from -6 to 6
- msg_w1: bfloat16 [2176, 1024], replicated, may hold values from -0.125 to 0.125
- msg_b1: float32 [1024], replicated, may hold values from -4 to 4
- msg_w2: bfloat16 [1024, 1024], replicated, may hold values from -0.1875 to 0.1875
- msg_b2: float32 [1024], replicated, may hold values from -3 to 3
- gru_in: bfloat16 [1024, 3072], replicated, may hold values from -0.1875 to 0.1875
- gru_hid: bfloat16 [1024, 3072], replicated, may hold values from -0.1875 to 0.1875
- gru_bias: float32 [3072], replicated, may hold values from -3 to 3
Outputs:
- new_memory: bfloat16 [131072, 1024], P(('node', 'tm'))
Inputs may be any that keep to these rules, and one draw needn't show every extreme that they name: `ends_owner`: within the events of one device (aligned blocks of 256 rows) no device is named by more than 5 endpoints, and some device by exactly 5; an event's two endpoints have different owners.
All inputs are finite; a program needn't handle non-finite values. No bound on the sum of `event_mask` on one device may be relied on, other than what follows from the above.
Results may differ from a plain program's by a relative error of at most 0.0026.
Values may be sent and summed in bfloat16 or wider, within the bound.
No kernel may reach another device: no remote copies, remote signals or barrier semaphores. Data moves between devices by JAX's collectives and lax.ppermute only.
A program may use at most 128 MiB of HBM per device.

v0:
```python
import jax
import jax.numpy as jnp
from jax import lax
from jax.sharding import PartitionSpec as P


def memory_update(aggregate, memory, gru_in, gru_hid, gru_bias, touched):
    feature_width = memory.shape[1]
    gates_in = jnp.dot(aggregate, gru_in, preferred_element_type=jnp.float32) + gru_bias
    gates_hid = jnp.dot(memory, gru_hid, preferred_element_type=jnp.float32)
    reset = jax.nn.sigmoid(gates_in[:, :feature_width] + gates_hid[:, :feature_width])
    update = jax.nn.sigmoid(
        gates_in[:, feature_width : 2 * feature_width]
        + gates_hid[:, feature_width : 2 * feature_width]
    )
    candidate = jnp.tanh(
        gates_in[:, 2 * feature_width :] + reset * gates_hid[:, 2 * feature_width :]
    )
    previous = memory.astype(jnp.float32)
    renewed = (1.0 - update) * candidate + update * previous
    return jnp.where(touched[:, None], renewed, previous).astype(jnp.bfloat16)


def on_device(
    memory,
    ends_owner,
    ends_row,
    event_mask,
    edge_feat,
    msg_w1,
    msg_b1,
    msg_w2,
    msg_b2,
    gru_in,
    gru_hid,
    gru_bias,
):
    devices = lax.axis_size(("node", "tm"))
    events = ends_owner.shape[0]
    feature_width = memory.shape[1]
    capacity = 5 * events // (2 * devices)
    slot_count = devices * capacity
    owners = ends_owner.reshape(-1)
    wanted = ends_row.reshape(-1)
    onehot = (owners[:, None] == jnp.arange(devices, dtype=jnp.int32)[None, :]).astype(jnp.int32)
    position = jnp.sum((jnp.cumsum(onehot, axis=0) - 1) * onehot, axis=1)
    location = owners * capacity + position
    requests = (
        jnp.zeros((slot_count,), jnp.int32).at[location].set(wanted).reshape(devices, capacity)
    )
    arrived = lax.all_to_all(requests, ("node", "tm"), split_axis=0, concat_axis=0, tiled=True)
    flat_ids = arrived.reshape(-1)
    answers = jnp.take(memory, flat_ids, axis=0)
    returned = lax.all_to_all(
        answers.reshape(devices, capacity, feature_width),
        ("node", "tm"),
        split_axis=0,
        concat_axis=0,
        tiled=True,
    )
    fetched = jnp.take(returned.reshape(slot_count, feature_width), location, axis=0).reshape(
        events, 2 * feature_width
    )
    inputs = jnp.concatenate([fetched, edge_feat], axis=1)
    hidden = jax.nn.relu(
        jnp.dot(inputs, msg_w1, preferred_element_type=jnp.float32) + msg_b1
    ).astype(jnp.bfloat16)
    weight_mask = event_mask.astype(jnp.float32)
    message = (
        (jnp.dot(hidden, msg_w2, preferred_element_type=jnp.float32) + msg_b2)
        * weight_mask[:, None]
    ).astype(jnp.bfloat16)
    target = location.reshape(events, 2)[:, 1]
    outgoing = jnp.zeros((slot_count, feature_width), jnp.bfloat16).at[target].set(message)
    tallies = jnp.zeros((slot_count,), jnp.bfloat16).at[target].set(event_mask.astype(jnp.bfloat16))
    incoming, counted = (
        lax.all_to_all(
            outgoing.reshape(devices, capacity, feature_width),
            ("node", "tm"),
            split_axis=0,
            concat_axis=0,
            tiled=True,
        ),
        lax.all_to_all(
            tallies.reshape(devices, capacity),
            ("node", "tm"),
            split_axis=0,
            concat_axis=0,
            tiled=True,
        ),
    )
    mates = (flat_ids[:, None] == flat_ids[None, :]).astype(jnp.bfloat16)
    summed = jnp.dot(
        mates, incoming.reshape(slot_count, feature_width), preferred_element_type=jnp.float32
    )
    tally_sum = jnp.dot(mates, counted.reshape(slot_count), preferred_element_type=jnp.float32)
    aggregate = (summed / jnp.maximum(tally_sum, 1.0)[:, None]).astype(jnp.bfloat16)
    renewed = memory_update(aggregate, answers, gru_in, gru_hid, gru_bias, tally_sum > 0.5)
    return memory.at[flat_ids].set(renewed)


def solution(mesh):
    return jax.shard_map(
        on_device,
        mesh=mesh,
        in_specs=(
            P(("node", "tm"), None),
            P(("node", "tm"), None),
            P(("node", "tm"), None),
            P(("node", "tm")),
            P(("node", "tm"), None),
            P(),
            P(),
            P(),
            P(),
            P(),
            P(),
            P(),
        ),
        out_specs=P(("node", "tm"), None),
        check_vma=False,
    )
```

profile of v0, /device:TPU:0, one launch (start us, length us, event | category | flops | bytes accessed | tf_op | source)
XLA Modules:
  0.0 172.5 jit_solution(12859606560121275107)
XLA Ops:
  0.0 3.2 %copy.56 = bf16[1024,1024]{1,0:T(8,128)(2,1)} copy(bf16[1024,1024]{1,0:T(8,128)(2,1)} %param.12) | data formatting | bytes 4194304
  3.2 0.1 copy.44
  3.4 0.1 eq.46
  3.5 0.1 eq.42
  3.7 0.1 copy.43
  3.8 0.1 mul.42
  4.0 0.1 copy.46
  4.1 0.1 copy.48
  4.2 0.1 reshape.169
  4.4 0.2 fusion.47
  4.6 0.1 add_add_fusion
  4.7 0.2 fusion.46
  5.0 2.4 %scatter_custom_fusion = s32[640]{0:T(1024)S(1)} fusion(s32[512]{0:T(512)S(1)} %bitcast.29, s32[512]{0:T(512)S(1)} %reshape.169, s32[]{:T(128)} %constant.18.clone.1), kind=kCustom, calls=%fused_computation.76 | custom fusion | bytes 2564 | tf_op jit(solution)/shard_map/scatter | solution.py:49
  7.4 0.8 all_to_all.18
  8.3 11.1 %all-to-all-start = ((s32[128,1,5]{2,1,0:T(1,128)}), s32[128,1,5]{2,1,0:T(1,128)S(1)}, u32[]{:S(2)}, u32[]{:S(2)}) async-start(s32[128,1,5]{2,1,0:T(1,128)} %bitcast.5), calls=%async_computation | async-start | bytes 131072 | tf_op jit(solution)/shard_map/all_to_all | solution.py:51
  19.4 0.1 reduce_sum.15
  19.6 0.1 copy.50
  19.6 0.6 compare_and_fusion.2
  20.2 0.0 copy-done.11
  20.2 0.6 fusion.61
  20.8 2.2 %scatter_custom_fusion.1 = bf16[640]{0:T(1024)(128)(2,1)S(1)} fusion(s32[256]{0:T(256)S(1)} %bitcast.31, bf16[256]{0:T(256)(128)(2,1)S(1)} %get-tuple-element.7, bf16[]{:T(256)} %constant.29.clone.1), kind=kCustom, calls=%fused_computation.78 | custom fusion | bytes 1282 | tf_op jit(solution)/shard_map/scatter | solution.py:75
  22.9 0.9 all_to_all.24
  23.8 5.0 %all-to-all-done = s32[128,1,5]{2,1,0:T(1,128)S(1)} async-done(((s32[128,1,5]{2,1,0:T(1,128)}), s32[128,1,5]{2,1,0:T(1,128)S(1)}, u32[]{:S(2)}, u32[]{:S(2)}) %all-to-all-start) | async-done | bytes 2592 | tf_op jit(solution)/shard_map/all_to_all | solution.py:51
  28.9 4.7 %all-to-all-start.1 = ((bf16[128,1,5]{2,1,0:T(2,128)(2,1)}), bf16[128,1,5]{2,1,0:T(2,128)(2,1)S(1)}, u32[]{:S(2)}, u32[]{:S(2)}) async-start(bf16[128,1,5]{2,1,0:T(2,128)(2,1)} %all_to_all.24), calls=%async_computation.1 | async-start | bytes 131072 | tf_op jit(solution)/shard_map/all_to_all | solution.py:84
  33.6 0.5 broadcast.156
  34.2 0.8 reduce.10
  34.9 0.2 reshape.144
  35.2 0.6 copy-done.6
  35.8 0.6 pad_clamp_fusion.1
  36.4 5.9 %gather_fusion = bf16[640,1024]{1,0:T(8,128)(2,1)S(1)} fusion(bf16[1024,1024]{1,0:T(8,128)(2,1)} %copy.56, s32[1024]{0:T(1024)} %pad_clamp_fusion.1), kind=kCustom, calls=%fused_computation | custom fusion | bytes 2624000 | tf_op jit(solution)/shard_map/jit(_take)/gather | solution.py:53
  42.3 1.7 %gather.13 = bf16[128,5,1024]{2,1,0:T(8,128)(2,1)} reshape(bf16[640,1024]{1,0:T(8,128)(2,1)S(1)} %gather_fusion) | data formatting | bytes 2621440 | tf_op jit(solution)/shard_map/jit(_take)/gather | solution.py:53
  44.0 3.2 %broadcast_select_fusion = bf16[128,5,1024]{2,1,0:T(8,128)(2,1)} fusion(bf16[128,5,1024]{2,1,0:T(8,128)(2,1)} %gather.13, pred[128,5]{1,0:T(8,128)(4,1)S(1)} %compare_and_fusion), kind=kLoop, calls=%fused_computation.27 | loop fusion | flops 655360 | bytes 2622080 | tf_op jit(solution)/shard_map/jit(_take)/select_n | solution.py:53
  47.2 0.0 all-to-all-done.1
  47.2 0.0 copy-start.3
  47.2 10.5 %all-to-all-start.2 = ((bf16[128,5,1024]{2,1,0:T(8,128)(2,1)}), bf16[128,5,1024]{2,1,0:T(8,128)(2,1)}, u32[]{:S(2)}, u32[]{:S(2)}) async-start(bf16[128,5,1024]{2,1,0:T(8,128)(2,1)} %broadcast_select_fusion), calls=%async_computation.2 | async-start | bytes 4194304 | tf_op jit(solution)/shard_map/all_to_all | solution.py:54
  57.7 0.0 copy-done.3
  57.7 0.7 copy.53
  58.5 0.0 copy-done.8
  58.5 0.2 reduce.3
  58.7 0.2 reshape.197
  58.9 0.2 eq.50
  59.1 0.4 fusion.30
  59.6 27.3 %all-to-all-done.2 = bf16[128,5,1024]{2,1,0:T(8,128)(2,1)} async-done(((bf16[128,5,1024]{2,1,0:T(8,128)(2,1)}), bf16[128,5,1024]{2,1,0:T(8,128)(2,1)}, u32[]{:S(2)}, u32[]{:S(2)}) %all-to-all-start.2) | async-done | bytes 1310752 | tf_op jit(solution)/shard_map/all_to_all | solution.py:54
  86.8 2.6 %reshape.146 = bf16[640,1024]{1,0:T(8,128)(2,1)S(1)} reshape(bf16[128,5,1024]{2,1,0:T(8,128)(2,1)} %all-to-all-done.2) | data formatting | bytes 2621440 | tf_op jit(solution)/shard_map/reshape | solution.py:61
  89.4 2.8 %gather_fusion.1 = bf16[512,1024]{1,0:T(8,128)(2,1)} fusion(bf16[640,1024]{1,0:T(8,128)(2,1)S(1)} %reshape.146, s32[1024]{0:T(1024)S(1)} %pad_clamp_fusion), kind=kCustom, calls=%fused_computation.1 | custom fusion | bytes 2099200 | tf_op jit(solution)/shard_map/jit(_take)/gather | solution.py:61
  92.2 1.4 gather.15
  93.7 0.0 copy-start.15
  93.7 0.0 copy-start.16
  93.7 1.3 copy.52
  95.0 1.3 bitcast_select_fusion
  96.4 0.0 copy-done
  96.4 0.0 copy-done.4
  96.4 0.0 copy-done.13
  96.4 0.0 copy-done.15
  96.4 0.0 copy-done.16
  96.4 5.0 %fusion.24 = bf16[256,1024]{1,0:T(8,128)(2,1)} fusion(bf16[1024,1024]{1,0:T(8,128)(2,1)S(1)} %copy-done, bf16[2176,1024]{1,0:T(8,128)(2,1)} %param.17, bf16[256,128]{0,1:T(8,128)(2,1)S(1)} %copy-done.4, bf16[256,2048]{0,1:T(8,128)(2,1)S(1)} %bitcast_select_fusion, f32[256]{0:T(256)S(1)} %copy-done.13, f32[1024]{0:T(1024)S(1)} %copy-done.15, ...), kind=kOutput, calls=%fused_computation.39 | convolution fusion | flops 1681522688 | bytes 8201216 | tf_op jit(solution)/shard_map/dot_general | solution.py:70
  101.4 2.5 %scatter_custom_fusion.2 = bf16[640,1024]{1,0:T(8,128)(2,1)S(1)} fusion(s32[256]{0:T(256)} %bitcast.32, bf16[256,1024]{1,0:T(8,128)(2,1)} %fusion.24, bf16[]{:T(256)} %constant.29.clone.1), kind=kCustom, calls=%fused_computation.48 | custom fusion | bytes 1311232 | tf_op jit(solution)/shard_map/scatter | solution.py:74
  104.0 1.6 reshape.147
  105.5 6.1 %all-to-all-start.3 = ((bf16[128,5,1024]{2,1,0:T(8,128)(2,1)}), bf16[128,5,1024]{2,1,0:T(8,128)(2,1)}, u32[]{:S(2)}, u32[]{:S(2)}) async-start(bf16[128,5,1024]{2,1,0:T(8,128)(2,1)} %reshape.147), calls=%async_computation.3 | async-start | bytes 4194304 | tf_op jit(solution)/shard_map/all_to_all | solution.py:77
  111.7 9.4 %fusion.43 = f32[640,3072]{1,0:T(8,128)} fusion(bf16[1024,3072]{1,0:T(8,128)(2,1)} %param.22, bf16[640,1024]{1,0:T(8,128)(2,1)S(1)} %copy-done.2, pred[640]{0:T(1024)(128)(4,1)S(1)} %compare_and_fusion.1), kind=kOutput, calls=%fused_computation.50 | convolution fusion | flops 4027187200 | bytes 15467136 | tf_op jit(solution)/shard_map/dot_general | solution.py:10
  121.1 19.6 %all-to-all-done.3 = bf16[128,5,1024]{2,1,0:T(8,128)(2,1)} async-done(((bf16[128,5,1024]{2,1,0:T(8,128)(2,1)}), bf16[128,5,1024]{2,1,0:T(8,128)(2,1)}, u32[]{:S(2)}, u32[]{:S(2)}) %all-to-all-start.3) | async-done | bytes 1310752 | tf_op jit(solution)/shard_map/all_to_all | solution.py:77
  140.7 3.7 %reshape.148 = bf16[640,1024]{1,0:T(8,128)(2,1)} reshape(bf16[128,5,1024]{2,1,0:T(8,128)(2,1)} %all-to-all-done.3) | data formatting | bytes 2621440 | tf_op jit(solution)/shard_map/reshape | solution.py:94
  144.4 11.6 %convolution_add_fusion = f32[640,3072]{1,0:T(8,128)} fusion(bf16[1024,3072]{1,0:T(8,128)(2,1)} %param.21, f32[3072]{0:T(1024)S(1)} %copy-done.14, bf16[640,1024]{1,0:T(8,128)(2,1)} %reshape.148, f32[640]{0:T(1024)S(1)} %broadcast_maximum_fusion, s32[640]{0:T(1024)S(1)} %eq.50), kind=kOutput, calls=%fused_computation.6 | convolution fusion | flops 4869079040 | bytes 15483904 | tf_op jit(solution)/shard_map/dot_general | solution.py:9
  156.1 16.4 %scatter_custom_fusion.3 = bf16[1024,1024]{1,0:T(8,128)(2,1)} fusion(bf16[1024,1024]{1,0:T(8,128)(2,1)} %copy.56, s32[640]{0:T(1024)} %copy-done.6, f32[640,3072]{1,0:T(8,128)} %fusion.43, f32[640,3072]{1,0:T(8,128)} %convolution_add_fusion, f32[]{:T(128)} %constant.31.clone.1, pred[640]{0:T(1024)(128)(4,1)S(1)} %broadcast_compare_fusion, ...), kind=kCustom, calls=%fused_computation.35 | custom fusion | flops 11796480 | bytes 19138816 | tf_op jit(solution)/shard_map/scatter | solution.py:99
  (35 shorter events, 0.2 us)
Async XLA Ops:
  0.0 96.4 %copy-start = (bf16[1024,1024]{1,0:T(8,128)(2,1)S(1)}, bf16[1024,1024]{1,0:T(8,128)(2,1)}, u32[]{:S(2)}) copy-start(bf16[1024,1024]{1,0:T(8,128)(2,1)} %param.19) | copy-start | bytes 6291460
  0.0 3.2 %copy-start.5 = (s32[256,2]{0,1:T(2,128)S(1)}, s32[256,2]{0,1:T(2,128)}, u32[]{:S(2)}) copy-start(s32[256,2]{0,1:T(2,128)} %param.13) | copy-start | bytes 6148
  0.0 4.1 %copy-start.10 = (s32[256,2]{0,1:T(2,128)S(1)}, s32[256,2]{0,1:T(2,128)}, u32[]{:S(2)}) copy-start(s32[256,2]{0,1:T(2,128)} %param.14) | copy-start | bytes 6148
  3.2 17.0 %copy-start.11 = (s32[256]{0:T(256)S(1)}, s32[256]{0:T(256)}, u32[]{:S(2)}) copy-start(s32[256]{0:T(256)} %param.15) | copy-start | bytes 3076
  5.0 30.2 %copy-start.7 = (s32[512,1]{0,1:T(1,128)}, s32[512,1]{0,1:T(1,128)S(1)}, u32[]{:S(2)}) copy-start(s32[512,1]{0,1:T(1,128)S(1)} %compare_select_fusion.2) | copy-start | bytes 6148
  8.3 20.6 %all-to-all-start = ((s32[128,1,5]{2,1,0:T(1,128)}), s32[128,1,5]{2,1,0:T(1,128)S(1)}, u32[]{:S(2)}, u32[]{:S(2)}) async-start(s32[128,1,5]{2,1,0:T(1,128)} %bitcast.5), calls=%async_computation | async-start | bytes 131072 | tf_op jit(solution)/shard_map/all_to_all | solution.py:51
  20.2 15.0 %copy-start.12 = (s32[256,1]{0,1:T(1,128)}, s32[256,1]{0,1:T(1,128)S(1)}, u32[]{:S(2)}) copy-start(s32[256,1]{0,1:T(1,128)S(1)} %compare_select_fusion.5) | copy-start | bytes 3076
  28.9 18.4 %all-to-all-start.1 = ((bf16[128,1,5]{2,1,0:T(2,128)(2,1)}), bf16[128,1,5]{2,1,0:T(2,128)(2,1)S(1)}, u32[]{:S(2)}, u32[]{:S(2)}) async-start(bf16[128,1,5]{2,1,0:T(2,128)(2,1)} %all_to_all.24), calls=%async_computation.1 | async-start | bytes 131072 | tf_op jit(solution)/shard_map/all_to_all | solution.py:84
  35.2 0.6 copy-start.6
  42.3 4.9 %copy-start.1 = (bf16[640,1024]{1,0:T(8,128)(2,1)}, bf16[640,1024]{1,0:T(8,128)(2,1)S(1)}, u32[]{:S(2)}) copy-start(bf16[640,1024]{1,0:T(8,128)(2,1)S(1)} %gather_fusion) | copy-start | bytes 3932164
  47.2 11.3 %copy-start.8 = (s32[512,1]{0,1:T(1,128)S(1)}, s32[512,1]{0,1:T(1,128)}, u32[]{:S(2)}) copy-start(s32[512,1]{0,1:T(1,128)} %copy-done.7) | copy-start | bytes 6148
  47.2 10.5 %copy-start.3 = (bf16[256,128]{1,0:T(8,128)(2,1)S(1)}, bf16[256,128]{1,0:T(8,128)(2,1)}, u32[]{:S(2)}) copy-start(bf16[256,128]{1,0:T(8,128)(2,1)} %param.16) | copy-start | bytes 196612
  47.2 39.6 %all-to-all-start.2 = ((bf16[128,5,1024]{2,1,0:T(8,128)(2,1)}), bf16[128,5,1024]{2,1,0:T(8,128)(2,1)}, u32[]{:S(2)}, u32[]{:S(2)}) async-start(bf16[128,5,1024]{2,1,0:T(8,128)(2,1)} %broadcast_select_fusion), calls=%async_computation.2 | async-start | bytes 4194304 | tf_op jit(solution)/shard_map/all_to_all | solution.py:54
  92.2 2.8 %copy-start.9 = (pred[256,2]{0,1:T(4,128)(4,1)S(1)}, pred[256,2]{0,1:T(4,128)(4,1)}, u32[]{:S(2)}) copy-start(pred[256,2]{0,1:T(4,128)(4,1)} %get-tuple-element.5) | copy-start | bytes 1540
  93.7 2.7 %copy-start.4 = (bf16[256,128]{0,1:T(8,128)(2,1)S(1)}, bf16[256,128]{0,1:T(8,128)(2,1)}, u32[]{:S(2)}) copy-start(bf16[256,128]{0,1:T(8,128)(2,1)} %copy.53) | copy-start | bytes 196612
  93.7 2.7 %copy-start.13 = (f32[256]{0:T(256)S(1)}, f32[256]{0:T(256)}, u32[]{:S(2)}) copy-start(f32[256]{0:T(256)} %get-tuple-element.8) | copy-start | bytes 3076
  93.7 2.7 %copy-start.15 = (f32[1024]{0:T(1024)S(1)}, f32[1024]{0:T(1024)}, u32[]{:S(2)}) copy-start(f32[1024]{0:T(1024)} %param.20) | copy-start | bytes 12292
  93.7 2.7 %copy-start.16 = (f32[1024]{0:T(1024)S(1)}, f32[1024]{0:T(1024)}, u32[]{:S(2)}) copy-start(f32[1024]{0:T(1024)} %param.18) | copy-start | bytes 12292
  105.5 6.2 %copy-start.2 = (bf16[640,1024]{1,0:T(8,128)(2,1)S(1)}, bf16[640,1024]{1,0:T(8,128)(2,1)}, u32[]{:S(2)}) copy-start(bf16[640,1024]{1,0:T(8,128)(2,1)} %copy-done.1) | copy-start | bytes 3932164
  105.5 35.2 %all-to-all-start.3 = ((bf16[128,5,1024]{2,1,0:T(8,128)(2,1)}), bf16[128,5,1024]{2,1,0:T(8,128)(2,1)}, u32[]{:S(2)}, u32[]{:S(2)}) async-start(bf16[128,5,1024]{2,1,0:T(8,128)(2,1)} %reshape.147), calls=%async_computation.3 | async-start | bytes 4194304 | tf_op jit(solution)/shard_map/all_to_all | solution.py:77
  121.1 23.3 %copy-start.14 = (f32[3072]{0:T(1024)S(1)}, f32[3072]{0:T(1024)}, u32[]{:S(2)}) copy-start(f32[3072]{0:T(1024)} %param.23) | copy-start | bytes 36868
where the time goes:
time: 173 us; the launch traced here: 172 us
  waiting for transfers between devices  51.9 us (30%)
  local copies, waits for them, and re-layouts  37 us (21%)
  starting transfers between devices  32.5 us (19%)
  matrix products  26.5 us (15%)
  other arithmetic  24.2 us (14%)
    all_to_all x1, waiting for transfers between devices, on_device(): lax.all_to_all(answers.reshape(devices, capacity, feature_width), ('node'...  27.3 us
    all_to_all x1, waiting for transfers between devices, on_device(): lax.all_to_all(outgoing.reshape(devices, capacity, feature_width), ('node...  19.6 us
    scatter x1, other arithmetic, on_device(): return memory.at[flat_ids].set(renewed)  16.4 us
    dot_general x1, matrix products, memory_update(): jnp.dot(aggregate, gru_in, preferred_element_type=jnp.float32) + gru_bias  11.6 us
    all_to_all x1, starting transfers between devices, on_device(): lax.all_to_all(requests, ('node', 'tm'), split_axis=0, concat_axis=0, til...  11.1 us
    all_to_all x1, starting transfers between devices, on_device(): lax.all_to_all(answers.reshape(devices, capacity, feature_width), ('node'...  10.5 us
    dot_general x1, matrix products, memory_update(): gates_hid = jnp.dot(memory, gru_hid, preferred_element_type=jnp.float32)  9.38 us
    gather x2, local copies, waits for them, and re-layouts, on_device(): answers = jnp.take(memory, flat_ids, axis=0)  7.61 us
  transfers between devices with their start and end apart: 4, of which 3 were waited for; matrix products, arithmetic and copies ran while one was open for 16% of the time, Pallas kernels for 0%

commit v1 on v0

v1 whole, which is shorter than its diff:
```python
import jax
import jax.numpy as jnp
from jax import lax
from jax.experimental import pallas as pl
from jax.experimental.pallas import tpu as pltpu
from jax.sharding import PartitionSpec as P

AXES = ("node", "tm")
LANES = 128
SUB = 8
ACTIVE = 1024
TILE = 256
MIB = 1 << 20

VM = pl.BlockSpec(memory_space=pltpu.VMEM)
SM = pl.BlockSpec(memory_space=pltpu.SMEM)


def plan_kernel(capacity, owner_ref, row_ref, mask_ref, ids_ref, place_ref):
    devices = ids_ref.shape[0]
    events = owner_ref.shape[1]
    ends = 2 * events
    owner = jnp.concatenate([owner_ref[0:1, :], owner_ref[1:2, :]], axis=1)
    code = jnp.concatenate([row_ref[0:1, :], row_ref[1:2, :] + ACTIVE * mask_ref[...]], axis=1)
    named = lax.broadcasted_iota(jnp.int32, (devices, ends), 0) == owner
    named_b = named.astype(jnp.float32).astype(jnp.bfloat16)
    before = (
        lax.broadcasted_iota(jnp.int32, (ends, ends), 0) < lax.broadcasted_iota(jnp.int32, (ends, ends), 1)
    ).astype(jnp.float32).astype(jnp.bfloat16)
    count = jnp.dot(named_b, before, preferred_element_type=jnp.float32)
    position = jnp.sum(jnp.where(named, count, 0.0), axis=0, keepdims=True).astype(jnp.int32)
    place = owner * capacity + position
    place_ref[0:1, :] = place[:, :events]
    place_ref[1:2, :] = place[:, events:]
    here = lax.broadcasted_iota(jnp.int32, (LANES, ends), 0) == position
    low = jnp.where(here, (code & 31).astype(jnp.float32), 0.0).astype(jnp.bfloat16)
    high = jnp.where(here, (code >> 5).astype(jnp.float32), 0.0).astype(jnp.bfloat16)
    contract = (((1,), (1,)), ((), ()))
    low_sum = lax.dot_general(named_b, low, contract, preferred_element_type=jnp.float32)
    high_sum = lax.dot_general(named_b, high, contract, preferred_element_type=jnp.float32)
    ids_ref[...] = (low_sum + 32.0 * high_sum).astype(jnp.int32)


def answer_kernel(capacity, ids_ref, memory_ref, out_ref):
    devices = ids_ref.shape[0]
    group = 8

    def step(i, carry):
        for a in range(group):
            p = i * group + a
            for k in range(capacity):
                row = ids_ref[p, k] & (ACTIVE - 1)
                out_ref[p * capacity + k] = memory_ref[row]
        return carry

    lax.fori_loop(0, devices // group, step, 0)


def compact_kernel(capacity, ids_ref, slot_ref, index_ref, count_ref, node_ref, of_ref, size_ref):
    devices = ids_ref.shape[0]
    rows = of_ref.shape[0]

    def clear(i, carry):
        for a in range(16):
            of_ref[i * 16 + a] = -1
        return carry

    lax.fori_loop(0, rows // 16, clear, 0)

    def step(p, carry):
        taken, nodes = carry
        for k in range(capacity):
            code = ids_ref[p, k]
            active = code >= ACTIVE
            node = code & (ACTIVE - 1)
            known = of_ref[node]
            fresh = active & (known < 0)
            index = jnp.where(known < 0, nodes, known)
            of_ref[node] = jnp.where(active, index, known)
            slot_ref[taken] = p * capacity + k
            index_ref[taken] = index
            old = count_ref[index]
            was = jnp.where(known < 0, 0, old)
            count_ref[index] = jnp.where(active, was + 1, was)
            node_ref[index] = jnp.where(fresh, node, jnp.where(known < 0, 0, node_ref[index]))
            taken = taken + active.astype(jnp.int32)
            nodes = nodes + fresh.astype(jnp.int32)
        return taken, nodes

    taken, nodes = lax.fori_loop(0, devices, step, (jnp.int32(0), jnp.int32(0)))
    size_ref[0] = taken
    size_ref[1] = nodes


def to_matrix(tiles_ref, start, rows):
    parts = [tiles_ref[pl.ds(start * SUB + c, rows, stride=SUB), :].astype(jnp.bfloat16) for c in range(SUB)]
    return jnp.concatenate(parts, axis=1)


def hidden_gates_kernel(node_ref, size_ref, memory_ref, gru_ref, previous_ref, gates_ref, tiles_ref):
    nodes = size_ref[1]
    steps = pl.cdiv(nodes, TILE)
    width = previous_ref.shape[1]

    def block(t, carry):
        def copy(i, c):
            for a in range(16):
                u = i * 16 + a
                row = node_ref[t * TILE + u] & (ACTIVE - 1)
                tiles_ref[pl.ds(pl.multiple_of(u * SUB, SUB), SUB), :] = memory_ref[row].astype(jnp.float32)
            return c

        lax.fori_loop(0, TILE // 16, copy, 0)
        here = pl.ds(pl.multiple_of(t * TILE, TILE), TILE)
        previous_ref[here, :] = to_matrix(tiles_ref, 0, TILE)

        def columns(j, c):
            cols = pl.ds(pl.multiple_of(j * 256, 256), 256)
            gates_ref[here, cols] = jnp.dot(
                previous_ref[here, :], gru_ref[:, cols], preferred_element_type=jnp.float32
            )
            return c

        lax.fori_loop(0, 3 * width // 256, columns, 0)
        return carry

    lax.fori_loop(0, steps, block, 0)


def message_kernel(
    place_ref, rows_ref, feat_ref, w1_ref, b1_ref, w2_ref, b2_ref, out_ref, tiles_ref, inputs_ref, hidden_ref
):
    events = feat_ref.shape[0]
    width = w2_ref.shape[1]
    hid = w2_ref.shape[0]
    group = 16
    for half in range(2):

        def fetch(i, c):
            for a in range(group):
                e = i * group + a
                tiles_ref[pl.ds(pl.multiple_of(e * SUB, SUB), SUB), :] = rows_ref[place_ref[half, e]].astype(
                    jnp.float32
                )
            return c

        lax.fori_loop(0, events // group, fetch, 0)
        inputs_ref[:, half * width : (half + 1) * width] = to_matrix(tiles_ref, 0, events)
    inputs_ref[:, 2 * width :] = feat_ref[...]
    for j in range(hid // 256):
        cols = slice(j * 256, (j + 1) * 256)
        h = jnp.dot(inputs_ref[...], w1_ref[:, cols], preferred_element_type=jnp.float32) + b1_ref[:, cols]
        hidden_ref[:, cols] = jnp.maximum(h, 0.0).astype(jnp.bfloat16)
    for j in range(width // 256):
        cols = slice(j * 256, (j + 1) * 256)
        m = jnp.dot(hidden_ref[...], w2_ref[:, cols], preferred_element_type=jnp.float32) + b2_ref[:, cols]
        for c in range(2):
            tiles_ref[pl.ds(2 * j + c, events, stride=SUB), :] = m[:, c * LANES : (c + 1) * LANES]
    out_ref[...] = jnp.zeros_like(out_ref)

    def send(i, c):
        for a in range(group):
            e = i * group + a
            out_ref[place_ref[1, e]] = tiles_ref[pl.ds(pl.multiple_of(e * SUB, SUB), SUB), :].astype(jnp.bfloat16)
        return c

    lax.fori_loop(0, events // group, send, 0)


def update_kernel(
    slot_ref,
    index_ref,
    count_ref,
    size_ref,
    incoming_ref,
    of_ref,
    memory_ref,
    previous_ref,
    gates_ref,
    gru_ref,
    bias_ref,
    out_ref,
    tiles_ref,
    aggregate_ref,
    renewed_ref,
):
    width = memory_ref.shape[1]
    taken = size_ref[0]
    nodes = size_ref[1]
    steps = pl.cdiv(nodes, TILE)

    def clear(t, c):
        start = pl.multiple_of(t * TILE * SUB, TILE * SUB)
        tiles_ref[pl.ds(start, TILE * SUB), :] = jnp.zeros((TILE * SUB, LANES), jnp.float32)
        return c

    lax.fori_loop(0, steps, clear, 0)

    def add(i, c):
        slot = slot_ref[i]
        here = pl.ds(pl.multiple_of(index_ref[i] * SUB, SUB), SUB)
        tiles_ref[here, :] += incoming_ref[slot].astype(jnp.float32)
        return c

    lax.fori_loop(0, taken, add, 0)

    def mean(i, c):
        here = pl.ds(pl.multiple_of(i * SUB, SUB), SUB)
        tiles_ref[here, :] = tiles_ref[here, :] / count_ref[i].astype(jnp.float32)
        return c

    lax.fori_loop(0, nodes, mean, 0)

    def block(t, c):
        here = pl.ds(pl.multiple_of(t * TILE, TILE), TILE)
        aggregate_ref[...] = to_matrix(tiles_ref, pl.multiple_of(t * TILE, TILE), TILE)
        for j in range(width // 256):
            pre = []
            for g in range(3):
                cols = slice(g * width + j * 256, g * width + (j + 1) * 256)
                pre.append(
                    jnp.dot(aggregate_ref[...], gru_ref[:, cols], preferred_element_type=jnp.float32)
                    + bias_ref[:, cols]
                )
            hid = [gates_ref[here, g * width + j * 256 : g * width + (j + 1) * 256] for g in range(3)]
            reset = jax.nn.sigmoid(pre[0] + hid[0])
            update = jax.nn.sigmoid(pre[1] + hid[1])
            candidate = jnp.tanh(pre[2] + reset * hid[2])
            previous = previous_ref[here, j * 256 : (j + 1) * 256].astype(jnp.float32)
            renewed = (1.0 - update) * candidate + update * previous
            renewed_ref[here, j * 256 : (j + 1) * 256] = renewed.astype(jnp.bfloat16)
        return c

    @pl.when(nodes == 0)
    def _():
        renewed_ref[...] = jnp.zeros_like(renewed_ref)

    lax.fori_loop(0, steps, block, 0)
    rows = 128

    def place(t):
        def band(i, c):
            here = pl.ds(pl.multiple_of(i * rows, rows), rows)
            of = of_ref[here, :]
            lane = lax.broadcasted_iota(jnp.int32, (rows, TILE), 1) + t * TILE
            pick = (of == lane).astype(jnp.float32).astype(jnp.bfloat16)
            found = jnp.dot(
                pick, renewed_ref[t * TILE : (t + 1) * TILE, :], preferred_element_type=jnp.float32
            )
            base = memory_ref if t == 0 else out_ref
            mine = (of >= t * TILE) & (of < (t + 1) * TILE)
            out_ref[here, :] = jnp.where(mine, found, base[here, :].astype(jnp.float32)).astype(jnp.bfloat16)
            return c

        lax.fori_loop(0, out_ref.shape[0] // rows, band, 0)

    place(0)
    for t in range(1, renewed_ref.shape[0] // TILE):

        @pl.when(t < steps)
        def _():
            place(t)


def on_device(
    memory,
    ends_owner,
    ends_row,
    event_mask,
    edge_feat,
    msg_w1,
    msg_b1,
    msg_w2,
    msg_b2,
    gru_in,
    gru_hid,
    gru_bias,
):
    devices = lax.axis_size(AXES)
    events = ends_owner.shape[0]
    node_rows, width = memory.shape
    hid = msg_w2.shape[0]
    capacity = 5 * events // (2 * devices)
    slots = devices * capacity
    padded = pl.cdiv(slots, TILE) * TILE
    cells = width // LANES
    f32, bf16, i32 = jnp.float32, jnp.bfloat16, jnp.int32
    shape = jax.ShapeDtypeStruct

    ids, place = pl.pallas_call(
        lambda *refs: plan_kernel(capacity, *refs),
        out_shape=(shape((devices, LANES), i32), shape((2, events), i32)),
        in_specs=[VM, VM, VM],
        out_specs=(VM, VM),
        name="plan",
    )(ends_owner.T, ends_row.T, event_mask.reshape(1, events))

    arrived = lax.all_to_all(
        ids.reshape(devices, 1, LANES), AXES, split_axis=0, concat_axis=0, tiled=True
    ).reshape(devices, LANES)
    tiles = memory.reshape(node_rows, cells, LANES)

    answers = pl.pallas_call(
        lambda *refs: answer_kernel(capacity, *refs),
        out_shape=shape((slots, cells, LANES), bf16),
        in_specs=[SM, VM],
        out_specs=VM,
        name="answer",
    )(arrived, tiles)
    returned = lax.all_to_all(
        answers.reshape(devices, capacity, cells, LANES), AXES, split_axis=0, concat_axis=0, tiled=True
    ).reshape(slots, cells, LANES)

    slot, index, count, node, of, size = pl.pallas_call(
        lambda *refs: compact_kernel(capacity, *refs),
        out_shape=(
            shape((1024,), i32),
            shape((1024,), i32),
            shape((1024,), i32),
            shape((1024,), i32),
            shape((node_rows,), i32),
            shape((8,), i32),
        ),
        in_specs=[SM],
        out_specs=(SM, SM, SM, SM, SM, SM),
        cost_estimate=pl.CostEstimate(flops=4_000_000_000, bytes_accessed=20_000_000, transcendentals=0),
        name="compact",
    )(arrived)

    previous, gates = pl.pallas_call(
        hidden_gates_kernel,
        out_shape=(shape((padded, width), bf16), shape((padded, 3 * width), f32)),
        in_specs=[SM, SM, VM, VM],
        out_specs=(VM, VM),
        scratch_shapes=[pltpu.VMEM((TILE * SUB, LANES), f32)],
        compiler_params=pltpu.CompilerParams(vmem_limit_bytes=40 * MIB),
        cost_estimate=pl.CostEstimate(flops=4_000_000_000, bytes_accessed=20_000_000, transcendentals=0),
        name="hidden_gates",
    )(node, size, tiles, gru_hid)

    outgoing = pl.pallas_call(
        message_kernel,
        out_shape=shape((slots, cells, LANES), bf16),
        in_specs=[SM, VM, VM, VM, VM, VM, VM],
        out_specs=VM,
        scratch_shapes=[
            pltpu.VMEM((events * SUB, LANES), f32),
            pltpu.VMEM((events, msg_w1.shape[0]), bf16),
            pltpu.VMEM((events, hid), bf16),
        ],
        compiler_params=pltpu.CompilerParams(vmem_limit_bytes=24 * MIB),
        name="message",
    )(place, returned, edge_feat, msg_w1, msg_b1.reshape(1, hid), msg_w2, msg_b2.reshape(1, width))
    incoming = lax.all_to_all(
        outgoing.reshape(devices, capacity, cells, LANES), AXES, split_axis=0, concat_axis=0, tiled=True
    ).reshape(slots, cells, LANES)

    return pl.pallas_call(
        update_kernel,
        out_shape=shape((node_rows, width), bf16),
        in_specs=[SM, SM, SM, SM, VM, VM, VM, VM, VM, VM, VM],
        out_specs=VM,
        scratch_shapes=[
            pltpu.VMEM((padded * SUB, LANES), f32),
            pltpu.VMEM((TILE, width), bf16),
            pltpu.VMEM((padded, width), bf16),
        ],
        compiler_params=pltpu.CompilerParams(vmem_limit_bytes=48 * MIB),
        name="update",
    )(
        slot,
        index,
        count,
        size,
        incoming,
        of.reshape(node_rows, 1),
        memory,
        previous,
        gates,
        gru_in,
        gru_bias.reshape(1, 3 * width),
    )


def solution(mesh):
    row = P(AXES, None)
    return jax.shard_map(
        on_device,
        mesh=mesh,
        in_specs=(row, row, row, P(AXES), row, P(), P(), P(), P(), P(), P(), P()),
        out_specs=row,
        check_vma=False,
    )
```

time: 173 us -> 112 us (0.65)
  waiting for transfers between devices: 51.9 us -> 5.94 us
  Pallas kernels: 0 us -> 45.2 us
  blocking collectives: 0 us -> 26.8 us
  matrix products: 26.5 us -> 0 us
  other arithmetic: 24.2 us -> 0 us
  local copies, waits for them, and re-layouts: 37 us -> 17.5 us
  starting transfers between devices: 32.5 us -> 15.8 us
    all_to_all x4 -> x2, waiting for transfers between devices: 51.9 us -> 5.94 us  [the longest x1 5.94 us: on_device(): lax.all_to_all(ids.reshape(devices, 1, LANES), AXES, split_axis=0, concat...]
    pallas_call x0 -> x6, Pallas kernels: none -> 45.2 us  [the longest x1 14.8 us: on_device(): pl.pallas_call(update_kernel, out_shape=shape((node_rows, width), bf16),...]
    all_to_all x0 -> x1, blocking collectives: none -> 26.8 us  [on_device(): lax.all_to_all(answers.reshape(devices, capacity, cells, LANES), AXES, sp...]
    dot_general x4 -> x0, matrix products: 26.5 us -> none  [the longest x1 11.6 us: memory_update(): jnp.dot(aggregate, gru_in, preferred_element_type=jnp.float32) + gru_bias]
    all_to_all x4 -> x2, starting transfers between devices: 32.5 us -> 15.8 us  [the longest x1 11.1 us: on_device(): lax.all_to_all(ids.reshape(devices, 1, LANES), AXES, split_axis=0, concat...]
    scatter x1 -> x0, other arithmetic: 16.4 us -> none  [on_device(): return memory.at[flat_ids].set(renewed)]
    gather x5 -> x0, local copies, waits for them, and re-layouts: 13.1 us -> none  [the longest x2 7.61 us: on_device(): answers = jnp.take(memory, flat_ids, axis=0)]
    unnamed x38 -> x41, local copies, waits for them, and re-layouts: 4.89 us -> 15.8 us
  transfers between devices with their start and end apart: 4 -> 2, of which waited for: 3 -> 1; matrix products, arithmetic and copies ran while one was open for 16% -> 5% of each run, Pallas kernels for 0% -> 17%
where the time goes in v1:
time: 112 us; the launch traced here: 111 us
  Pallas kernels  45.2 us (40%)
  blocking collectives  26.8 us (24%)
  local copies, waits for them, and re-layouts  17.5 us (16%)
  starting transfers between devices  15.8 us (14%)
  waiting for transfers between devices  5.94 us (5%)
    all_to_all x1, blocking collectives, on_device(): lax.all_to_all(answers.reshape(devices, capacity, cells, LANES), AXES, sp...  26.8 us
    unnamed x41, local copies, waits for them, and re-layouts  15.8 us
    pallas_call x1, Pallas kernels, on_device(): pl.pallas_call(update_kernel, out_shape=shape((node_rows, width), bf16),...  14.8 us
    all_to_all x1, starting transfers between devices, on_device(): lax.all_to_all(ids.reshape(devices, 1, LANES), AXES, split_axis=0, concat...  11.1 us
    pallas_call x1, Pallas kernels, on_device(): pl.pallas_call(lambda *refs: compact_kernel(capacity, *refs), out_shape=(...  10.2 us
    pallas_call x1, Pallas kernels, on_device(): pl.pallas_call(hidden_gates_kernel, out_shape=(shape((padded, width), bf1...  8.77 us
    all_to_all x1, waiting for transfers between devices, on_device(): lax.all_to_all(ids.reshape(devices, 1, LANES), AXES, split_axis=0, concat...  5.94 us
    pallas_call x1, Pallas kernels, on_device(): pl.pallas_call(message_kernel, out_shape=shape((slots, cells, LANES), bf1...  5.91 us
  transfers between devices with their start and end apart: 2, of which 1 were waited for; matrix products, arithmetic and copies ran while one was open for 5% of the time, Pallas kernels for 17%

profile of v1, /device:TPU:0, one launch (start us, length us, event | category | flops | bytes accessed | tf_op | source)
XLA Modules:
  0.0 111.3 jit_solution(17130374368235844337)
XLA Ops:
  0.0 1.8 %plan.1 = (s32[128,128]{1,0:T(8,128)}, s32[2,256]{1,0:T(2,128)}) custom-call(s32[2,256]{1,0:T(2,128)} %bitcast.30, s32[2,256]{1,0:T(2,128)} %bitcast.31, s32[1,256]{1,0:T(1,128)} %bitcast.32), custom_call_target="tpu_custom_call" | custom-call | tf_op jit(solution)/shard_map/plan/pallas_call | solution.py:290
  1.8 11.1 %all-to-all-start = ((s32[128,1,128]{2,1,0:T(1,128)}), s32[128,1,128]{2,1,0:T(1,128)S(1)}, u32[]{:S(2)}, u32[]{:S(2)}) async-start(s32[128,1,128]{2,1,0:T(1,128)} %bitcast.28), calls=%async_computation | async-start | bytes 131072 | tf_op jit(solution)/shard_map/all_to_all | solution.py:298
  13.0 3.5 %copy.16 = bf16[128,8,8,128]{3,2,1,0:T(8,128)(2,1)} copy(bf16[128,8,8,128]{3,1,2,0:T(8,128)(2,1)} %bitcast.19) | data formatting | bytes 4194304
  16.5 5.9 %all-to-all-done = s32[128,1,128]{2,1,0:T(1,128)S(1)} async-done(((s32[128,1,128]{2,1,0:T(1,128)}), s32[128,1,128]{2,1,0:T(1,128)S(1)}, u32[]{:S(2)}, u32[]{:S(2)}) %all-to-all-start) | async-done | bytes 65568 | tf_op jit(solution)/shard_map/all_to_all | solution.py:298
  22.5 0.0 copy-start.19
  22.5 0.6 copy-done.19
  23.1 3.7 %answer.1 = bf16[640,8,128]{2,1,0:T(8,128)(2,1)} custom-call(s32[128,128]{1,0:T(8,128)} %bitcast.26, bf16[1024,8,128]{2,1,0:T(8,128)(2,1)} %bitcast.17), custom_call_target="tpu_custom_call" | custom-call | tf_op jit(solution)/shard_map/answer/pallas_call | solution.py:303
  26.8 0.0 copy-start.4
  26.8 0.0 copy-start.7
  26.8 0.0 copy-start.9
  26.8 0.0 copy-start.10
  26.8 0.0 copy-start.14
  26.8 26.8 %all_to_all.15 = bf16[128,5,8,128]{3,2,1,0:T(8,128)(2,1)S(1)} all-to-all(bf16[128,5,8,128]{3,2,1,0:T(8,128)(2,1)} %bitcast.25), channel_id=1, replica_groups=mesh['node'=8,'tm'=16] {'node','tm'}, dimensions={0} | all-to-all | bytes 2621440 | tf_op jit(solution)/shard_map/all_to_all | solution.py:310
  53.6 0.0 copy-done.4
  53.6 0.0 copy-done.7
  53.6 0.0 copy-done.9
  53.6 0.0 copy-done.10
  53.6 0.0 copy-done.14
  53.7 0.0 copy-start.2
  53.7 2.3 %copy-done.2 = bf16[2176,1024]{1,0:T(8,128)(2,1)S(1)} copy-done((bf16[2176,1024]{1,0:T(8,128)(2,1)S(1)}, bf16[2176,1024]{1,0:T(8,128)(2,1)}, u32[]{:S(2)}) %copy-start.2) | copy-done | bytes 4456472
  55.9 5.9 %message.1 = bf16[640,8,128]{2,1,0:T(8,128)(2,1)} custom-call(s32[2,256]{1,0:T(2,128)S(1)} %copy-done.14, bf16[640,8,128]{2,1,0:T(8,128)(2,1)S(1)} %bitcast.21, bf16[256,128]{1,0:T(8,128)(2,1)S(1)} %copy-done.7, bf16[2176,1024]{1,0:T(8,128)(2,1)S(1)} %copy-done.2, f32[1,1024]{1,0:T(1,128)S(1)} %bitcast.23, bf16[1024,1024]{1,0:T(8,128)(2,1)S(1)} %copy-done.4, ...), custom_call_target="tpu_custom_call" | custom-call | tf_op jit(solution)/shard_map/message/pallas_call | solution.py:341
  61.8 4.6 %all-to-all-start.2 = ((bf16[128,5,8,128]{3,2,1,0:T(8,128)(2,1)}), bf16[128,5,8,128]{3,2,1,0:T(8,128)(2,1)S(1)}, u32[]{:S(2)}, u32[]{:S(2)}) async-start(bf16[128,5,8,128]{3,2,1,0:T(8,128)(2,1)} %bitcast.10), calls=%async_computation.2 | async-start | bytes 2621440 | tf_op jit(solution)/shard_map/all_to_all | solution.py:354
  66.5 0.0 copy-start
  66.5 10.2 %compact.1 = (s32[1024]{0:T(1024)}, s32[1024]{0:T(1024)}, s32[1024]{0:T(1024)}, s32[1024]{0:T(1024)}, s32[1024]{0:T(1024)}, /*index=5*/s32[8]{0:T(128)}) custom-call(s32[128,128]{1,0:T(8,128)} %bitcast.27), custom_call_target="tpu_custom_call" | custom-call | flops 4000000000 | bytes 20000000 | tf_op jit(solution)/shard_map/compact/pallas_call | solution.py:314
  76.7 1.7 %copy.15.of_ref = s32[1024,1]{1,0:T(8,128)} copy(s32[1024,1]{0,1:T(1,128)} %bitcast.29) | data formatting | bytes 8192 | tf_op jit(solution)/shard_map/reshape | solution.py:376
  78.4 0.0 copy-done
  78.4 0.0 copy-start.15
  78.4 0.7 copy-done.15
  79.0 0.0 copy-start.17
  79.0 2.8 %copy-done.17 = bf16[1024,3072]{1,0:T(8,128)(2,1)S(1)} copy-done((bf16[1024,3072]{1,0:T(8,128)(2,1)S(1)}, bf16[1024,3072]{1,0:T(8,128)(2,1)}, u32[]{:S(2)}) %copy-start.17) | copy-done | bytes 6291480
  81.8 0.0 copy-start.18
  81.8 0.7 copy-done.18
  82.5 0.0 copy-start.8
  82.5 0.0 copy-start.11
  82.5 0.0 copy-start.12
  82.5 0.0 copy-start.13
  82.5 0.0 copy-start.16
  82.5 8.8 %hidden_gates.1 = (bf16[768,1024]{1,0:T(8,128)(2,1)S(1)}, f32[768,3072]{1,0:T(8,128)}) custom-call(s32[1024]{0:T(1024)S(1)} %copy-done.18, s32[8]{0:T(128)S(1)} %copy-done.15, bf16[1024,8,128]{2,1,0:T(8,128)(2,1)S(1)} %bitcast.18, bf16[1024,3072]{1,0:T(8,128)(2,1)S(1)} %copy-done.17), custom_call_target="tpu_custom_call" | custom-call | flops 4000000000 | bytes 20000000 | tf_op jit(solution)/shard_map/hidden_gates/pallas_call | solution.py:330
  91.3 0.0 copy-start.5
  91.3 1.1 %copy-done.5 = bf16[768,1024]{1,0:T(8,128)(2,1)} copy-done((bf16[768,1024]{1,0:T(8,128)(2,1)}, bf16[768,1024]{1,0:T(8,128)(2,1)S(1)}, u32[]{:S(2)}) %copy-start.5) | copy-done | bytes 1572888
  92.5 0.0 all-to-all-done.2
  92.5 0.0 copy-done.8
  92.5 0.0 copy-done.11
  92.5 0.0 copy-done.12
  92.5 0.0 copy-done.13
  92.5 0.0 copy-done.16
  92.5 0.0 copy-start.1
  92.5 1.6 %copy-done.1 = bf16[1024,1024]{1,0:T(8,128)(2,1)S(1)} copy-done((bf16[1024,1024]{1,0:T(8,128)(2,1)S(1)}, bf16[1024,1024]{1,0:T(8,128)(2,1)}, u32[]{:S(2)}) %copy-start.1) | copy-done | bytes 2097176
  94.1 0.0 copy-start.3
  94.1 1.0 copy-done.3
  95.1 0.0 copy-start.6
  95.1 1.4 %copy-done.6 = bf16[768,1024]{1,0:T(8,128)(2,1)S(1)} copy-done((bf16[768,1024]{1,0:T(8,128)(2,1)S(1)}, bf16[768,1024]{1,0:T(8,128)(2,1)}, u32[]{:S(2)}) %copy-start.6) | copy-done | bytes 1572888
  96.5 14.8 %update.1 = bf16[1024,1024]{1,0:T(8,128)(2,1)} custom-call(s32[1024]{0:T(1024)S(1)} %copy-done.11, s32[1024]{0:T(1024)S(1)} %copy-done.12, s32[1024]{0:T(1024)S(1)} %copy-done.13, s32[8]{0:T(128)S(1)} %copy-done.16, bf16[640,8,128]{2,1,0:T(8,128)(2,1)S(1)} %bitcast.20, s32[1024,1]{1,0:T(8,128)S(1)} %copy-done.3, bf16[1024,1024]{1,0:T(8,128)(2,1)S(1)} %copy-done.1, ...), custom_call_target="tpu_custom_call" | custom-call | tf_op jit(solution)/shard_map/update/pallas_call | solution.py:358
Async XLA Ops:
  1.8 20.6 %all-to-all-start = ((s32[128,1,128]{2,1,0:T(1,128)}), s32[128,1,128]{2,1,0:T(1,128)S(1)}, u32[]{:S(2)}, u32[]{:S(2)}) async-start(s32[128,1,128]{2,1,0:T(1,128)} %bitcast.28), calls=%async_computation | async-start | bytes 131072 | tf_op jit(solution)/shard_map/all_to_all | solution.py:298
  22.5 0.6 copy-start.19
  26.8 26.8 %copy-start.4 = (bf16[1024,1024]{1,0:T(8,128)(2,1)S(1)}, bf16[1024,1024]{1,0:T(8,128)(2,1)}, u32[]{:S(2)}) copy-start(bf16[1024,1024]{1,0:T(8,128)(2,1)} %w2_ref.1) | copy-start | bytes 6291460
  26.8 26.8 %copy-start.7 = (bf16[256,128]{1,0:T(8,128)(2,1)S(1)}, bf16[256,128]{1,0:T(8,128)(2,1)}, u32[]{:S(2)}) copy-start(bf16[256,128]{1,0:T(8,128)(2,1)} %feat_ref.1) | copy-start | bytes 196612
  26.8 26.8 %copy-start.9 = (f32[1024]{0:T(1024)S(1)}, f32[1024]{0:T(1024)}, u32[]{:S(2)}) copy-start(f32[1024]{0:T(1024)} %param.18) | copy-start | bytes 12292
  26.8 26.8 %copy-start.10 = (f32[1024]{0:T(1024)S(1)}, f32[1024]{0:T(1024)}, u32[]{:S(2)}) copy-start(f32[1024]{0:T(1024)} %param.20) | copy-start | bytes 12292
  26.8 26.8 %copy-start.14 = (s32[2,256]{1,0:T(2,128)S(1)}, s32[2,256]{1,0:T(2,128)}, u32[]{:S(2)}) copy-start(s32[2,256]{1,0:T(2,128)} %get-tuple-element.20.place_ref) | copy-start | bytes 6148
  53.7 2.3 %copy-start.2 = (bf16[2176,1024]{1,0:T(8,128)(2,1)S(1)}, bf16[2176,1024]{1,0:T(8,128)(2,1)}, u32[]{:S(2)}) copy-start(bf16[2176,1024]{1,0:T(8,128)(2,1)} %w1_ref.1) | copy-start | bytes 13369348
  61.8 30.6 %all-to-all-start.2 = ((bf16[128,5,8,128]{3,2,1,0:T(8,128)(2,1)}), bf16[128,5,8,128]{3,2,1,0:T(8,128)(2,1)S(1)}, u32[]{:S(2)}, u32[]{:S(2)}) async-start(bf16[128,5,8,128]{3,2,1,0:T(8,128)(2,1)} %bitcast.10), calls=%async_computation.2 | async-start | bytes 2621440 | tf_op jit(solution)/shard_map/all_to_all | solution.py:354
  66.5 11.9 %copy-start = (bf16[128,8,8,128]{3,2,1,0:T(8,128)(2,1)S(1)}, bf16[128,8,8,128]{3,2,1,0:T(8,128)(2,1)}, u32[]{:S(2)}) copy-start(bf16[128,8,8,128]{3,2,1,0:T(8,128)(2,1)} %copy.16) | copy-start | bytes 6291460
  78.4 0.7 copy-start.15
  79.0 2.8 %copy-start.17 = (bf16[1024,3072]{1,0:T(8,128)(2,1)S(1)}, bf16[1024,3072]{1,0:T(8,128)(2,1)}, u32[]{:S(2)}) copy-start(bf16[1024,3072]{1,0:T(8,128)(2,1)} %gru_ref.2) | copy-start | bytes 18874372
  81.8 0.7 copy-start.18
  82.5 9.9 %copy-start.8 = (f32[3072]{0:T(1024)S(1)}, f32[3072]{0:T(1024)}, u32[]{:S(2)}) copy-start(f32[3072]{0:T(1024)} %param.23) | copy-start | bytes 36868
  82.5 9.9 %copy-start.11 = (s32[1024]{0:T(1024)S(1)}, s32[1024]{0:T(1024)}, u32[]{:S(2)}) copy-start(s32[1024]{0:T(1024)} %get-tuple-element.16.slot_ref) | copy-start | bytes 12292
  82.5 9.9 %copy-start.12 = (s32[1024]{0:T(1024)S(1)}, s32[1024]{0:T(1024)}, u32[]{:S(2)}) copy-start(s32[1024]{0:T(1024)} %get-tuple-element.17.index_ref) | copy-start | bytes 12292
  82.5 10.0 %copy-start.13 = (s32[1024]{0:T(1024)S(1)}, s32[1024]{0:T(1024)}, u32[]{:S(2)}) copy-start(s32[1024]{0:T(1024)} %get-tuple-element.18.count_ref) | copy-start | bytes 12292
  82.5 10.0 %copy-start.16 = (s32[8]{0:T(128)S(1)}, s32[8]{0:T(128)}, u32[]{:S(2)}) copy-start(s32[8]{0:T(128)} %get-tuple-element.19.size_ref) | copy-start | bytes 100
  91.3 1.1 %copy-start.5 = (bf16[768,1024]{1,0:T(8,128)(2,1)}, bf16[768,1024]{1,0:T(8,128)(2,1)S(1)}, u32[]{:S(2)}) copy-start(bf16[768,1024]{1,0:T(8,128)(2,1)S(1)} %get-tuple-element.23.previous_ref) | copy-start | bytes 4718596
  92.5 1.6 %copy-start.1 = (bf16[1024,1024]{1,0:T(8,128)(2,1)S(1)}, bf16[1024,1024]{1,0:T(8,128)(2,1)}, u32[]{:S(2)}) copy-start(bf16[1024,1024]{1,0:T(8,128)(2,1)} %memory_ref.1) | copy-start | bytes 6291460
  94.1 1.0 copy-start.3
  95.1 1.4 %copy-start.6 = (bf16[768,1024]{1,0:T(8,128)(2,1)S(1)}, bf16[768,1024]{1,0:T(8,128)(2,1)}, u32[]{:S(2)}) copy-start(bf16[768,1024]{1,0:T(8,128)(2,1)} %copy-done.5) | copy-start | bytes 4718596

commit v2 on v1

v2 whole, which is shorter than its diff:
```python
import jax
import jax.numpy as jnp
from jax import lax
from jax.experimental import pallas as pl
from jax.experimental.pallas import tpu as pltpu
from jax.sharding import PartitionSpec as P

AXES = ("node", "tm")
LANES = 128
SUB = 8
ACTIVE = 1024
TILE = 256
COLS = 256
UNROLL = 16
MIB = 1 << 20
WHOLE = 58 * MIB
MOST = 51 * MIB
ANSWER = 51968 * 1024

VM = pl.BlockSpec(memory_space=pltpu.VMEM)
SM = pl.BlockSpec(memory_space=pltpu.SMEM)
HBM = pl.BlockSpec(memory_space=pltpu.HBM)


def plan_kernel(capacity, owner_ref, row_ref, mask_ref, ids_ref, place_ref):
    devices = ids_ref.shape[0]
    events = owner_ref.shape[1]
    ends = 2 * events
    owner = jnp.concatenate([owner_ref[0:1, :], owner_ref[1:2, :]], axis=1)
    code = jnp.concatenate([row_ref[0:1, :], row_ref[1:2, :] + ACTIVE * mask_ref[...]], axis=1)
    named = lax.broadcasted_iota(jnp.int32, (devices, ends), 0) == owner
    named_b = named.astype(jnp.float32).astype(jnp.bfloat16)
    before = (
        lax.broadcasted_iota(jnp.int32, (ends, ends), 0) < lax.broadcasted_iota(jnp.int32, (ends, ends), 1)
    ).astype(jnp.float32).astype(jnp.bfloat16)
    count = jnp.dot(named_b, before, preferred_element_type=jnp.float32)
    position = jnp.sum(jnp.where(named, count, 0.0), axis=0, keepdims=True).astype(jnp.int32)
    place = owner * capacity + position
    place_ref[0:1, :] = place[:, :events]
    place_ref[1:2, :] = place[:, events:]
    here = lax.broadcasted_iota(jnp.int32, (LANES, ends), 0) == position
    low = jnp.where(here, (code & 31).astype(jnp.float32), 0.0).astype(jnp.bfloat16)
    high = jnp.where(here, (code >> 5).astype(jnp.float32), 0.0).astype(jnp.bfloat16)
    contract = (((1,), (1,)), ((), ()))
    low_sum = lax.dot_general(named_b, low, contract, preferred_element_type=jnp.float32)
    high_sum = lax.dot_general(named_b, high, contract, preferred_element_type=jnp.float32)
    ids_ref[...] = (low_sum + 32.0 * high_sum).astype(jnp.int32)


def answer_kernel(capacity, ids_ref, memory_ref, out_ref, codes_ref, turned_ref, wanted_ref, rows_ref, load_sem, sems):
    devices = ids_ref.shape[0]
    turned = jnp.transpose(ids_ref[...])[:SUB, :]
    codes_ref[...] = turned
    turned_ref[...] = turned
    load = pltpu.make_async_copy(turned_ref, wanted_ref, load_sem)
    load.start()
    load.wait()
    group = 8
    chunks = sems.shape[0]
    part = devices // chunks
    sends = []
    for q in range(chunks):

        def step(i, carry):
            for a in range(group):
                p = q * part + i * group + a
                for k in range(capacity):
                    rows_ref[p * capacity + k] = memory_ref[wanted_ref[k, p] & (ACTIVE - 1)]
            return carry

        lax.fori_loop(0, part // group, step, 0)
        here = pl.ds(q * part * capacity, part * capacity)
        send = pltpu.make_async_copy(rows_ref.at[here], out_ref.at[here], sems.at[q])
        send.start()
        sends.append(send)
    for send in sends:
        send.wait()


def compact_kernel(capacity, spare_row, ids_ref, slot_ref, index_ref, count_ref, node_ref, of_ref, size_ref):
    devices = ids_ref.shape[1]
    rows = of_ref.shape[0]

    def clear(i, carry):
        for a in range(16):
            of_ref[i * 16 + a] = -1
        return carry

    lax.fori_loop(0, rows // 16, clear, 0)

    def step(p, carry):
        taken, nodes = carry
        for k in range(capacity):
            code = ids_ref[k, p]
            active = code >= ACTIVE
            node = code & (ACTIVE - 1)
            known = of_ref[node]
            fresh = active & (known < 0)
            index = jnp.where(known < 0, nodes, known)
            of_ref[node] = jnp.where(active, index, known)
            slot_ref[taken] = p * capacity + k
            index_ref[taken] = index
            old = count_ref[index]
            was = jnp.where(known < 0, 0, old)
            count_ref[index] = jnp.where(active, was + 1, was)
            node_ref[index] = jnp.where(fresh, node, jnp.where(known < 0, 0, node_ref[index]))
            taken = taken + active.astype(jnp.int32)
            nodes = nodes + fresh.astype(jnp.int32)
        return taken, nodes

    taken, nodes = lax.fori_loop(0, devices, step, (jnp.int32(0), jnp.int32(0)))
    size_ref[0] = taken
    size_ref[1] = nodes
    for a in range(UNROLL):
        slot_ref[taken + a] = 0
        index_ref[taken + a] = spare_row
        count_ref[nodes + a] = 1


def to_matrix(tiles_ref, start, rows):
    parts = [tiles_ref[pl.ds(start * SUB + c, rows, stride=SUB), :].astype(jnp.bfloat16) for c in range(SUB)]
    return jnp.concatenate(parts, axis=1)


def hidden_gates_kernel(
    node_ref, size_ref, memory_ref, gru_ref, previous_ref, gates_ref, tiles_ref, rows_ref, made_ref, sems
):
    steps = jnp.maximum(pl.cdiv(size_ref[1], TILE), 1)
    width = rows_ref.shape[1]

    def block(t, carry):
        def copy(i, c):
            for a in range(16):
                u = i * 16 + a
                row = node_ref[t * TILE + u] & (ACTIVE - 1)
                tiles_ref[pl.ds(pl.multiple_of(u * SUB, SUB), SUB), :] = memory_ref[row].astype(jnp.float32)
            return c

        lax.fori_loop(0, TILE // 16, copy, 0)
        here = pl.ds(pl.multiple_of(t * TILE, TILE), TILE)
        rows_ref[...] = to_matrix(tiles_ref, 0, TILE)
        for j in range(width // COLS):
            for g in range(3):
                made_ref[:, (j * 3 + g) * COLS : (j * 3 + g + 1) * COLS] = jnp.dot(
                    rows_ref[...],
                    gru_ref[:, g * width + j * COLS : g * width + (j + 1) * COLS],
                    preferred_element_type=jnp.float32,
                )
        first = pltpu.make_async_copy(rows_ref, previous_ref.at[here], sems.at[0])
        second = pltpu.make_async_copy(made_ref, gates_ref.at[here], sems.at[1])
        first.start()
        second.start()
        first.wait()
        second.wait()
        return carry

    lax.fori_loop(0, steps, block, 0)


def message_kernel(
    place_ref,
    size_ref,
    rows_ref,
    feat_ref,
    w1_hbm,
    b1_ref,
    w2_hbm,
    b2_ref,
    out_ref,
    w1_ref,
    w2_ref,
    tiles_ref,
    inputs_ref,
    hidden_ref,
    sent_ref,
    sem,
    sems,
):
    events = feat_ref.shape[0]
    hid, width = w2_ref.shape
    group = 16
    parts = hid // COLS
    loads = []
    for source, target in ((w1_hbm, w1_ref), (w2_hbm, w2_ref)):
        for j in range(source.shape[1] // COLS):
            cols = pl.ds(j * COLS, COLS)
            load = pltpu.make_async_copy(source.at[:, cols], target.at[:, cols], sems.at[len(loads)])
            load.start()
            loads.append(load)
    for half in range(2):

        def fetch(i, c):
            for a in range(group):
                e = i * group + a
                tiles_ref[pl.ds(pl.multiple_of(e * SUB, SUB), SUB), :] = rows_ref[place_ref[half, e]].astype(
                    jnp.float32
                )
            return c

        lax.fori_loop(0, events // group, fetch, 0)
        inputs_ref[:, half * width : (half + 1) * width] = to_matrix(tiles_ref, 0, events)
    inputs_ref[:, 2 * width :] = feat_ref[...]
    for j in range(parts):
        cols = slice(j * COLS, (j + 1) * COLS)
        loads[j].wait()
        h = jnp.dot(inputs_ref[...], w1_ref[:, cols], preferred_element_type=jnp.float32) + b1_ref[:, cols]
        hidden_ref[:, cols] = jnp.maximum(h, 0.0).astype(jnp.bfloat16)
    for j in range(width // COLS):
        cols = slice(j * COLS, (j + 1) * COLS)
        loads[parts + j].wait()
        m = jnp.dot(hidden_ref[...], w2_ref[:, cols], preferred_element_type=jnp.float32) + b2_ref[:, cols]
        for c in range(COLS // LANES):
            tiles_ref[pl.ds(j * (COLS // LANES) + c, events, stride=SUB), :] = m[:, c * LANES : (c + 1) * LANES]

    def send(i, c):
        for a in range(group):
            e = i * group + a
            sent_ref[place_ref[1, e]] = tiles_ref[pl.ds(pl.multiple_of(e * SUB, SUB), SUB), :].astype(jnp.bfloat16)
        return c

    lax.fori_loop(0, events // group, send, 0)
    leave = pltpu.make_async_copy(sent_ref, out_ref, sem)
    leave.start()
    leave.wait()


def update_kernel(
    slot_ref,
    index_ref,
    count_ref,
    size_ref,
    incoming_ref,
    of_hbm,
    memory_hbm,
    previous_hbm,
    gates_hbm,
    gru_hbm,
    bias_ref,
    out_ref,
    of_ref,
    memory_ref,
    previous_ref,
    gates_ref,
    gru_ref,
    even_ref,
    odd_ref,
    aggregate_ref,
    renewed_ref,
    load_sems,
    sems,
):
    width = memory_ref.shape[1]
    taken = size_ref[0]
    nodes = size_ref[1]
    steps = jnp.maximum(pl.cdiv(nodes, TILE), 1)
    parts = width // COLS

    def load(source, target):
        copy = pltpu.make_async_copy(source, target, load_sems.at[len(loads)])
        loads.append(copy)
        return copy

    loads, early = [], []
    first = load(previous_hbm.at[pl.ds(0, TILE)], previous_ref)
    for j in range(parts):
        block_cols = pl.ds(j * 3 * COLS, 3 * COLS)
        group = [load(gates_hbm.at[pl.ds(0, TILE), block_cols], gates_ref.at[:, block_cols])]
        for g in range(3):
            cols = pl.ds(g * width + j * COLS, COLS)
            group.append(load(gru_hbm.at[:, cols], gru_ref.at[:, cols]))
        early.append(group)
    early[0].append(first)
    late = [load(of_hbm, of_ref), load(memory_hbm, memory_ref)]
    for copy in loads:
        copy.start()

    def clear(t, c):
        here = pl.ds(pl.multiple_of(t * TILE * SUB, TILE * SUB), TILE * SUB)
        even_ref[here, :] = jnp.zeros((TILE * SUB, LANES), jnp.float32)
        odd_ref[here, :] = jnp.zeros((TILE * SUB, LANES), jnp.float32)
        return c

    lax.fori_loop(0, steps, clear, 0)

    def add(i, c):
        for a in range(UNROLL):
            into = odd_ref if a % 2 else even_ref
            here = pl.ds(pl.multiple_of(index_ref[i * UNROLL + a] * SUB, SUB), SUB)
            into[here, :] += incoming_ref[slot_ref[i * UNROLL + a]].astype(jnp.float32)
        return c

    lax.fori_loop(0, pl.cdiv(taken, UNROLL), add, 0)

    def mean(i, c):
        for a in range(UNROLL):
            u = i * UNROLL + a
            here = pl.ds(pl.multiple_of(u * SUB, SUB), SUB)
            even_ref[here, :] = (even_ref[here, :] + odd_ref[here, :]) / count_ref[u].astype(jnp.float32)
        return c

    lax.fori_loop(0, pl.cdiv(nodes, UNROLL), mean, 0)

    def block(t, c):
        here = pl.ds(pl.multiple_of(t * TILE, TILE), TILE)

        @pl.when(t > 0)
        def _():
            again = [
                pltpu.make_async_copy(previous_hbm.at[here], previous_ref, load_sems.at[0]),
                pltpu.make_async_copy(gates_hbm.at[here], gates_ref, load_sems.at[1]),
            ]
            for copy in again:
                copy.start()
            for copy in again:
                copy.wait()

        aggregate_ref[...] = to_matrix(even_ref, pl.multiple_of(t * TILE, TILE), TILE)
        for j in range(parts):

            @pl.when(t == 0)
            def _(j=j):
                for copy in early[j]:
                    copy.wait()

            pre = []
            for g in range(3):
                cols = slice(g * width + j * COLS, g * width + (j + 1) * COLS)
                hid = gates_ref[:, (j * 3 + g) * COLS : (j * 3 + g + 1) * COLS]
                into = (
                    jnp.dot(aggregate_ref[...], gru_ref[:, cols], preferred_element_type=jnp.float32)
                    + bias_ref[:, cols]
                )
                pre.append((into, hid))
            reset = jax.nn.sigmoid(pre[0][0] + pre[0][1])
            update = jax.nn.sigmoid(pre[1][0] + pre[1][1])
            candidate = jnp.tanh(pre[2][0] + reset * pre[2][1])
            previous = previous_ref[:, j * COLS : (j + 1) * COLS].astype(jnp.float32)
            renewed = (1.0 - update) * candidate + update * previous
            renewed_ref[here, j * COLS : (j + 1) * COLS] = renewed.astype(jnp.bfloat16)
        return c

    lax.fori_loop(0, steps, block, 0)
    for copy in late:
        copy.wait()
    bands = sems.shape[0]
    rows = memory_ref.shape[0] // bands
    sends = []
    for i in range(bands):
        here = pl.ds(i * rows, rows)

        def place(t, i=i):
            of = of_ref[i * rows : (i + 1) * rows, :]
            lane = lax.broadcasted_iota(jnp.int32, (rows, TILE), 1) + t * TILE
            pick = (of == lane).astype(jnp.float32).astype(jnp.bfloat16)
            found = jnp.dot(
                pick, renewed_ref[t * TILE : (t + 1) * TILE, :], preferred_element_type=jnp.float32
            )
            mine = (of >= t * TILE) & (of < (t + 1) * TILE)
            kept = memory_ref[i * rows : (i + 1) * rows, :].astype(jnp.float32)
            memory_ref[i * rows : (i + 1) * rows, :] = jnp.where(mine, found, kept).astype(jnp.bfloat16)

        place(0)
        for t in range(1, renewed_ref.shape[0] // TILE):

            @pl.when(t < steps)
            def _():
                place(t)

        send = pltpu.make_async_copy(memory_ref.at[here], out_ref.at[here], sems.at[i])
        send.start()
        sends.append(send)
    for send in sends:
        send.wait()


def on_device(
    memory,
    ends_owner,
    ends_row,
    event_mask,
    edge_feat,
    msg_w1,
    msg_b1,
    msg_w2,
    msg_b2,
    gru_in,
    gru_hid,
    gru_bias,
):
    devices = lax.axis_size(AXES)
    events = ends_owner.shape[0]
    node_rows, width = memory.shape
    hid = msg_w2.shape[0]
    capacity = 5 * events // (2 * devices)
    slots = devices * capacity
    padded = pl.cdiv(slots, TILE) * TILE
    cells = width // LANES
    f32, bf16, i32 = jnp.float32, jnp.bfloat16, jnp.int32
    shape = jax.ShapeDtypeStruct

    ids, place = pl.pallas_call(
        lambda *refs: plan_kernel(capacity, *refs),
        out_shape=(shape((devices, LANES), i32), shape((2, events), i32)),
        in_specs=[VM, VM, VM],
        out_specs=(VM, VM),
        compiler_params=pltpu.CompilerParams(vmem_limit_bytes=WHOLE),
        name="plan",
    )(ends_owner.T, ends_row.T, event_mask.reshape(1, events))

    arrived = lax.all_to_all(
        ids.reshape(devices, 1, LANES), AXES, split_axis=0, concat_axis=0, tiled=True
    ).reshape(devices, LANES)
    tiles = memory.reshape(node_rows, cells, LANES)

    answers, codes = pl.pallas_call(
        lambda *refs: answer_kernel(capacity, *refs),
        out_shape=(shape((slots, cells, LANES), bf16), shape((SUB, devices), i32)),
        in_specs=[VM, VM],
        out_specs=(HBM, VM),
        scratch_shapes=[
            pltpu.VMEM((SUB, devices), i32),
            pltpu.SMEM((SUB, devices), i32),
            pltpu.VMEM((slots, cells, LANES), bf16),
            pltpu.SemaphoreType.DMA,
            pltpu.SemaphoreType.DMA((4,)),
        ],
        compiler_params=pltpu.CompilerParams(vmem_limit_bytes=ANSWER),
        name="answer",
    )(arrived, tiles)
    returned = lax.all_to_all(
        answers.reshape(devices, capacity, cells, LANES), AXES, split_axis=0, concat_axis=0, tiled=True
    ).reshape(slots, cells, LANES)

    slot, index, count, node, of, size = pl.pallas_call(
        lambda *refs: compact_kernel(capacity, padded, *refs),
        out_shape=(
            shape((1024,), i32),
            shape((1024,), i32),
            shape((1024,), i32),
            shape((1024,), i32),
            shape((node_rows,), i32),
            shape((8,), i32),
        ),
        in_specs=[SM],
        out_specs=(SM, SM, SM, SM, SM, SM),
        compiler_params=pltpu.CompilerParams(vmem_limit_bytes=WHOLE),
        cost_estimate=pl.CostEstimate(flops=4_000_000_000, bytes_accessed=20_000_000, transcendentals=0),
        name="compact",
    )(codes)

    previous, gates = pl.pallas_call(
        hidden_gates_kernel,
        out_shape=(shape((padded, width), bf16), shape((padded, 3 * width), f32)),
        in_specs=[SM, SM, VM, VM],
        out_specs=(HBM, HBM),
        scratch_shapes=[
            pltpu.VMEM((TILE * SUB, LANES), f32),
            pltpu.VMEM((TILE, width), bf16),
            pltpu.VMEM((TILE, 3 * width), f32),
            pltpu.SemaphoreType.DMA((2,)),
        ],
        compiler_params=pltpu.CompilerParams(vmem_limit_bytes=WHOLE),
        cost_estimate=pl.CostEstimate(flops=4_000_000_000, bytes_accessed=20_000_000, transcendentals=0),
        name="hidden_gates",
    )(node, size, tiles, gru_hid)

    outgoing = pl.pallas_call(
        message_kernel,
        out_shape=shape((slots, cells, LANES), bf16),
        in_specs=[SM, SM, VM, VM, HBM, VM, HBM, VM],
        out_specs=HBM,
        scratch_shapes=[
            pltpu.VMEM(msg_w1.shape, bf16),
            pltpu.VMEM(msg_w2.shape, bf16),
            pltpu.VMEM((events * SUB, LANES), f32),
            pltpu.VMEM((events, msg_w1.shape[0]), bf16),
            pltpu.VMEM((events, hid), bf16),
            pltpu.VMEM((slots, cells, LANES), bf16),
            pltpu.SemaphoreType.DMA,
            pltpu.SemaphoreType.DMA((hid // COLS + width // COLS,)),
        ],
        compiler_params=pltpu.CompilerParams(vmem_limit_bytes=MOST),
        name="message",
    )(place, size, returned, edge_feat, msg_w1, msg_b1.reshape(1, hid), msg_w2, msg_b2.reshape(1, width))
    incoming = lax.all_to_all(
        outgoing.reshape(devices, capacity, cells, LANES), AXES, split_axis=0, concat_axis=0, tiled=True
    ).reshape(slots, cells, LANES)

    return pl.pallas_call(
        update_kernel,
        out_shape=shape((node_rows, width), bf16),
        in_specs=[SM, SM, SM, SM, VM, HBM, HBM, HBM, HBM, HBM, VM],
        out_specs=HBM,
        scratch_shapes=[
            pltpu.VMEM((node_rows, 1), i32),
            pltpu.VMEM((node_rows, width), bf16),
            pltpu.VMEM((TILE, width), bf16),
            pltpu.VMEM((TILE, 3 * width), f32),
            pltpu.VMEM((width, 3 * width), bf16),
            pltpu.VMEM(((padded + 1) * SUB, LANES), f32),
            pltpu.VMEM(((padded + 1) * SUB, LANES), f32),
            pltpu.VMEM((TILE, width), bf16),
            pltpu.VMEM((padded, width), bf16),
            pltpu.SemaphoreType.DMA((4 * (width // COLS) + 3,)),
            pltpu.SemaphoreType.DMA((8,)),
        ],
        compiler_params=pltpu.CompilerParams(vmem_limit_bytes=MOST),
        name="update",
    )(
        slot,
        index,
        count,
        size,
        incoming,
        of.reshape(node_rows, 1),
        memory,
        previous,
        gates,
        gru_in,
        gru_bias.reshape(1, 3 * width),
    )


def solution(mesh):
    row = P(AXES, None)
    return jax.shard_map(
        on_device,
        mesh=mesh,
        in_specs=(row, row, row, P(AXES), row, P(), P(), P(), P(), P(), P(), P()),
        out_specs=row,
        check_vma=False,
    )
```

time: 112 us -> 99 us (0.88)
  blocking collectives: 26.8 us -> 0 us
  waiting for transfers between devices: 5.94 us -> 32.1 us
  local copies, waits for them, and re-layouts: 17.5 us -> 5.02 us
  starting transfers between devices: 15.8 us -> 20.4 us
  Pallas kernels: 45.2 us -> 40.7 us
    all_to_all x1 -> x0, blocking collectives: 26.8 us -> none  [on_device(): lax.all_to_all(answers.reshape(devices, capacity, cells, LANES), AXES, sp...]
    all_to_all x1, waiting for transfers between devices: 0.01 us -> 14 us  [on_device(): lax.all_to_all(outgoing.reshape(devices, capacity, cells, LANES), AXES, s...]
    all_to_all x0 -> x1, waiting for transfers between devices: none -> 12.1 us  [on_device(): lax.all_to_all(answers.reshape(devices, capacity, cells, LANES), AXES, sp...]
    unnamed x41 -> x25, local copies, waits for them, and re-layouts: 15.8 us -> 4.79 us
    pallas_call x1, Pallas kernels: 14.8 us -> 8.76 us  [on_device(): pl.pallas_call(update_kernel, out_shape=shape((node_rows, width), bf16),...]
    all_to_all x0 -> x1, starting transfers between devices: none -> 4.63 us  [on_device(): lax.all_to_all(answers.reshape(devices, capacity, cells, LANES), AXES, sp...]
    pallas_call x1, Pallas kernels: 5.91 us -> 8.82 us  [on_device(): pl.pallas_call(message_kernel, out_shape=shape((slots, cells, LANES), bf1...]
    reshape x1, local copies, waits for them, and re-layouts: 1.7 us -> 0.22 us  [on_device(): of.reshape(node_rows, 1)]
  transfers between devices with their start and end apart: 2 -> 3, of which waited for: 1 -> 3; matrix products, arithmetic and copies ran while one was open for 5% -> 4% of each run, Pallas kernels for 17% -> 17%
where the time goes in v2:
time: 99 us; the launch traced here: 98.5 us
  Pallas kernels  40.7 us (41%)
  waiting for transfers between devices  32.1 us (32%)
  starting transfers between devices  20.4 us (21%)
  local copies, waits for them, and re-layouts  5.02 us (5%)
    all_to_all x1, waiting for transfers between devices, on_device(): lax.all_to_all(outgoing.reshape(devices, capacity, cells, LANES), AXES, s...  14 us
    all_to_all x1, waiting for transfers between devices, on_device(): lax.all_to_all(answers.reshape(devices, capacity, cells, LANES), AXES, sp...  12.1 us
    all_to_all x1, starting transfers between devices, on_device(): lax.all_to_all(ids.reshape(devices, 1, LANES), AXES, split_axis=0, concat...  11.1 us
    pallas_call x1, Pallas kernels, on_device(): pl.pallas_call(lambda *refs: compact_kernel(capacity, padded, *refs), out...  9.58 us
    pallas_call x1, Pallas kernels, on_device(): pl.pallas_call(message_kernel, out_shape=shape((slots, cells, LANES), bf1...  8.82 us
    pallas_call x1, Pallas kernels, on_device(): pl.pallas_call(update_kernel, out_shape=shape((node_rows, width), bf16),...  8.76 us
    pallas_call x1, Pallas kernels, on_device(): pl.pallas_call(hidden_gates_kernel, out_shape=(shape((padded, width), bf1...  7.48 us
    all_to_all x1, waiting for transfers between devices, on_device(): lax.all_to_all(ids.reshape(devices, 1, LANES), AXES, split_axis=0, concat...  5.94 us
  transfers between devices with their start and end apart: 3, of which 3 were waited for; matrix products, arithmetic and copies ran while one was open for 4% of the time, Pallas kernels for 17%

profile of v2, /device:TPU:0, one launch (start us, length us, event | category | flops | bytes accessed | tf_op | source)
XLA Modules:
  0.0 98.5 jit_solution(8523059735195457254)
XLA Ops:
  0.0 1.8 %plan.1 = (s32[128,128]{1,0:T(8,128)}, s32[2,256]{1,0:T(2,128)}) custom-call(s32[2,256]{1,0:T(2,128)} %bitcast.28, s32[2,256]{1,0:T(2,128)} %bitcast.29, s32[1,256]{1,0:T(1,128)} %bitcast.30), custom_call_target="tpu_custom_call" | custom-call | tf_op jit(solution)/shard_map/plan/pallas_call | solution.py:401
  1.8 11.1 %all-to-all-start = ((s32[128,1,128]{2,1,0:T(1,128)}), s32[128,1,128]{2,1,0:T(1,128)S(1)}, u32[]{:S(2)}, u32[]{:S(2)}) async-start(s32[128,1,128]{2,1,0:T(1,128)} %bitcast.26), calls=%async_computation | async-start | bytes 131072 | tf_op jit(solution)/shard_map/all_to_all | solution.py:410
  13.0 3.5 %copy.16 = bf16[128,8,8,128]{3,2,1,0:T(8,128)(2,1)} copy(bf16[128,8,8,128]{3,1,2,0:T(8,128)(2,1)} %bitcast.25) | data formatting | bytes 4194304
  16.5 5.9 %all-to-all-done = s32[128,1,128]{2,1,0:T(1,128)S(1)} async-done(((s32[128,1,128]{2,1,0:T(1,128)}), s32[128,1,128]{2,1,0:T(1,128)S(1)}, u32[]{:S(2)}, u32[]{:S(2)}) %all-to-all-start) | async-done | bytes 65568 | tf_op jit(solution)/shard_map/all_to_all | solution.py:410
  22.5 4.2 %answer.1 = (bf16[640,8,128]{2,1,0:T(8,128)(2,1)}, s32[8,128]{1,0:T(8,128)S(1)}) custom-call(s32[128,128]{1,0:T(8,128)S(1)} %bitcast.19, bf16[1024,8,128]{2,1,0:T(8,128)(2,1)} %bitcast.23), custom_call_target="tpu_custom_call" | custom-call | tf_op jit(solution)/shard_map/answer/pallas_call | solution.py:415
  26.7 0.0 copy-start.10
  26.7 0.6 copy-done.10
  27.3 4.6 %all-to-all-start.1 = ((bf16[128,5,8,128]{3,2,1,0:T(8,128)(2,1)}), bf16[128,5,8,128]{3,2,1,0:T(8,128)(2,1)S(1)}, u32[]{:S(2)}, u32[]{:S(2)}) async-start(bf16[128,5,8,128]{3,2,1,0:T(8,128)(2,1)} %bitcast.6), calls=%async_computation.1 | async-start | bytes 2621440 | tf_op jit(solution)/shard_map/all_to_all | solution.py:430
  31.9 0.0 copy-start
  31.9 0.0 copy-start.2
  31.9 0.0 copy-start.3
  31.9 0.0 copy-start.7
  31.9 9.6 %compact.1 = (s32[1024]{0:T(1024)}, s32[1024]{0:T(1024)}, s32[1024]{0:T(1024)}, s32[1024]{0:T(1024)}, s32[1024]{0:T(1024)}, /*index=5*/s32[8]{0:T(128)}) custom-call(s32[8,128]{1,0:T(8,128)} %copy-done.10), custom_call_target="tpu_custom_call" | custom-call | flops 4000000000 | bytes 20000000 | tf_op jit(solution)/shard_map/compact/pallas_call | solution.py:434
  41.5 12.1 %all-to-all-done.1 = bf16[128,5,8,128]{3,2,1,0:T(8,128)(2,1)S(1)} async-done(((bf16[128,5,8,128]{3,2,1,0:T(8,128)(2,1)}), bf16[128,5,8,128]{3,2,1,0:T(8,128)(2,1)S(1)}, u32[]{:S(2)}, u32[]{:S(2)}) %all-to-all-start.1) | async-done | bytes 1310752 | tf_op jit(solution)/shard_map/all_to_all | solution.py:430
  53.7 0.0 copy-done
  53.7 0.0 copy-done.2
  53.7 0.0 copy-done.3
  53.7 0.0 copy-done.7
  53.7 0.0 copy-start.8
  53.7 0.6 copy-done.8
  54.3 8.8 %message.1 = bf16[640,8,128]{2,1,0:T(8,128)(2,1)} custom-call(s32[2,256]{1,0:T(2,128)S(1)} %copy-done.7, s32[8]{0:T(128)S(1)} %copy-done.8, bf16[640,8,128]{2,1,0:T(8,128)(2,1)S(1)} %bitcast.17, bf16[256,128]{1,0:T(8,128)(2,1)S(1)} %copy-done, bf16[2176,1024]{1,0:T(8,128)(2,1)} %w1_hbm.1, f32[1,1024]{1,0:T(1,128)S(1)} %bitcast.21, ...), custom_call_target="tpu_custom_call" | custom-call | tf_op jit(solution)/shard_map/message/pallas_call | solution.py:467
  63.1 0.0 copy-start.11
  63.1 4.7 %all-to-all-start.2 = ((bf16[128,5,8,128]{3,2,1,0:T(8,128)(2,1)}), bf16[128,5,8,128]{3,2,1,0:T(8,128)(2,1)S(1)}, u32[]{:S(2)}, u32[]{:S(2)}) async-start(bf16[128,5,8,128]{3,2,1,0:T(8,128)(2,1)} %bitcast.10), calls=%async_computation.2 | async-start | bytes 2621440 | tf_op jit(solution)/shard_map/all_to_all | solution.py:485
  67.8 0.0 copy-done.11
  67.8 0.2 copy.15.of_hbm
  68.0 0.0 copy-start.1
  68.1 0.0 copy-start.4
  68.1 0.0 copy-start.5
  68.1 0.0 copy-start.6
  68.1 0.0 copy-start.9
  68.1 7.5 %hidden_gates.1 = (bf16[768,1024]{1,0:T(8,128)(2,1)}, f32[768,3072]{1,0:T(8,128)}) custom-call(s32[1024]{0:T(1024)} %get-tuple-element.26.node_ref, s32[8]{0:T(128)} %get-tuple-element.22.size_ref, bf16[1024,8,128]{2,1,0:T(8,128)(2,1)} %bitcast.24, bf16[1024,3072]{1,0:T(8,128)(2,1)} %gru_ref.1), custom_call_target="tpu_custom_call" | custom-call | flops 4000000000 | bytes 20000000 | tf_op jit(solution)/shard_map/hidden_gates/pallas_call | solution.py:451
  75.6 14.0 %all-to-all-done.2 = bf16[128,5,8,128]{3,2,1,0:T(8,128)(2,1)S(1)} async-done(((bf16[128,5,8,128]{3,2,1,0:T(8,128)(2,1)}), bf16[128,5,8,128]{3,2,1,0:T(8,128)(2,1)S(1)}, u32[]{:S(2)}, u32[]{:S(2)}) %all-to-all-start.2) | async-done | bytes 1310752 | tf_op jit(solution)/shard_map/all_to_all | solution.py:485
  89.6 0.0 copy-done.1
  89.6 0.0 copy-done.4
  89.6 0.0 copy-done.5
  89.6 0.0 copy-done.6
  89.6 0.0 copy-done.9
  89.6 8.8 %update.1 = bf16[1024,1024]{1,0:T(8,128)(2,1)} custom-call(s32[1024]{0:T(1024)S(1)} %copy-done.4, s32[1024]{0:T(1024)S(1)} %copy-done.5, s32[1024]{0:T(1024)S(1)} %copy-done.6, s32[8]{0:T(128)S(1)} %copy-done.9, bf16[640,8,128]{2,1,0:T(8,128)(2,1)S(1)} %bitcast.18, s32[1024,1]{1,0:T(8,128)S(1)} %copy.15.of_hbm, bf16[1024,1024]{1,0:T(8,128)(2,1)} %memory_hbm.1, ...), custom_call_target="tpu_custom_call" | custom-call | tf_op jit(solution)/shard_map/update/pallas_call | solution.py:489
Async XLA Ops:
  1.8 20.6 %all-to-all-start = ((s32[128,1,128]{2,1,0:T(1,128)}), s32[128,1,128]{2,1,0:T(1,128)S(1)}, u32[]{:S(2)}, u32[]{:S(2)}) async-start(s32[128,1,128]{2,1,0:T(1,128)} %bitcast.26), calls=%async_computation | async-start | bytes 131072 | tf_op jit(solution)/shard_map/all_to_all | solution.py:410
  26.7 0.6 copy-start.10
  27.3 26.4 %all-to-all-start.1 = ((bf16[128,5,8,128]{3,2,1,0:T(8,128)(2,1)}), bf16[128,5,8,128]{3,2,1,0:T(8,128)(2,1)S(1)}, u32[]{:S(2)}, u32[]{:S(2)}) async-start(bf16[128,5,8,128]{3,2,1,0:T(8,128)(2,1)} %bitcast.6), calls=%async_computation.1 | async-start | bytes 2621440 | tf_op jit(solution)/shard_map/all_to_all | solution.py:430
  31.9 21.8 %copy-start = (bf16[256,128]{1,0:T(8,128)(2,1)S(1)}, bf16[256,128]{1,0:T(8,128)(2,1)}, u32[]{:S(2)}) copy-start(bf16[256,128]{1,0:T(8,128)(2,1)} %feat_ref.1) | copy-start | bytes 196612
  31.9 21.8 %copy-start.2 = (f32[1024]{0:T(1024)S(1)}, f32[1024]{0:T(1024)}, u32[]{:S(2)}) copy-start(f32[1024]{0:T(1024)} %param.18) | copy-start | bytes 12292
  31.9 21.8 %copy-start.3 = (f32[1024]{0:T(1024)S(1)}, f32[1024]{0:T(1024)}, u32[]{:S(2)}) copy-start(f32[1024]{0:T(1024)} %param.20) | copy-start | bytes 12292
  31.9 21.7 %copy-start.7 = (s32[2,256]{1,0:T(2,128)S(1)}, s32[2,256]{1,0:T(2,128)}, u32[]{:S(2)}) copy-start(s32[2,256]{1,0:T(2,128)} %get-tuple-element.23.place_ref) | copy-start | bytes 6148
  53.7 0.6 copy-start.8
  63.1 4.7 %copy-start.11 = (s32[1024]{0:T(1024)S(1)}, s32[1024]{0:T(1024)}, u32[]{:S(2)}) copy-start(s32[1024]{0:T(1024)} %get-tuple-element.25) | copy-start | bytes 12292
  63.1 26.4 %all-to-all-start.2 = ((bf16[128,5,8,128]{3,2,1,0:T(8,128)(2,1)}), bf16[128,5,8,128]{3,2,1,0:T(8,128)(2,1)S(1)}, u32[]{:S(2)}, u32[]{:S(2)}) async-start(bf16[128,5,8,128]{3,2,1,0:T(8,128)(2,1)} %bitcast.10), calls=%async_computation.2 | async-start | bytes 2621440 | tf_op jit(solution)/shard_map/all_to_all | solution.py:485
  68.0 21.5 %copy-start.1 = (f32[3072]{0:T(1024)S(1)}, f32[3072]{0:T(1024)}, u32[]{:S(2)}) copy-start(f32[3072]{0:T(1024)} %param.23) | copy-start | bytes 36868
  68.1 21.5 %copy-start.4 = (s32[1024]{0:T(1024)S(1)}, s32[1024]{0:T(1024)}, u32[]{:S(2)}) copy-start(s32[1024]{0:T(1024)} %get-tuple-element.19.slot_ref) | copy-start | bytes 12292
  68.1 21.5 %copy-start.5 = (s32[1024]{0:T(1024)S(1)}, s32[1024]{0:T(1024)}, u32[]{:S(2)}) copy-start(s32[1024]{0:T(1024)} %get-tuple-element.20.index_ref) | copy-start | bytes 12292
  68.1 21.5 %copy-start.6 = (s32[1024]{0:T(1024)S(1)}, s32[1024]{0:T(1024)}, u32[]{:S(2)}) copy-start(s32[1024]{0:T(1024)} %get-tuple-element.21.count_ref) | copy-start | bytes 12292
  68.1 21.5 %copy-start.9 = (s32[8]{0:T(128)S(1)}, s32[8]{0:T(128)}, u32[]{:S(2)}) copy-start(s32[8]{0:T(128)} %get-tuple-element.22.size_ref) | copy-start | bytes 100

commit v3 on v2

--- a/solution.py
+++ b/solution.py
@@ -159,7 +159,6 @@
 
 def message_kernel(
     place_ref,
-    size_ref,
     rows_ref,
     feat_ref,
     w1_hbm,
@@ -179,14 +178,11 @@
     events = feat_ref.shape[0]
     hid, width = w2_ref.shape
     group = 16
-    parts = hid // COLS
     loads = []
     for source, target in ((w1_hbm, w1_ref), (w2_hbm, w2_ref)):
-        for j in range(source.shape[1] // COLS):
-            cols = pl.ds(j * COLS, COLS)
-            load = pltpu.make_async_copy(source.at[:, cols], target.at[:, cols], sems.at[len(loads)])
-            load.start()
-            loads.append(load)
+        load = pltpu.make_async_copy(source, target, sems.at[len(loads)])
+        load.start()
+        loads.append(load)
     for half in range(2):
 
         def fetch(i, c):
@@ -200,14 +196,14 @@
         lax.fori_loop(0, events // group, fetch, 0)
         inputs_ref[:, half * width : (half + 1) * width] = to_matrix(tiles_ref, 0, events)
     inputs_ref[:, 2 * width :] = feat_ref[...]
-    for j in range(parts):
+    loads[0].wait()
+    for j in range(hid // COLS):
         cols = slice(j * COLS, (j + 1) * COLS)
-        loads[j].wait()
         h = jnp.dot(inputs_ref[...], w1_ref[:, cols], preferred_element_type=jnp.float32) + b1_ref[:, cols]
         hidden_ref[:, cols] = jnp.maximum(h, 0.0).astype(jnp.bfloat16)
+    loads[1].wait()
     for j in range(width // COLS):
         cols = slice(j * COLS, (j + 1) * COLS)
-        loads[parts + j].wait()
         m = jnp.dot(hidden_ref[...], w2_ref[:, cols], preferred_element_type=jnp.float32) + b2_ref[:, cols]
         for c in range(COLS // LANES):
             tiles_ref[pl.ds(j * (COLS // LANES) + c, events, stride=SUB), :] = m[:, c * LANES : (c + 1) * LANES]
@@ -230,14 +226,13 @@
     count_ref,
     size_ref,
     incoming_ref,
-    of_hbm,
+    of_ref,
     memory_hbm,
     previous_hbm,
     gates_hbm,
     gru_hbm,
     bias_ref,
     out_ref,
-    of_ref,
     memory_ref,
     previous_ref,
     gates_ref,
@@ -260,17 +255,13 @@
         loads.append(copy)
         return copy
 
-    loads, early = [], []
-    first = load(previous_hbm.at[pl.ds(0, TILE)], previous_ref)
-    for j in range(parts):
-        block_cols = pl.ds(j * 3 * COLS, 3 * COLS)
-        group = [load(gates_hbm.at[pl.ds(0, TILE), block_cols], gates_ref.at[:, block_cols])]
-        for g in range(3):
-            cols = pl.ds(g * width + j * COLS, COLS)
-            group.append(load(gru_hbm.at[:, cols], gru_ref.at[:, cols]))
-        early.append(group)
-    early[0].append(first)
-    late = [load(of_hbm, of_ref), load(memory_hbm, memory_ref)]
+    loads = []
+    early = [
+        load(gru_hbm, gru_ref),
+        load(gates_hbm.at[pl.ds(0, TILE)], gates_ref),
+        load(previous_hbm.at[pl.ds(0, TILE)], previous_ref),
+    ]
+    late = load(memory_hbm, memory_ref)
     for copy in loads:
         copy.start()
 
@@ -306,8 +297,8 @@
         @pl.when(t > 0)
         def _():
             again = [
-                pltpu.make_async_copy(previous_hbm.at[here], previous_ref, load_sems.at[0]),
                 pltpu.make_async_copy(gates_hbm.at[here], gates_ref, load_sems.at[1]),
+                pltpu.make_async_copy(previous_hbm.at[here], previous_ref, load_sems.at[2]),
             ]
             for copy in again:
                 copy.start()
@@ -316,12 +307,6 @@
 
         aggregate_ref[...] = to_matrix(even_ref, pl.multiple_of(t * TILE, TILE), TILE)
         for j in range(parts):
-
-            @pl.when(t == 0)
-            def _(j=j):
-                for copy in early[j]:
-                    copy.wait()
-
             pre = []
             for g in range(3):
                 cols = slice(g * width + j * COLS, g * width + (j + 1) * COLS)
@@ -339,9 +324,10 @@
             renewed_ref[here, j * COLS : (j + 1) * COLS] = renewed.astype(jnp.bfloat16)
         return c
 
+    for copy in early:
+        copy.wait()
     lax.fori_loop(0, steps, block, 0)
-    for copy in late:
-        copy.wait()
+    late.wait()
     bands = sems.shape[0]
     rows = memory_ref.shape[0] // bands
     sends = []
@@ -464,10 +450,11 @@
         name="hidden_gates",
     )(node, size, tiles, gru_hid)
 
+    returned, size = lax.optimization_barrier((returned, size))
     outgoing = pl.pallas_call(
         message_kernel,
         out_shape=shape((slots, cells, LANES), bf16),
-        in_specs=[SM, SM, VM, VM, HBM, VM, HBM, VM],
+        in_specs=[SM, VM, VM, HBM, VM, HBM, VM],
         out_specs=HBM,
         scratch_shapes=[
             pltpu.VMEM(msg_w1.shape, bf16),
@@ -477,11 +464,11 @@
             pltpu.VMEM((events, hid), bf16),
             pltpu.VMEM((slots, cells, LANES), bf16),
             pltpu.SemaphoreType.DMA,
-            pltpu.SemaphoreType.DMA((hid // COLS + width // COLS,)),
+            pltpu.SemaphoreType.DMA((2,)),
         ],
         compiler_params=pltpu.CompilerParams(vmem_limit_bytes=MOST),
         name="message",
-    )(place, size, returned, edge_feat, msg_w1, msg_b1.reshape(1, hid), msg_w2, msg_b2.reshape(1, width))
+    )(place, returned, edge_feat, msg_w1, msg_b1.reshape(1, hid), msg_w2, msg_b2.reshape(1, width))
     incoming = lax.all_to_all(
         outgoing.reshape(devices, capacity, cells, LANES), AXES, split_axis=0, concat_axis=0, tiled=True
     ).reshape(slots, cells, LANES)
@@ -489,10 +476,9 @@
     return pl.pallas_call(
         update_kernel,
         out_shape=shape((node_rows, width), bf16),
-        in_specs=[SM, SM, SM, SM, VM, HBM, HBM, HBM, HBM, HBM, VM],
+        in_specs=[SM, SM, SM, SM, VM, VM, HBM, HBM, HBM, HBM, VM],
         out_specs=HBM,
         scratch_shapes=[
-            pltpu.VMEM((node_rows, 1), i32),
             pltpu.VMEM((node_rows, width), bf16),
             pltpu.VMEM((TILE, width), bf16),
             pltpu.VMEM((TILE, 3 * width), f32),
@@ -501,7 +487,7 @@
             pltpu.VMEM(((padded + 1) * SUB, LANES), f32),
             pltpu.VMEM((TILE, width), bf16),
             pltpu.VMEM((padded, width), bf16),
-            pltpu.SemaphoreType.DMA((4 * (width // COLS) + 3,)),
+            pltpu.SemaphoreType.DMA((4,)),
             pltpu.SemaphoreType.DMA((8,)),
         ],
         compiler_params=pltpu.CompilerParams(vmem_limit_bytes=MOST),

time: 99 us -> 96.9 us (0.979)
  Pallas kernels: 40.7 us -> 39.4 us
    pallas_call x1, Pallas kernels: 8.82 us -> 6.75 us  [on_device(): pl.pallas_call(message_kernel, out_shape=shape((slots, cells, LANES), bf1...]
    unnamed x25 -> x23, local copies, waits for them, and re-layouts: 4.79 us -> 4.18 us
  transfers between devices with their start and end apart: 3 -> 3, of which waited for: 3 -> 3; matrix products, arithmetic and copies ran while one was open for 4% -> 4% of each run, Pallas kernels for 17% -> 18%
where the time goes in v3:
time: 96.9 us; the launch traced here: 96.4 us
  Pallas kernels  39.4 us (41%)
  waiting for transfers between devices  32.1 us (33%)
  starting transfers between devices  20.4 us (21%)
  local copies, waits for them, and re-layouts  4.4 us (5%)
    all_to_all x1, waiting for transfers between devices, on_device(): lax.all_to_all(outgoing.reshape(devices, capacity, cells, LANES), AXES, s...  14 us
    all_to_all x1, waiting for transfers between devices, on_device(): lax.all_to_all(answers.reshape(devices, capacity, cells, LANES), AXES, sp...  12.1 us
    all_to_all x1, starting transfers between devices, on_device(): lax.all_to_all(ids.reshape(devices, 1, LANES), AXES, split_axis=0, concat...  11.1 us
    pallas_call x1, Pallas kernels, on_device(): pl.pallas_call(lambda *refs: compact_kernel(capacity, padded, *refs), out...  9.58 us
    pallas_call x1, Pallas kernels, on_device(): pl.pallas_call(update_kernel, out_shape=shape((node_rows, width), bf16),...  9.53 us
    pallas_call x1, Pallas kernels, on_device(): pl.pallas_call(hidden_gates_kernel, out_shape=(shape((padded, width), bf1...  7.48 us
    pallas_call x1, Pallas kernels, on_device(): pl.pallas_call(message_kernel, out_shape=shape((slots, cells, LANES), bf1...  6.75 us
    all_to_all x1, waiting for transfers between devices, on_device(): lax.all_to_all(ids.reshape(devices, 1, LANES), AXES, split_axis=0, concat...  5.94 us
  transfers between devices with their start and end apart: 3, of which 3 were waited for; matrix products, arithmetic and copies ran while one was open for 4% of the time, Pallas kernels for 18%

profile of v3, /device:TPU:0, one launch (start us, length us, event | category | flops | bytes accessed | tf_op | source)
XLA Modules:
  0.0 96.4 jit_solution(7690447099525463597)
XLA Ops:
  0.0 1.8 %plan.1 = (s32[128,128]{1,0:T(8,128)}, s32[2,256]{1,0:T(2,128)}) custom-call(s32[2,256]{1,0:T(2,128)} %bitcast.28, s32[2,256]{1,0:T(2,128)} %bitcast.29, s32[1,256]{1,0:T(1,128)} %bitcast.30), custom_call_target="tpu_custom_call" | custom-call | tf_op jit(solution)/shard_map/plan/pallas_call | solution.py:387
  1.8 11.1 %all-to-all-start = ((s32[128,1,128]{2,1,0:T(1,128)}), s32[128,1,128]{2,1,0:T(1,128)S(1)}, u32[]{:S(2)}, u32[]{:S(2)}) async-start(s32[128,1,128]{2,1,0:T(1,128)} %bitcast.26), calls=%async_computation | async-start | bytes 131072 | tf_op jit(solution)/shard_map/all_to_all | solution.py:396
  13.0 3.5 %copy.16 = bf16[128,8,8,128]{3,2,1,0:T(8,128)(2,1)} copy(bf16[128,8,8,128]{3,1,2,0:T(8,128)(2,1)} %bitcast.25) | data formatting | bytes 4194304
  16.5 5.9 %all-to-all-done = s32[128,1,128]{2,1,0:T(1,128)S(1)} async-done(((s32[128,1,128]{2,1,0:T(1,128)}), s32[128,1,128]{2,1,0:T(1,128)S(1)}, u32[]{:S(2)}, u32[]{:S(2)}) %all-to-all-start) | async-done | bytes 65568 | tf_op jit(solution)/shard_map/all_to_all | solution.py:396
  22.4 4.2 %answer.1 = (bf16[640,8,128]{2,1,0:T(8,128)(2,1)}, s32[8,128]{1,0:T(8,128)S(1)}) custom-call(s32[128,128]{1,0:T(8,128)S(1)} %bitcast.19, bf16[1024,8,128]{2,1,0:T(8,128)(2,1)} %bitcast.23), custom_call_target="tpu_custom_call" | custom-call | tf_op jit(solution)/shard_map/answer/pallas_call | solution.py:401
  26.7 0.0 copy-start.9
  26.7 0.6 copy-done.9
  27.2 4.6 %all-to-all-start.1 = ((bf16[128,5,8,128]{3,2,1,0:T(8,128)(2,1)}), bf16[128,5,8,128]{3,2,1,0:T(8,128)(2,1)S(1)}, u32[]{:S(2)}, u32[]{:S(2)}) async-start(bf16[128,5,8,128]{3,2,1,0:T(8,128)(2,1)} %bitcast.6), calls=%async_computation.1 | async-start | bytes 2621440 | tf_op jit(solution)/shard_map/all_to_all | solution.py:416
  31.9 0.0 copy-start
  31.9 0.0 copy-start.2
  31.9 0.0 copy-start.3
  31.9 0.0 copy-start.7
  31.9 9.6 %compact.1 = (s32[1024]{0:T(1024)}, s32[1024]{0:T(1024)}, s32[1024]{0:T(1024)}, s32[1024]{0:T(1024)}, s32[1024]{0:T(1024)}, /*index=5*/s32[8]{0:T(128)}) custom-call(s32[8,128]{1,0:T(8,128)} %copy-done.9), custom_call_target="tpu_custom_call" | custom-call | flops 4000000000 | bytes 20000000 | tf_op jit(solution)/shard_map/compact/pallas_call | solution.py:420
  41.5 12.1 %all-to-all-done.1 = bf16[128,5,8,128]{3,2,1,0:T(8,128)(2,1)S(1)} async-done(((bf16[128,5,8,128]{3,2,1,0:T(8,128)(2,1)}), bf16[128,5,8,128]{3,2,1,0:T(8,128)(2,1)S(1)}, u32[]{:S(2)}, u32[]{:S(2)}) %all-to-all-start.1) | async-done | bytes 1310752 | tf_op jit(solution)/shard_map/all_to_all | solution.py:416
  53.7 0.0 copy-done
  53.7 0.0 copy-done.2
  53.7 0.0 copy-done.3
  53.7 0.0 copy-done.7
  53.7 6.7 %message.1 = bf16[640,8,128]{2,1,0:T(8,128)(2,1)} custom-call(s32[2,256]{1,0:T(2,128)S(1)} %copy-done.7, bf16[640,8,128]{2,1,0:T(8,128)(2,1)S(1)} %bitcast.18, bf16[256,128]{1,0:T(8,128)(2,1)S(1)} %copy-done, bf16[2176,1024]{1,0:T(8,128)(2,1)} %w1_hbm.1, f32[1,1024]{1,0:T(1,128)S(1)} %bitcast.21, bf16[1024,1024]{1,0:T(8,128)(2,1)} %w2_hbm.1, ...), custom_call_target="tpu_custom_call" | custom-call | tf_op jit(solution)/shard_map/message/pallas_call | solution.py:454
  60.4 0.0 copy-start.10
  60.4 4.7 %all-to-all-start.2 = ((bf16[128,5,8,128]{3,2,1,0:T(8,128)(2,1)}), bf16[128,5,8,128]{3,2,1,0:T(8,128)(2,1)S(1)}, u32[]{:S(2)}, u32[]{:S(2)}) async-start(bf16[128,5,8,128]{3,2,1,0:T(8,128)(2,1)} %bitcast.10), calls=%async_computation.2 | async-start | bytes 2621440 | tf_op jit(solution)/shard_map/all_to_all | solution.py:472
  65.1 0.0 copy-done.10
  65.1 0.2 copy.15.of_ref
  65.3 0.0 copy-start.1
  65.4 0.0 copy-start.4
  65.4 0.0 copy-start.5
  65.4 0.0 copy-start.6
  65.4 0.0 copy-start.8
  65.4 7.5 %hidden_gates.1 = (bf16[768,1024]{1,0:T(8,128)(2,1)}, f32[768,3072]{1,0:T(8,128)}) custom-call(s32[1024]{0:T(1024)} %get-tuple-element.30.node_ref, s32[8]{0:T(128)} %get-tuple-element.26.size_ref, bf16[1024,8,128]{2,1,0:T(8,128)(2,1)} %bitcast.24, bf16[1024,3072]{1,0:T(8,128)(2,1)} %gru_ref.1), custom_call_target="tpu_custom_call" | custom-call | flops 4000000000 | bytes 20000000 | tf_op jit(solution)/shard_map/hidden_gates/pallas_call | solution.py:437
  72.9 14.0 %all-to-all-done.2 = bf16[128,5,8,128]{3,2,1,0:T(8,128)(2,1)S(1)} async-done(((bf16[128,5,8,128]{3,2,1,0:T(8,128)(2,1)}), bf16[128,5,8,128]{3,2,1,0:T(8,128)(2,1)S(1)}, u32[]{:S(2)}, u32[]{:S(2)}) %all-to-all-start.2) | async-done | bytes 1310752 | tf_op jit(solution)/shard_map/all_to_all | solution.py:472
  86.9 0.0 copy-done.1
  86.9 0.0 copy-done.4
  86.9 0.0 copy-done.5
  86.9 0.0 copy-done.6
  86.9 0.0 copy-done.8
  86.9 9.5 %update.1 = bf16[1024,1024]{1,0:T(8,128)(2,1)} custom-call(s32[1024]{0:T(1024)S(1)} %copy-done.4, s32[1024]{0:T(1024)S(1)} %copy-done.5, s32[1024]{0:T(1024)S(1)} %copy-done.6, s32[8]{0:T(128)S(1)} %copy-done.8, bf16[640,8,128]{2,1,0:T(8,128)(2,1)S(1)} %bitcast.17, s32[1024,1]{1,0:T(8,128)S(1)} %copy.15.of_ref, bf16[1024,1024]{1,0:T(8,128)(2,1)} %memory_hbm.1, ...), custom_call_target="tpu_custom_call" | custom-call | tf_op jit(solution)/shard_map/update/pallas_call | solution.py:476
Async XLA Ops:
  1.8 20.6 %all-to-all-start = ((s32[128,1,128]{2,1,0:T(1,128)}), s32[128,1,128]{2,1,0:T(1,128)S(1)}, u32[]{:S(2)}, u32[]{:S(2)}) async-start(s32[128,1,128]{2,1,0:T(1,128)} %bitcast.26), calls=%async_computation | async-start | bytes 131072 | tf_op jit(solution)/shard_map/all_to_all | solution.py:396
  26.7 0.6 copy-start.9
  27.2 26.4 %all-to-all-start.1 = ((bf16[128,5,8,128]{3,2,1,0:T(8,128)(2,1)}), bf16[128,5,8,128]{3,2,1,0:T(8,128)(2,1)S(1)}, u32[]{:S(2)}, u32[]{:S(2)}) async-start(bf16[128,5,8,128]{3,2,1,0:T(8,128)(2,1)} %bitcast.6), calls=%async_computation.1 | async-start | bytes 2621440 | tf_op jit(solution)/shard_map/all_to_all | solution.py:416
  31.9 21.8 %copy-start = (bf16[256,128]{1,0:T(8,128)(2,1)S(1)}, bf16[256,128]{1,0:T(8,128)(2,1)}, u32[]{:S(2)}) copy-start(bf16[256,128]{1,0:T(8,128)(2,1)} %feat_ref.1) | copy-start | bytes 196612
  31.9 21.8 %copy-start.2 = (f32[1024]{0:T(1024)S(1)}, f32[1024]{0:T(1024)}, u32[]{:S(2)}) copy-start(f32[1024]{0:T(1024)} %param.18) | copy-start | bytes 12292
  31.9 21.8 %copy-start.3 = (f32[1024]{0:T(1024)S(1)}, f32[1024]{0:T(1024)}, u32[]{:S(2)}) copy-start(f32[1024]{0:T(1024)} %param.20) | copy-start | bytes 12292
  31.9 21.7 %copy-start.7 = (s32[2,256]{1,0:T(2,128)S(1)}, s32[2,256]{1,0:T(2,128)}, u32[]{:S(2)}) copy-start(s32[2,256]{1,0:T(2,128)} %get-tuple-element.27.place_ref) | copy-start | bytes 6148
  60.4 4.7 %copy-start.10 = (s32[1024]{0:T(1024)S(1)}, s32[1024]{0:T(1024)}, u32[]{:S(2)}) copy-start(s32[1024]{0:T(1024)} %get-tuple-element.29) | copy-start | bytes 12292
  60.4 26.4 %all-to-all-start.2 = ((bf16[128,5,8,128]{3,2,1,0:T(8,128)(2,1)}), bf16[128,5,8,128]{3,2,1,0:T(8,128)(2,1)S(1)}, u32[]{:S(2)}, u32[]{:S(2)}) async-start(bf16[128,5,8,128]{3,2,1,0:T(8,128)(2,1)} %bitcast.10), calls=%async_computation.2 | async-start | bytes 2621440 | tf_op jit(solution)/shard_map/all_to_all | solution.py:472
  65.3 21.5 %copy-start.1 = (f32[3072]{0:T(1024)S(1)}, f32[3072]{0:T(1024)}, u32[]{:S(2)}) copy-start(f32[3072]{0:T(1024)} %param.23) | copy-start | bytes 36868
  65.4 21.5 %copy-start.4 = (s32[1024]{0:T(1024)S(1)}, s32[1024]{0:T(1024)}, u32[]{:S(2)}) copy-start(s32[1024]{0:T(1024)} %get-tuple-element.21.slot_ref) | copy-start | bytes 12292
  65.4 21.5 %copy-start.5 = (s32[1024]{0:T(1024)S(1)}, s32[1024]{0:T(1024)}, u32[]{:S(2)}) copy-start(s32[1024]{0:T(1024)} %get-tuple-element.22.index_ref) | copy-start | bytes 12292
  65.4 21.5 %copy-start.6 = (s32[1024]{0:T(1024)S(1)}, s32[1024]{0:T(1024)}, u32[]{:S(2)}) copy-start(s32[1024]{0:T(1024)} %get-tuple-element.23.count_ref) | copy-start | bytes 12292
  65.4 21.5 %copy-start.8 = (s32[8]{0:T(128)S(1)}, s32[8]{0:T(128)}, u32[]{:S(2)}) copy-start(s32[8]{0:T(128)} %get-tuple-element.26.size_ref) | copy-start | bytes 100

commit v4 on v3

--- a/solution.py
+++ b/solution.py
@@ -11,7 +11,9 @@
 ACTIVE = 1024
 TILE = 256
 COLS = 256
+GATES = jnp.bfloat16
 UNROLL = 16
+BAND = 512
 MIB = 1 << 20
 WHOLE = 58 * MIB
 MOST = 51 * MIB
@@ -30,10 +32,16 @@
     code = jnp.concatenate([row_ref[0:1, :], row_ref[1:2, :] + ACTIVE * mask_ref[...]], axis=1)
     named = lax.broadcasted_iota(jnp.int32, (devices, ends), 0) == owner
     named_b = named.astype(jnp.float32).astype(jnp.bfloat16)
-    before = (
-        lax.broadcasted_iota(jnp.int32, (ends, ends), 0) < lax.broadcasted_iota(jnp.int32, (ends, ends), 1)
-    ).astype(jnp.float32).astype(jnp.bfloat16)
-    count = jnp.dot(named_b, before, preferred_element_type=jnp.float32)
+    block = (LANES, LANES)
+    before = lax.broadcasted_iota(jnp.int32, block, 0) < lax.broadcasted_iota(jnp.int32, block, 1)
+    table = jnp.concatenate([before.astype(jnp.float32), jnp.ones(block, jnp.float32)], axis=1).astype(jnp.bfloat16)
+    total = jnp.zeros((devices, LANES), jnp.float32)
+    counts = []
+    for i in range(ends // LANES):
+        both = jnp.dot(named_b[:, i * LANES : (i + 1) * LANES], table, preferred_element_type=jnp.float32)
+        counts.append(both[:, :LANES] + total)
+        total = total + both[:, LANES:]
+    count = jnp.concatenate(counts, axis=1)
     position = jnp.sum(jnp.where(named, count, 0.0), axis=0, keepdims=True).astype(jnp.int32)
     place = owner * capacity + position
     place_ref[0:1, :] = place[:, :events]
@@ -47,14 +55,30 @@
     ids_ref[...] = (low_sum + 32.0 * high_sum).astype(jnp.int32)
 
 
-def answer_kernel(capacity, ids_ref, memory_ref, out_ref, codes_ref, turned_ref, wanted_ref, rows_ref, load_sem, sems):
+def answer_kernel(
+    capacity,
+    ids_ref,
+    memory_hbm,
+    out_ref,
+    codes_ref,
+    memory_ref,
+    turned_ref,
+    wanted_ref,
+    rows_ref,
+    memory_sem,
+    load_sem,
+    sems,
+):
     devices = ids_ref.shape[0]
+    memory_load = pltpu.make_async_copy(memory_hbm, memory_ref, memory_sem)
+    memory_load.start()
     turned = jnp.transpose(ids_ref[...])[:SUB, :]
     codes_ref[...] = turned
     turned_ref[...] = turned
     load = pltpu.make_async_copy(turned_ref, wanted_ref, load_sem)
     load.start()
     load.wait()
+    memory_load.wait()
     group = 8
     chunks = sems.shape[0]
     part = devices // chunks
@@ -77,9 +101,14 @@
         send.wait()
 
 
-def compact_kernel(capacity, spare_row, ids_ref, slot_ref, index_ref, count_ref, node_ref, of_ref, size_ref):
+def compact_kernel(
+    capacity, spare_row, codes_ref, slot_ref, index_ref, count_ref, node_ref, of_ref, size_ref, ids_ref, load_sem
+):
     devices = ids_ref.shape[1]
     rows = of_ref.shape[0]
+    load = pltpu.make_async_copy(codes_ref, ids_ref, load_sem)
+    load.start()
+    load.wait()
 
     def clear(i, carry):
         for a in range(16):
@@ -123,8 +152,24 @@
 
 
 def hidden_gates_kernel(
-    node_ref, size_ref, memory_ref, gru_ref, previous_ref, gates_ref, tiles_ref, rows_ref, made_ref, sems
+    node_ref,
+    size_ref,
+    memory_ref,
+    gru_ref,
+    plain_ref,
+    of_ref,
+    previous_ref,
+    gates_ref,
+    kept_ref,
+    tiles_ref,
+    rows_ref,
+    made_ref,
+    left_ref,
+    sems,
 ):
+    left_ref[...] = jnp.where(of_ref[...] < 0, plain_ref[...].astype(jnp.float32), 0.0).astype(jnp.bfloat16)
+    third = pltpu.make_async_copy(left_ref, kept_ref, sems.at[2])
+    third.start()
     steps = jnp.maximum(pl.cdiv(size_ref[1], TILE), 1)
     width = rows_ref.shape[1]
 
@@ -145,7 +190,7 @@
                     rows_ref[...],
                     gru_ref[:, g * width + j * COLS : g * width + (j + 1) * COLS],
                     preferred_element_type=jnp.float32,
-                )
+                ).astype(made_ref.dtype)
         first = pltpu.make_async_copy(rows_ref, previous_ref.at[here], sems.at[0])
         second = pltpu.make_async_copy(made_ref, gates_ref.at[here], sems.at[1])
         first.start()
@@ -155,6 +200,7 @@
         return carry
 
     lax.fori_loop(0, steps, block, 0)
+    third.wait()
 
 
 def message_kernel(
@@ -227,42 +273,41 @@
     size_ref,
     incoming_ref,
     of_ref,
-    memory_hbm,
+    kept_hbm,
     previous_hbm,
     gates_hbm,
     gru_hbm,
     bias_ref,
     out_ref,
-    memory_ref,
+    final_ref,
     previous_ref,
     gates_ref,
     gru_ref,
     even_ref,
     odd_ref,
     aggregate_ref,
-    renewed_ref,
+    pick_ref,
     load_sems,
     sems,
 ):
-    width = memory_ref.shape[1]
+    width = final_ref.shape[1]
     taken = size_ref[0]
     nodes = size_ref[1]
     steps = jnp.maximum(pl.cdiv(nodes, TILE), 1)
-    parts = width // COLS
-
-    def load(source, target):
-        copy = pltpu.make_async_copy(source, target, load_sems.at[len(loads)])
-        loads.append(copy)
-        return copy
-
-    loads = []
-    early = [
-        load(gru_hbm, gru_ref),
-        load(gates_hbm.at[pl.ds(0, TILE)], gates_ref),
-        load(previous_hbm.at[pl.ds(0, TILE)], previous_ref),
-    ]
-    late = load(memory_hbm, memory_ref)
-    for copy in loads:
+    half = width // 2
+    first_tile = pl.ds(0, TILE)
+    halves = []
+    for h in range(2):
+        loads = [(gates_hbm.at[first_tile, pl.ds(h * 3 * half, 3 * half)], gates_ref.at[:, pl.ds(h * 3 * half, 3 * half)])]
+        for g in range(3):
+            cols = pl.ds(g * width + h * half, half)
+            loads.append((gru_hbm.at[:, cols], gru_ref.at[:, cols]))
+        if h == 0:
+            loads.append((previous_hbm.at[first_tile], previous_ref))
+        else:
+            loads.append((kept_hbm, final_ref))
+        halves.append([pltpu.make_async_copy(a, b, load_sems.at[h, i]) for i, (a, b) in enumerate(loads)])
+    for copy in halves[0] + halves[1]:
         copy.start()
 
     def clear(t, c):
@@ -281,7 +326,6 @@
         return c
 
     lax.fori_loop(0, pl.cdiv(taken, UNROLL), add, 0)
-
     def mean(i, c):
         for a in range(UNROLL):
             u = i * UNROLL + a
@@ -291,70 +335,75 @@
 
     lax.fori_loop(0, pl.cdiv(nodes, UNROLL), mean, 0)
 
-    def block(t, c):
-        here = pl.ds(pl.multiple_of(t * TILE, TILE), TILE)
-
-        @pl.when(t > 0)
-        def _():
+    def prepare(t):
+        aggregate_ref[...] = to_matrix(even_ref, pl.multiple_of(t * TILE, TILE), TILE)
+        lane = lax.broadcasted_iota(jnp.int32, (of_ref.shape[0], TILE), 1) + t * TILE
+        pick_ref[...] = (of_ref[...] == lane).astype(jnp.float32).astype(jnp.bfloat16)
+
+    def renew(j):
+        pre = []
+        for g in range(3):
+            cols = slice(g * width + j * COLS, g * width + (j + 1) * COLS)
+            hid = gates_ref[:, (j * 3 + g) * COLS : (j * 3 + g + 1) * COLS].astype(jnp.float32)
+            into = jnp.dot(aggregate_ref[...], gru_ref[:, cols], preferred_element_type=jnp.float32) + bias_ref[:, cols]
+            pre.append((into, hid))
+        reset = jax.nn.sigmoid(pre[0][0] + pre[0][1])
+        update = jax.nn.sigmoid(pre[1][0] + pre[1][1])
+        candidate = jnp.tanh(pre[2][0] + reset * pre[2][1])
+        previous = previous_ref[:, j * COLS : (j + 1) * COLS].astype(jnp.float32)
+        return ((1.0 - update) * candidate + update * previous).astype(jnp.bfloat16)
+
+    def place(j, renewed):
+        cols = slice(j * COLS, (j + 1) * COLS)
+        for i in range(final_ref.shape[0] // BAND):
+            rows = slice(i * BAND, (i + 1) * BAND)
+            found = jnp.dot(pick_ref[rows, :], renewed, preferred_element_type=jnp.float32)
+            final_ref[rows, cols] = found.astype(jnp.bfloat16) + final_ref[rows, cols]
+
+    per = half // COLS
+    prepare(0)
+    for copy in halves[0]:
+        copy.wait()
+    made = [renew(j) for j in range(per)]
+    for copy in halves[1]:
+        copy.wait()
+    sends = [
+        pltpu.make_async_copy(
+            final_ref.at[:, pl.ds(h * half, half)], out_ref.at[:, pl.ds(h * half, half)], sems.at[h]
+        )
+        for h in range(2)
+    ]
+    for j in range(per):
+        place(j, made[j])
+
+    @pl.when(steps == 1)
+    def _():
+        sends[0].start()
+
+    for j in range(per, 2 * per):
+        place(j, renew(j))
+
+    @pl.when(steps > 1)
+    def _():
+        def block(t, c):
+            here = pl.ds(pl.multiple_of(t * TILE, TILE), TILE)
             again = [
-                pltpu.make_async_copy(gates_hbm.at[here], gates_ref, load_sems.at[1]),
-                pltpu.make_async_copy(previous_hbm.at[here], previous_ref, load_sems.at[2]),
+                pltpu.make_async_copy(gates_hbm.at[here], gates_ref, load_sems.at[0, 0]),
+                pltpu.make_async_copy(previous_hbm.at[here], previous_ref, load_sems.at[0, 1]),
             ]
             for copy in again:
                 copy.start()
+            prepare(t)
             for copy in again:
                 copy.wait()
-
-        aggregate_ref[...] = to_matrix(even_ref, pl.multiple_of(t * TILE, TILE), TILE)
-        for j in range(parts):
-            pre = []
-            for g in range(3):
-                cols = slice(g * width + j * COLS, g * width + (j + 1) * COLS)
-                hid = gates_ref[:, (j * 3 + g) * COLS : (j * 3 + g + 1) * COLS]
-                into = (
-                    jnp.dot(aggregate_ref[...], gru_ref[:, cols], preferred_element_type=jnp.float32)
-                    + bias_ref[:, cols]
-                )
-                pre.append((into, hid))
-            reset = jax.nn.sigmoid(pre[0][0] + pre[0][1])
-            update = jax.nn.sigmoid(pre[1][0] + pre[1][1])
-            candidate = jnp.tanh(pre[2][0] + reset * pre[2][1])
-            previous = previous_ref[:, j * COLS : (j + 1) * COLS].astype(jnp.float32)
-            renewed = (1.0 - update) * candidate + update * previous
-            renewed_ref[here, j * COLS : (j + 1) * COLS] = renewed.astype(jnp.bfloat16)
-        return c
-
-    for copy in early:
-        copy.wait()
-    lax.fori_loop(0, steps, block, 0)
-    late.wait()
-    bands = sems.shape[0]
-    rows = memory_ref.shape[0] // bands
-    sends = []
-    for i in range(bands):
-        here = pl.ds(i * rows, rows)
-
-        def place(t, i=i):
-            of = of_ref[i * rows : (i + 1) * rows, :]
-            lane = lax.broadcasted_iota(jnp.int32, (rows, TILE), 1) + t * TILE
-            pick = (of == lane).astype(jnp.float32).astype(jnp.bfloat16)
-            found = jnp.dot(
-                pick, renewed_ref[t * TILE : (t + 1) * TILE, :], preferred_element_type=jnp.float32
-            )
-            mine = (of >= t * TILE) & (of < (t + 1) * TILE)
-            kept = memory_ref[i * rows : (i + 1) * rows, :].astype(jnp.float32)
-            memory_ref[i * rows : (i + 1) * rows, :] = jnp.where(mine, found, kept).astype(jnp.bfloat16)
-
-        place(0)
-        for t in range(1, renewed_ref.shape[0] // TILE):
-
-            @pl.when(t < steps)
-            def _():
-                place(t)
-
-        send = pltpu.make_async_copy(memory_ref.at[here], out_ref.at[here], sems.at[i])
-        send.start()
-        sends.append(send)
+            for j in range(2 * per):
+                place(j, renew(j))
+            return c
+
+        lax.fori_loop(1, steps, block, 0)
+        sends[0].start()
+
+    sends[1].start()
     for send in sends:
         send.wait()
 
@@ -401,12 +450,14 @@
     answers, codes = pl.pallas_call(
         lambda *refs: answer_kernel(capacity, *refs),
         out_shape=(shape((slots, cells, LANES), bf16), shape((SUB, devices), i32)),
-        in_specs=[VM, VM],
+        in_specs=[VM, HBM],
         out_specs=(HBM, VM),
         scratch_shapes=[
+            pltpu.VMEM((node_rows, cells, LANES), bf16),
             pltpu.VMEM((SUB, devices), i32),
             pltpu.SMEM((SUB, devices), i32),
             pltpu.VMEM((slots, cells, LANES), bf16),
+            pltpu.SemaphoreType.DMA,
             pltpu.SemaphoreType.DMA,
             pltpu.SemaphoreType.DMA((4,)),
         ],
@@ -427,28 +478,35 @@
             shape((node_rows,), i32),
             shape((8,), i32),
         ),
-        in_specs=[SM],
+        in_specs=[VM],
         out_specs=(SM, SM, SM, SM, SM, SM),
-        compiler_params=pltpu.CompilerParams(vmem_limit_bytes=WHOLE),
+        scratch_shapes=[pltpu.SMEM((SUB, devices), i32), pltpu.SemaphoreType.DMA],
+        compiler_params=pltpu.CompilerParams(vmem_limit_bytes=MOST),
         cost_estimate=pl.CostEstimate(flops=4_000_000_000, bytes_accessed=20_000_000, transcendentals=0),
         name="compact",
     )(codes)
 
-    previous, gates = pl.pallas_call(
+    of = of.reshape(node_rows, 1)
+    previous, gates, kept = pl.pallas_call(
         hidden_gates_kernel,
-        out_shape=(shape((padded, width), bf16), shape((padded, 3 * width), f32)),
-        in_specs=[SM, SM, VM, VM],
-        out_specs=(HBM, HBM),
+        out_shape=(
+            shape((padded, width), bf16),
+            shape((padded, 3 * width), GATES),
+            shape((node_rows, width), bf16),
+        ),
+        in_specs=[SM, SM, VM, VM, VM, VM],
+        out_specs=(HBM, HBM, HBM),
         scratch_shapes=[
             pltpu.VMEM((TILE * SUB, LANES), f32),
             pltpu.VMEM((TILE, width), bf16),
-            pltpu.VMEM((TILE, 3 * width), f32),
-            pltpu.SemaphoreType.DMA((2,)),
+            pltpu.VMEM((TILE, 3 * width), GATES),
+            pltpu.VMEM((node_rows, width), bf16),
+            pltpu.SemaphoreType.DMA((3,)),
         ],
         compiler_params=pltpu.CompilerParams(vmem_limit_bytes=WHOLE),
         cost_estimate=pl.CostEstimate(flops=4_000_000_000, bytes_accessed=20_000_000, transcendentals=0),
         name="hidden_gates",
-    )(node, size, tiles, gru_hid)
+    )(node, size, tiles, gru_hid, memory, of)
 
     returned, size = lax.optimization_barrier((returned, size))
     outgoing = pl.pallas_call(
@@ -481,14 +539,14 @@
         scratch_shapes=[
             pltpu.VMEM((node_rows, width), bf16),
             pltpu.VMEM((TILE, width), bf16),
-            pltpu.VMEM((TILE, 3 * width), f32),
+            pltpu.VMEM((TILE, 3 * width), GATES),
             pltpu.VMEM((width, 3 * width), bf16),
             pltpu.VMEM(((padded + 1) * SUB, LANES), f32),
             pltpu.VMEM(((padded + 1) * SUB, LANES), f32),
             pltpu.VMEM((TILE, width), bf16),
-            pltpu.VMEM((padded, width), bf16),
-            pltpu.SemaphoreType.DMA((4,)),
-            pltpu.SemaphoreType.DMA((8,)),
+            pltpu.VMEM((node_rows, TILE), bf16),
+            pltpu.SemaphoreType.DMA((2, 5)),
+            pltpu.SemaphoreType.DMA((2,)),
         ],
         compiler_params=pltpu.CompilerParams(vmem_limit_bytes=MOST),
         name="update",
@@ -498,8 +556,8 @@
         count,
         size,
         incoming,
-        of.reshape(node_rows, 1),
-        memory,
+        of,
+        kept,
         previous,
         gates,
         gru_in,

time: 96.9 us -> 94.5 us (0.975)
  waiting for transfers between devices: 32.1 us -> 30.1 us
  Pallas kernels: 39.4 us -> 37.5 us
  local copies, waits for them, and re-layouts: 4.4 us -> 5.7 us
    all_to_all x1, waiting for transfers between devices: 14 us -> 12.6 us  [on_device(): lax.all_to_all(outgoing.reshape(devices, capacity, cells, LANES), AXES, s...]
    pallas_call x1, Pallas kernels: 9.53 us -> 8.26 us  [on_device(): pl.pallas_call(update_kernel, out_shape=shape((node_rows, width), bf16),...]
    unnamed x23 -> x19, local copies, waits for them, and re-layouts: 4.18 us -> 4.69 us
  transfers between devices with their start and end apart: 3 -> 3, of which waited for: 3 -> 3; matrix products, arithmetic and copies ran while one was open for 4% -> 5% of each run, Pallas kernels for 18% -> 18%
where the time goes in v4:
time: 94.5 us; the launch traced here: 94.1 us
  Pallas kernels  37.5 us (40%)
  waiting for transfers between devices  30.1 us (32%)
  starting transfers between devices  20.4 us (22%)
  local copies, waits for them, and re-layouts  5.7 us (6%)
    all_to_all x1, waiting for transfers between devices, on_device(): lax.all_to_all(outgoing.reshape(devices, capacity, cells, LANES), AXES, s...  12.6 us
    all_to_all x1, waiting for transfers between devices, on_device(): lax.all_to_all(answers.reshape(devices, capacity, cells, LANES), AXES, sp...  11.6 us
    all_to_all x1, starting transfers between devices, on_device(): lax.all_to_all(ids.reshape(devices, 1, LANES), AXES, split_axis=0, concat...  11.1 us
    pallas_call x1, Pallas kernels, on_device(): pl.pallas_call(lambda *refs: compact_kernel(capacity, padded, *refs), out...  8.99 us
    pallas_call x1, Pallas kernels, on_device(): pl.pallas_call(update_kernel, out_shape=shape((node_rows, width), bf16),...  8.26 us
    pallas_call x1, Pallas kernels, on_device(): pl.pallas_call(hidden_gates_kernel, out_shape=(shape((padded, width), bf1...  8.12 us
    pallas_call x1, Pallas kernels, on_device(): pl.pallas_call(message_kernel, out_shape=shape((slots, cells, LANES), bf1...  6.84 us
    all_to_all x1, waiting for transfers between devices, on_device(): lax.all_to_all(ids.reshape(devices, 1, LANES), AXES, split_axis=0, concat...  5.91 us
  transfers between devices with their start and end apart: 3, of which 3 were waited for; matrix products, arithmetic and copies ran while one was open for 5% of the time, Pallas kernels for 18%

profile of v4, /device:TPU:0, one launch (start us, length us, event | category | flops | bytes accessed | tf_op | source)
XLA Modules:
  0.0 94.1 jit_solution(124050580435257895)
XLA Ops:
  0.0 1.8 %plan.1 = (s32[128,128]{1,0:T(8,128)}, s32[2,256]{1,0:T(2,128)}) custom-call(s32[2,256]{1,0:T(2,128)} %bitcast.28, s32[2,256]{1,0:T(2,128)} %bitcast.29, s32[1,256]{1,0:T(1,128)} %bitcast.30), custom_call_target="tpu_custom_call" | custom-call | tf_op jit(solution)/shard_map/plan/pallas_call | solution.py:436
  1.8 11.1 %all-to-all-start = ((s32[128,1,128]{2,1,0:T(1,128)}), s32[128,1,128]{2,1,0:T(1,128)S(1)}, u32[]{:S(2)}, u32[]{:S(2)}) async-start(s32[128,1,128]{2,1,0:T(1,128)} %bitcast.27), calls=%async_computation | async-start | bytes 131072 | tf_op jit(solution)/shard_map/all_to_all | solution.py:445
  12.9 3.5 %copy.18 = bf16[128,8,8,128]{3,2,1,0:T(8,128)(2,1)} copy(bf16[128,8,8,128]{3,1,2,0:T(8,128)(2,1)} %bitcast.26) | data formatting | bytes 4194304
  16.5 5.9 %all-to-all-done = s32[128,1,128]{2,1,0:T(1,128)S(1)} async-done(((s32[128,1,128]{2,1,0:T(1,128)}), s32[128,1,128]{2,1,0:T(1,128)S(1)}, u32[]{:S(2)}, u32[]{:S(2)}) %all-to-all-start) | async-done | bytes 65568 | tf_op jit(solution)/shard_map/all_to_all | solution.py:445
  22.4 3.5 %answer.1 = (bf16[640,8,128]{2,1,0:T(8,128)(2,1)}, s32[8,128]{1,0:T(8,128)S(1)}) custom-call(s32[128,128]{1,0:T(8,128)S(1)} %bitcast.19, bf16[1024,8,128]{2,1,0:T(8,128)(2,1)} %bitcast.24), custom_call_target="tpu_custom_call" | custom-call | tf_op jit(solution)/shard_map/answer/pallas_call | solution.py:450
  25.9 4.7 %all-to-all-start.1 = ((bf16[128,5,8,128]{3,2,1,0:T(8,128)(2,1)}), bf16[128,5,8,128]{3,2,1,0:T(8,128)(2,1)S(1)}, u32[]{:S(2)}, u32[]{:S(2)}) async-start(bf16[128,5,8,128]{3,2,1,0:T(8,128)(2,1)} %bitcast.6), calls=%async_computation.1 | async-start | bytes 2621440 | tf_op jit(solution)/shard_map/all_to_all | solution.py:467
  30.6 0.0 copy-start.1
  30.6 0.0 copy-start.3
  30.6 0.0 copy-start.4
  30.6 0.0 copy-start.5
  30.6 9.0 %compact.1 = (s32[1024]{0:T(1024)S(1)}, s32[1024]{0:T(1024)S(1)}, s32[1024]{0:T(1024)S(1)}, s32[1024]{0:T(1024)S(1)}, s32[1024]{0:T(1024)S(1)}, /*index=5*/s32[8]{0:T(128)S(1)}) custom-call(s32[8,128]{1,0:T(8,128)S(1)} %get-tuple-element.21.refs_0_), custom_call_target="tpu_custom_call" | custom-call | flops 4000000000 | bytes 20000000 | tf_op jit(solution)/shard_map/compact/pallas_call | solution.py:471
  39.6 0.0 copy-start.6
  39.6 0.5 copy-done.6
  40.2 0.0 copy-start.8
  40.2 0.6 copy-done.8
  40.8 11.6 %all-to-all-done.1 = bf16[128,5,8,128]{3,2,1,0:T(8,128)(2,1)S(1)} async-done(((bf16[128,5,8,128]{3,2,1,0:T(8,128)(2,1)}), bf16[128,5,8,128]{3,2,1,0:T(8,128)(2,1)S(1)}, u32[]{:S(2)}, u32[]{:S(2)}) %all-to-all-start.1) | async-done | bytes 1310752 | tf_op jit(solution)/shard_map/all_to_all | solution.py:467
  52.4 0.0 copy-done.1
  52.4 0.0 copy-done.3
  52.4 0.0 copy-done.4
  52.4 0.0 copy-done.5
  52.4 6.8 %message.1 = bf16[640,8,128]{2,1,0:T(8,128)(2,1)} custom-call(s32[2,256]{1,0:T(2,128)S(1)} %copy-done.5, bf16[640,8,128]{2,1,0:T(8,128)(2,1)S(1)} %bitcast.18, bf16[256,128]{1,0:T(8,128)(2,1)S(1)} %copy-done.1, bf16[2176,1024]{1,0:T(8,128)(2,1)} %w1_hbm.1, f32[1,1024]{1,0:T(1,128)S(1)} %bitcast.21, bf16[1024,1024]{1,0:T(8,128)(2,1)} %w2_hbm.1, ...), custom_call_target="tpu_custom_call" | custom-call | tf_op jit(solution)/shard_map/message/pallas_call | solution.py:512
  59.2 4.7 %all-to-all-start.2 = ((bf16[128,5,8,128]{3,2,1,0:T(8,128)(2,1)}), bf16[128,5,8,128]{3,2,1,0:T(8,128)(2,1)S(1)}, u32[]{:S(2)}, u32[]{:S(2)}) async-start(bf16[128,5,8,128]{3,2,1,0:T(8,128)(2,1)} %bitcast.10), calls=%async_computation.2 | async-start | bytes 2621440 | tf_op jit(solution)/shard_map/all_to_all | solution.py:530
  63.9 1.0 %copy.17.of_ref = s32[1024,1]{1,0:T(8,128)} copy(s32[1024,1]{0,1:T(1,128)S(1)} %bitcast.23) | data formatting | bytes 8192 | tf_op jit(solution)/shard_map/reshape | solution.py:489
  64.9 0.0 copy-start
  64.9 0.0 copy-start.2
  64.9 0.0 copy-start.7
  64.9 8.1 %hidden_gates.1 = (bf16[768,1024]{1,0:T(8,128)(2,1)}, bf16[768,3072]{1,0:T(8,128)(2,1)}, bf16[1024,1024]{1,0:T(8,128)(2,1)}) custom-call(s32[1024]{0:T(1024)} %copy-done.8, s32[8]{0:T(128)} %copy-done.6, bf16[1024,8,128]{2,1,0:T(8,128)(2,1)} %bitcast.25, bf16[1024,3072]{1,0:T(8,128)(2,1)} %gru_ref.1, bf16[1024,1024]{1,0:T(8,128)(2,1)} %plain_ref.1, ...), custom_call_target="tpu_custom_call" | custom-call | flops 4000000000 | bytes 20000000 | tf_op jit(solution)/shard_map/hidden_gates/pallas_call | solution.py:490
  73.0 12.6 %all-to-all-done.2 = bf16[128,5,8,128]{3,2,1,0:T(8,128)(2,1)S(1)} async-done(((bf16[128,5,8,128]{3,2,1,0:T(8,128)(2,1)}), bf16[128,5,8,128]{3,2,1,0:T(8,128)(2,1)S(1)}, u32[]{:S(2)}, u32[]{:S(2)}) %all-to-all-start.2) | async-done | bytes 1310752 | tf_op jit(solution)/shard_map/all_to_all | solution.py:530
  85.7 0.0 copy-done
  85.7 0.0 copy-done.2
  85.7 0.0 copy-done.7
  85.7 8.3 %update.1 = bf16[1024,1024]{1,0:T(8,128)(2,1)} custom-call(s32[1024]{0:T(1024)S(1)} %get-tuple-element.22.slot_ref, s32[1024]{0:T(1024)S(1)} %get-tuple-element.23.index_ref, s32[1024]{0:T(1024)S(1)} %get-tuple-element.24.count_ref, s32[8]{0:T(128)S(1)} %copy-done.7, bf16[640,8,128]{2,1,0:T(8,128)(2,1)S(1)} %bitcast.17, s32[1024,1]{1,0:T(8,128)S(1)} %copy-done, ...), custom_call_target="tpu_custom_call" | custom-call | tf_op jit(solution)/shard_map/update/pallas_call | solution.py:534
Async XLA Ops:
  1.8 20.6 %all-to-all-start = ((s32[128,1,128]{2,1,0:T(1,128)}), s32[128,1,128]{2,1,0:T(1,128)S(1)}, u32[]{:S(2)}, u32[]{:S(2)}) async-start(s32[128,1,128]{2,1,0:T(1,128)} %bitcast.27), calls=%async_computation | async-start | bytes 131072 | tf_op jit(solution)/shard_map/all_to_all | solution.py:445
  25.9 26.4 %all-to-all-start.1 = ((bf16[128,5,8,128]{3,2,1,0:T(8,128)(2,1)}), bf16[128,5,8,128]{3,2,1,0:T(8,128)(2,1)S(1)}, u32[]{:S(2)}, u32[]{:S(2)}) async-start(bf16[128,5,8,128]{3,2,1,0:T(8,128)(2,1)} %bitcast.6), calls=%async_computation.1 | async-start | bytes 2621440 | tf_op jit(solution)/shard_map/all_to_all | solution.py:467
  30.6 21.8 %copy-start.1 = (bf16[256,128]{1,0:T(8,128)(2,1)S(1)}, bf16[256,128]{1,0:T(8,128)(2,1)}, u32[]{:S(2)}) copy-start(bf16[256,128]{1,0:T(8,128)(2,1)} %feat_ref.1) | copy-start | bytes 196612
  30.6 21.8 %copy-start.3 = (f32[1024]{0:T(1024)S(1)}, f32[1024]{0:T(1024)}, u32[]{:S(2)}) copy-start(f32[1024]{0:T(1024)} %param.18) | copy-start | bytes 12292
  30.6 21.8 %copy-start.4 = (f32[1024]{0:T(1024)S(1)}, f32[1024]{0:T(1024)}, u32[]{:S(2)}) copy-start(f32[1024]{0:T(1024)} %param.20) | copy-start | bytes 12292
  30.6 21.7 %copy-start.5 = (s32[2,256]{1,0:T(2,128)S(1)}, s32[2,256]{1,0:T(2,128)}, u32[]{:S(2)}) copy-start(s32[2,256]{1,0:T(2,128)} %get-tuple-element.28.place_ref) | copy-start | bytes 6148
  39.6 0.5 copy-start.6
  40.2 0.6 copy-start.8
  59.2 26.4 %all-to-all-start.2 = ((bf16[128,5,8,128]{3,2,1,0:T(8,128)(2,1)}), bf16[128,5,8,128]{3,2,1,0:T(8,128)(2,1)S(1)}, u32[]{:S(2)}, u32[]{:S(2)}) async-start(bf16[128,5,8,128]{3,2,1,0:T(8,128)(2,1)} %bitcast.10), calls=%async_computation.2 | async-start | bytes 2621440 | tf_op jit(solution)/shard_map/all_to_all | solution.py:530
  64.9 20.8 %copy-start = (s32[1024,1]{1,0:T(8,128)S(1)}, s32[1024,1]{1,0:T(8,128)}, u32[]{:S(2)}) copy-start(s32[1024,1]{1,0:T(8,128)} %copy.17.of_ref) | copy-start | bytes 12292
  64.9 20.8 %copy-start.2 = (f32[3072]{0:T(1024)S(1)}, f32[3072]{0:T(1024)}, u32[]{:S(2)}) copy-start(f32[3072]{0:T(1024)} %param.23) | copy-start | bytes 36868
  64.9 20.8 %copy-start.7 = (s32[8]{0:T(128)S(1)}, s32[8]{0:T(128)}, u32[]{:S(2)}) copy-start(s32[8]{0:T(128)} %copy-done.6) | copy-start | bytes 100

commit v5 on v4

--- a/solution.py
+++ b/solution.py
@@ -203,30 +203,39 @@
     third.wait()
 
 
+def fold_kernel(w2_ref, b2_ref, gru_ref, bias_ref, folded_ref, shift_ref):
+    folded_ref[...] = jnp.dot(w2_ref[...], gru_ref[...], preferred_element_type=jnp.float32).astype(jnp.bfloat16)
+    rest = jnp.broadcast_to(b2_ref[...], (SUB, b2_ref.shape[1]))
+    shift = bias_ref[...]
+    for i in range(3):
+        term = rest.astype(jnp.bfloat16)
+        shift = shift + jnp.dot(term, gru_ref[...], preferred_element_type=jnp.float32)[0:1, :]
+        rest = rest - term.astype(jnp.float32)
+    shift_ref[...] = shift
+
+
 def message_kernel(
     place_ref,
     rows_ref,
     feat_ref,
     w1_hbm,
     b1_ref,
-    w2_hbm,
-    b2_ref,
     out_ref,
     w1_ref,
-    w2_ref,
     tiles_ref,
     inputs_ref,
-    hidden_ref,
+    partial_ref,
     sent_ref,
     sem,
     sems,
 ):
     events = feat_ref.shape[0]
-    hid, width = w2_ref.shape
+    depth, hid = w1_ref.shape
+    width = (depth - feat_ref.shape[1]) // 2
     group = 16
     loads = []
-    for source, target in ((w1_hbm, w1_ref), (w2_hbm, w2_ref)):
-        load = pltpu.make_async_copy(source, target, sems.at[len(loads)])
+    for i, rows in enumerate((pl.ds(0, width), pl.ds(width, depth - width))):
+        load = pltpu.make_async_copy(w1_hbm.at[rows], w1_ref.at[rows], sems.at[i])
         load.start()
         loads.append(load)
     for half in range(2):
@@ -245,14 +254,18 @@
     loads[0].wait()
     for j in range(hid // COLS):
         cols = slice(j * COLS, (j + 1) * COLS)
-        h = jnp.dot(inputs_ref[...], w1_ref[:, cols], preferred_element_type=jnp.float32) + b1_ref[:, cols]
-        hidden_ref[:, cols] = jnp.maximum(h, 0.0).astype(jnp.bfloat16)
+        partial_ref[:, cols] = (
+            jnp.dot(inputs_ref[:, :width], w1_ref[:width, cols], preferred_element_type=jnp.float32) + b1_ref[:, cols]
+        )
     loads[1].wait()
-    for j in range(width // COLS):
+    for j in range(hid // COLS):
         cols = slice(j * COLS, (j + 1) * COLS)
-        m = jnp.dot(hidden_ref[...], w2_ref[:, cols], preferred_element_type=jnp.float32) + b2_ref[:, cols]
+        h = partial_ref[:, cols] + jnp.dot(
+            inputs_ref[:, width:], w1_ref[width:, cols], preferred_element_type=jnp.float32
+        )
+        h = jnp.maximum(h, 0.0)
         for c in range(COLS // LANES):
-            tiles_ref[pl.ds(j * (COLS // LANES) + c, events, stride=SUB), :] = m[:, c * LANES : (c + 1) * LANES]
+            tiles_ref[pl.ds(j * (COLS // LANES) + c, events, stride=SUB), :] = h[:, c * LANES : (c + 1) * LANES]
 
     def send(i, c):
         for a in range(group):
@@ -276,8 +289,10 @@
     kept_hbm,
     previous_hbm,
     gates_hbm,
-    gru_hbm,
-    bias_ref,
+    gates_in_hbm,
+    candidate_in_hbm,
+    gates_bias_ref,
+    candidate_bias_ref,
     out_ref,
     final_ref,
     previous_ref,
@@ -301,7 +316,8 @@
         loads = [(gates_hbm.at[first_tile, pl.ds(h * 3 * half, 3 * half)], gates_ref.at[:, pl.ds(h * 3 * half, 3 * half)])]
         for g in range(3):
             cols = pl.ds(g * width + h * half, half)
-            loads.append((gru_hbm.at[:, cols], gru_ref.at[:, cols]))
+            source = gates_in_hbm.at[:, cols] if g < 2 else candidate_in_hbm.at[:, pl.ds(h * half, half)]
+            loads.append((source, gru_ref.at[:, cols]))
         if h == 0:
             loads.append((previous_hbm.at[first_tile], previous_ref))
         else:
@@ -345,7 +361,8 @@
         for g in range(3):
             cols = slice(g * width + j * COLS, g * width + (j + 1) * COLS)
             hid = gates_ref[:, (j * 3 + g) * COLS : (j * 3 + g + 1) * COLS].astype(jnp.float32)
-            into = jnp.dot(aggregate_ref[...], gru_ref[:, cols], preferred_element_type=jnp.float32) + bias_ref[:, cols]
+            bias = gates_bias_ref[:, cols] if g < 2 else candidate_bias_ref[:, j * COLS : (j + 1) * COLS]
+            into = jnp.dot(aggregate_ref[...], gru_ref[:, cols], preferred_element_type=jnp.float32) + bias
             pre.append((into, hid))
         reset = jax.nn.sigmoid(pre[0][0] + pre[0][1])
         update = jax.nn.sigmoid(pre[1][0] + pre[1][1])
@@ -508,25 +525,47 @@
         name="hidden_gates",
     )(node, size, tiles, gru_hid, memory, of)
 
-    returned, size = lax.optimization_barrier((returned, size))
+    def fold(first, last):
+        step = 512
+        offset = first // step
+        return pl.pallas_call(
+            fold_kernel,
+            out_shape=(shape((hid, last - first), bf16), shape((1, last - first), f32)),
+            grid=((last - first) // step,),
+            in_specs=[
+                pl.BlockSpec((hid, width), lambda i: (0, 0)),
+                pl.BlockSpec((1, width), lambda i: (0, 0)),
+                pl.BlockSpec((width, step), lambda i: (0, i + offset)),
+                pl.BlockSpec((1, step), lambda i: (0, i + offset)),
+            ],
+            out_specs=(pl.BlockSpec((hid, step), lambda i: (0, i)), pl.BlockSpec((1, step), lambda i: (0, i))),
+            compiler_params=pltpu.CompilerParams(vmem_limit_bytes=WHOLE),
+            cost_estimate=pl.CostEstimate(
+                flops=2 * hid * width * (last - first), bytes_accessed=4 * width * (last - first), transcendentals=0
+            ),
+            name="fold",
+        )(msg_w2, msg_b2.reshape(1, width), gru_in, gru_bias.reshape(1, 3 * width))
+
+    gates_in, gates_bias = fold(0, 2 * width)
+    returned, size, gates_in = lax.optimization_barrier((returned, size, gates_in))
     outgoing = pl.pallas_call(
         message_kernel,
         out_shape=shape((slots, cells, LANES), bf16),
-        in_specs=[SM, VM, VM, HBM, VM, HBM, VM],
+        in_specs=[SM, VM, VM, HBM, VM],
         out_specs=HBM,
         scratch_shapes=[
             pltpu.VMEM(msg_w1.shape, bf16),
-            pltpu.VMEM(msg_w2.shape, bf16),
             pltpu.VMEM((events * SUB, LANES), f32),
             pltpu.VMEM((events, msg_w1.shape[0]), bf16),
-            pltpu.VMEM((events, hid), bf16),
+            pltpu.VMEM((events, hid), f32),
             pltpu.VMEM((slots, cells, LANES), bf16),
             pltpu.SemaphoreType.DMA,
             pltpu.SemaphoreType.DMA((2,)),
         ],
         compiler_params=pltpu.CompilerParams(vmem_limit_bytes=MOST),
         name="message",
-    )(place, returned, edge_feat, msg_w1, msg_b1.reshape(1, hid), msg_w2, msg_b2.reshape(1, width))
+    )(place, returned, edge_feat, msg_w1, msg_b1.reshape(1, hid))
+    candidate_in, candidate_bias = fold(2 * width, 3 * width)
     incoming = lax.all_to_all(
         outgoing.reshape(devices, capacity, cells, LANES), AXES, split_axis=0, concat_axis=0, tiled=True
     ).reshape(slots, cells, LANES)
@@ -534,7 +573,7 @@
     return pl.pallas_call(
         update_kernel,
         out_shape=shape((node_rows, width), bf16),
-        in_specs=[SM, SM, SM, SM, VM, VM, HBM, HBM, HBM, HBM, VM],
+        in_specs=[SM, SM, SM, SM, VM, VM, HBM, HBM, HBM, HBM, HBM, VM, VM],
         out_specs=HBM,
         scratch_shapes=[
             pltpu.VMEM((node_rows, width), bf16),
@@ -560,8 +599,10 @@
         kept,
         previous,
         gates,
-        gru_in,
-        gru_bias.reshape(1, 3 * width),
+        gates_in,
+        candidate_in,
+        gates_bias,
+        candidate_bias,
     )
 
 

time: 94.5 us -> 95.7 us (1.013)
  waiting for transfers between devices: 30.1 us -> 15 us
  Pallas kernels: 37.5 us -> 51.1 us
  starting transfers between devices: 20.4 us -> 23.2 us
    pallas_call x0 -> x2, Pallas kernels: none -> 15.1 us  [fold(): pl.pallas_call(fold_kernel, out_shape=(shape((hid, last - first), bf16),...]
    all_to_all x1, waiting for transfers between devices: 11.6 us -> 2.39 us  [on_device(): lax.all_to_all(answers.reshape(devices, capacity, cells, LANES), AXES, sp...]
    all_to_all x1, waiting for transfers between devices: 12.6 us -> 6.71 us  [on_device(): lax.all_to_all(outgoing.reshape(devices, capacity, cells, LANES), AXES, s...]
    all_to_all x1, starting transfers between devices: 4.65 us -> 7.39 us  [on_device(): lax.all_to_all(outgoing.reshape(devices, capacity, cells, LANES), AXES, s...]
    pallas_call x1, Pallas kernels: 6.84 us -> 5.57 us  [on_device(): pl.pallas_call(message_kernel, out_shape=shape((slots, cells, LANES), bf1...]
  transfers between devices with their start and end apart: 3 -> 3, of which waited for: 3 -> 3; matrix products, arithmetic and copies ran while one was open for 5% -> 5% of each run, Pallas kernels for 18% -> 34%
where the time goes in v5:
time: 95.7 us; the launch traced here: 95.3 us
  Pallas kernels  51.1 us (53%)
  starting transfers between devices  23.2 us (24%)
  waiting for transfers between devices  15 us (16%)
  local copies, waits for them, and re-layouts  5.78 us (6%)
    pallas_call x2, Pallas kernels, fold(): pl.pallas_call(fold_kernel, out_shape=(shape((hid, last - first), bf16),...  15.1 us
    all_to_all x1, starting transfers between devices, on_device(): lax.all_to_all(ids.reshape(devices, 1, LANES), AXES, split_axis=0, concat...  11.1 us
    pallas_call x1, Pallas kernels, on_device(): pl.pallas_call(lambda *refs: compact_kernel(capacity, padded, *refs), out...  8.99 us
    pallas_call x1, Pallas kernels, on_device(): pl.pallas_call(hidden_gates_kernel, out_shape=(shape((padded, width), bf1...  8.12 us
    pallas_call x1, Pallas kernels, on_device(): pl.pallas_call(update_kernel, out_shape=shape((node_rows, width), bf16),...  8.03 us
    all_to_all x1, starting transfers between devices, on_device(): lax.all_to_all(outgoing.reshape(devices, capacity, cells, LANES), AXES, s...  7.39 us
    all_to_all x1, waiting for transfers between devices, on_device(): lax.all_to_all(outgoing.reshape(devices, capacity, cells, LANES), AXES, s...  6.71 us
    all_to_all x1, waiting for transfers between devices, on_device(): lax.all_to_all(ids.reshape(devices, 1, LANES), AXES, split_axis=0, concat...  5.94 us
  transfers between devices with their start and end apart: 3, of which 3 were waited for; matrix products, arithmetic and copies ran while one was open for 5% of the time, Pallas kernels for 34%

profile of v5, /device:TPU:0, one launch (start us, length us, event | category | flops | bytes accessed | tf_op | source)
XLA Modules:
  0.0 95.3 jit_solution(1656172660345942217)
XLA Ops:
  0.0 1.8 %plan.1 = (s32[128,128]{1,0:T(8,128)}, s32[2,256]{1,0:T(2,128)}) custom-call(s32[2,256]{1,0:T(2,128)} %bitcast.30, s32[2,256]{1,0:T(2,128)} %bitcast.31, s32[1,256]{1,0:T(1,128)} %bitcast.32), custom_call_target="tpu_custom_call" | custom-call | tf_op jit(solution)/shard_map/plan/pallas_call | solution.py:453
  1.8 11.1 %all-to-all-start = ((s32[128,1,128]{2,1,0:T(1,128)}), s32[128,1,128]{2,1,0:T(1,128)S(1)}, u32[]{:S(2)}, u32[]{:S(2)}) async-start(s32[128,1,128]{2,1,0:T(1,128)} %bitcast.25), calls=%async_computation | async-start | bytes 131072 | tf_op jit(solution)/shard_map/all_to_all | solution.py:462
  12.9 3.5 %copy.18 = bf16[128,8,8,128]{3,2,1,0:T(8,128)(2,1)} copy(bf16[128,8,8,128]{3,1,2,0:T(8,128)(2,1)} %bitcast.24) | data formatting | bytes 4194304
  16.4 5.9 %all-to-all-done = s32[128,1,128]{2,1,0:T(1,128)S(1)} async-done(((s32[128,1,128]{2,1,0:T(1,128)}), s32[128,1,128]{2,1,0:T(1,128)S(1)}, u32[]{:S(2)}, u32[]{:S(2)}) %all-to-all-start) | async-done | bytes 65568 | tf_op jit(solution)/shard_map/all_to_all | solution.py:462
  22.4 3.5 %answer.1 = (bf16[640,8,128]{2,1,0:T(8,128)(2,1)}, s32[8,128]{1,0:T(8,128)S(1)}) custom-call(s32[128,128]{1,0:T(8,128)S(1)} %bitcast.19, bf16[1024,8,128]{2,1,0:T(8,128)(2,1)} %bitcast.22), custom_call_target="tpu_custom_call" | custom-call | tf_op jit(solution)/shard_map/answer/pallas_call | solution.py:467
  25.9 4.7 %all-to-all-start.1 = ((bf16[128,5,8,128]{3,2,1,0:T(8,128)(2,1)}), bf16[128,5,8,128]{3,2,1,0:T(8,128)(2,1)S(1)}, u32[]{:S(2)}, u32[]{:S(2)}) async-start(bf16[128,5,8,128]{3,2,1,0:T(8,128)(2,1)} %bitcast.6), calls=%async_computation.1 | async-start | bytes 2621440 | tf_op jit(solution)/shard_map/all_to_all | solution.py:484
  30.6 9.2 %fold.2 = (bf16[1024,2048]{1,0:T(8,128)(2,1)}, f32[1,2048]{1,0:T(1,128)}) custom-call(bf16[1024,1024]{1,0:T(8,128)(2,1)} %w2_ref.3, f32[1,1024]{1,0:T(1,128)} %bitcast.28, bf16[1024,3072]{1,0:T(8,128)(2,1)} %gru_ref.5, f32[1,3072]{1,0:T(1,128)} %bitcast.26), custom_call_target="tpu_custom_call" | custom-call | flops 4294967296 | bytes 8388608 | tf_op jit(solution)/shard_map/fold/pallas_call | solution.py:531
  39.8 0.0 copy-start.1
  39.8 0.0 copy-start.3
  39.8 0.0 copy-start.5
  39.8 9.0 %compact.1 = (s32[1024]{0:T(1024)S(1)}, s32[1024]{0:T(1024)S(1)}, s32[1024]{0:T(1024)S(1)}, s32[1024]{0:T(1024)S(1)}, s32[1024]{0:T(1024)S(1)}, /*index=5*/s32[8]{0:T(128)S(1)}) custom-call(s32[8,128]{1,0:T(8,128)S(1)} %get-tuple-element.26.refs_0_), custom_call_target="tpu_custom_call" | custom-call | flops 4000000000 | bytes 20000000 | tf_op jit(solution)/shard_map/compact/pallas_call | solution.py:488
  48.8 0.0 copy-start.6
  48.8 0.6 copy-done.6
  49.4 0.0 copy-start.8
  49.4 0.6 copy-done.8
  50.0 2.4 %all-to-all-done.1 = bf16[128,5,8,128]{3,2,1,0:T(8,128)(2,1)S(1)} async-done(((bf16[128,5,8,128]{3,2,1,0:T(8,128)(2,1)}), bf16[128,5,8,128]{3,2,1,0:T(8,128)(2,1)S(1)}, u32[]{:S(2)}, u32[]{:S(2)}) %all-to-all-start.1) | async-done | bytes 1310752 | tf_op jit(solution)/shard_map/all_to_all | solution.py:484
  52.4 0.0 copy-done.1
  52.4 0.0 copy-done.3
  52.4 0.0 copy-done.5
  52.4 5.6 %message.1 = bf16[640,8,128]{2,1,0:T(8,128)(2,1)} custom-call(s32[2,256]{1,0:T(2,128)S(1)} %copy-done.5, bf16[640,8,128]{2,1,0:T(8,128)(2,1)S(1)} %bitcast.18, bf16[256,128]{1,0:T(8,128)(2,1)S(1)} %copy-done.1, bf16[2176,1024]{1,0:T(8,128)(2,1)} %w1_hbm.1, f32[1,1024]{1,0:T(1,128)S(1)} %bitcast.20), custom_call_target="tpu_custom_call" | custom-call | tf_op jit(solution)/shard_map/message/pallas_call | solution.py:551
  57.9 7.4 %all-to-all-start.2 = ((bf16[128,5,8,128]{3,2,1,0:T(8,128)(2,1)}), bf16[128,5,8,128]{3,2,1,0:T(8,128)(2,1)S(1)}, u32[]{:S(2)}, u32[]{:S(2)}) async-start(bf16[128,5,8,128]{3,2,1,0:T(8,128)(2,1)} %bitcast.11), calls=%async_computation.2 | async-start | bytes 2621440 | tf_op jit(solution)/shard_map/all_to_all | solution.py:569
  65.3 5.9 %fold.3 = (bf16[1024,1024]{1,0:T(8,128)(2,1)}, f32[1,1024]{1,0:T(1,128)}) custom-call(bf16[1024,1024]{1,0:T(8,128)(2,1)} %w2_ref.3, f32[1,1024]{1,0:T(1,128)} %bitcast.29, bf16[1024,3072]{1,0:T(8,128)(2,1)} %gru_ref.5, f32[1,3072]{1,0:T(1,128)} %bitcast.27), custom_call_target="tpu_custom_call" | custom-call | flops 2147483648 | bytes 4194304 | tf_op jit(solution)/shard_map/fold/pallas_call | solution.py:531
  71.2 1.0 %copy.17.of_ref = s32[1024,1]{1,0:T(8,128)} copy(s32[1024,1]{0,1:T(1,128)S(1)} %bitcast.21) | data formatting | bytes 8192 | tf_op jit(solution)/shard_map/reshape | solution.py:506
  72.3 0.0 copy-start
  72.3 0.0 copy-start.2
  72.3 0.0 copy-start.4
  72.3 0.0 copy-start.7
  72.3 8.1 %hidden_gates.1 = (bf16[768,1024]{1,0:T(8,128)(2,1)}, bf16[768,3072]{1,0:T(8,128)(2,1)}, bf16[1024,1024]{1,0:T(8,128)(2,1)}) custom-call(s32[1024]{0:T(1024)} %copy-done.8, s32[8]{0:T(128)} %copy-done.6, bf16[1024,8,128]{2,1,0:T(8,128)(2,1)} %bitcast.23, bf16[1024,3072]{1,0:T(8,128)(2,1)} %gru_ref.4, bf16[1024,1024]{1,0:T(8,128)(2,1)} %plain_ref.1, ...), custom_call_target="tpu_custom_call" | custom-call | flops 4000000000 | bytes 20000000 | tf_op jit(solution)/shard_map/hidden_gates/pallas_call | solution.py:507
  80.4 6.7 %all-to-all-done.2 = bf16[128,5,8,128]{3,2,1,0:T(8,128)(2,1)S(1)} async-done(((bf16[128,5,8,128]{3,2,1,0:T(8,128)(2,1)}), bf16[128,5,8,128]{3,2,1,0:T(8,128)(2,1)S(1)}, u32[]{:S(2)}, u32[]{:S(2)}) %all-to-all-start.2) | async-done | bytes 1310752 | tf_op jit(solution)/shard_map/all_to_all | solution.py:569
  87.1 0.0 copy-done
  87.1 0.0 copy-done.2
  87.1 0.0 copy-done.4
  87.1 0.0 copy-done.7
  87.1 8.0 %update.1 = bf16[1024,1024]{1,0:T(8,128)(2,1)} custom-call(s32[1024]{0:T(1024)S(1)} %get-tuple-element.27.slot_ref, s32[1024]{0:T(1024)S(1)} %get-tuple-element.28.index_ref, s32[1024]{0:T(1024)S(1)} %get-tuple-element.29.count_ref, s32[8]{0:T(128)S(1)} %copy-done.7, bf16[640,8,128]{2,1,0:T(8,128)(2,1)S(1)} %bitcast.17, s32[1024,1]{1,0:T(8,128)S(1)} %copy-done, ...), custom_call_target="tpu_custom_call" | custom-call | tf_op jit(solution)/shard_map/update/pallas_call | solution.py:573
Async XLA Ops:
  1.8 20.6 %all-to-all-start = ((s32[128,1,128]{2,1,0:T(1,128)}), s32[128,1,128]{2,1,0:T(1,128)S(1)}, u32[]{:S(2)}, u32[]{:S(2)}) async-start(s32[128,1,128]{2,1,0:T(1,128)} %bitcast.25), calls=%async_computation | async-start | bytes 131072 | tf_op jit(solution)/shard_map/all_to_all | solution.py:462
  25.9 26.4 %all-to-all-start.1 = ((bf16[128,5,8,128]{3,2,1,0:T(8,128)(2,1)}), bf16[128,5,8,128]{3,2,1,0:T(8,128)(2,1)S(1)}, u32[]{:S(2)}, u32[]{:S(2)}) async-start(bf16[128,5,8,128]{3,2,1,0:T(8,128)(2,1)} %bitcast.6), calls=%async_computation.1 | async-start | bytes 2621440 | tf_op jit(solution)/shard_map/all_to_all | solution.py:484
  39.8 12.6 %copy-start.1 = (bf16[256,128]{1,0:T(8,128)(2,1)S(1)}, bf16[256,128]{1,0:T(8,128)(2,1)}, u32[]{:S(2)}) copy-start(bf16[256,128]{1,0:T(8,128)(2,1)} %feat_ref.1) | copy-start | bytes 196612
  39.8 12.6 %copy-start.3 = (f32[1024]{0:T(1024)S(1)}, f32[1024]{0:T(1024)}, u32[]{:S(2)}) copy-start(f32[1024]{0:T(1024)} %param.18) | copy-start | bytes 12292
  39.8 12.6 %copy-start.5 = (s32[2,256]{1,0:T(2,128)S(1)}, s32[2,256]{1,0:T(2,128)}, u32[]{:S(2)}) copy-start(s32[2,256]{1,0:T(2,128)} %get-tuple-element.34.place_ref) | copy-start | bytes 6148
  48.8 0.6 copy-start.6
  49.4 0.6 copy-start.8
  57.9 29.2 %all-to-all-start.2 = ((bf16[128,5,8,128]{3,2,1,0:T(8,128)(2,1)}), bf16[128,5,8,128]{3,2,1,0:T(8,128)(2,1)S(1)}, u32[]{:S(2)}, u32[]{:S(2)}) async-start(bf16[128,5,8,128]{3,2,1,0:T(8,128)(2,1)} %bitcast.11), calls=%async_computation.2 | async-start | bytes 2621440 | tf_op jit(solution)/shard_map/all_to_all | solution.py:569
  72.3 14.9 %copy-start = (s32[1024,1]{1,0:T(8,128)S(1)}, s32[1024,1]{1,0:T(8,128)}, u32[]{:S(2)}) copy-start(s32[1024,1]{1,0:T(8,128)} %copy.17.of_ref) | copy-start | bytes 12292
  72.3 14.9 %copy-start.2 = (f32[1,2048]{1,0:T(1,128)S(1)}, f32[1,2048]{1,0:T(1,128)}, u32[]{:S(2)}) copy-start(f32[1,2048]{1,0:T(1,128)} %get-tuple-element.43.gates_bias_ref) | copy-start | bytes 24580
  72.3 14.9 %copy-start.4 = (f32[1,1024]{1,0:T(1,128)S(1)}, f32[1,1024]{1,0:T(1,128)}, u32[]{:S(2)}) copy-start(f32[1,1024]{1,0:T(1,128)} %get-tuple-element.44.candidate_bias_ref) | copy-start | bytes 12292
  72.3 14.9 %copy-start.7 = (s32[8]{0:T(128)S(1)}, s32[8]{0:T(128)}, u32[]{:S(2)}) copy-start(s32[8]{0:T(128)} %copy-done.6) | copy-start | bytes 100

commit v6 on v5

--- a/solution.py
+++ b/solution.py
@@ -73,11 +73,12 @@
     memory_load = pltpu.make_async_copy(memory_hbm, memory_ref, memory_sem)
     memory_load.start()
     turned = jnp.transpose(ids_ref[...])[:SUB, :]
-    codes_ref[...] = turned
     turned_ref[...] = turned
     load = pltpu.make_async_copy(turned_ref, wanted_ref, load_sem)
     load.start()
     load.wait()
+    keep = pltpu.make_async_copy(turned_ref, codes_ref, load_sem)
+    keep.start()
     memory_load.wait()
     group = 8
     chunks = sems.shape[0]
@@ -97,6 +98,7 @@
         send = pltpu.make_async_copy(rows_ref.at[here], out_ref.at[here], sems.at[q])
         send.start()
         sends.append(send)
+    keep.wait()
     for send in sends:
         send.wait()
 
@@ -117,27 +119,28 @@
 
     lax.fori_loop(0, rows // 16, clear, 0)
 
-    def step(p, carry):
-        taken, nodes = carry
+    def choose(p, taken):
         for k in range(capacity):
             code = ids_ref[k, p]
-            active = code >= ACTIVE
-            node = code & (ACTIVE - 1)
-            known = of_ref[node]
-            fresh = active & (known < 0)
-            index = jnp.where(known < 0, nodes, known)
-            of_ref[node] = jnp.where(active, index, known)
             slot_ref[taken] = p * capacity + k
-            index_ref[taken] = index
-            old = count_ref[index]
-            was = jnp.where(known < 0, 0, old)
-            count_ref[index] = jnp.where(active, was + 1, was)
-            node_ref[index] = jnp.where(fresh, node, jnp.where(known < 0, 0, node_ref[index]))
-            taken = taken + active.astype(jnp.int32)
-            nodes = nodes + fresh.astype(jnp.int32)
-        return taken, nodes
-
-    taken, nodes = lax.fori_loop(0, devices, step, (jnp.int32(0), jnp.int32(0)))
+            index_ref[taken] = code & (ACTIVE - 1)
+            taken = taken + (code >= ACTIVE).astype(jnp.int32)
+        return taken
+
+    taken = lax.fori_loop(0, devices, choose, jnp.int32(0), unroll=2)
+
+    def number(i, nodes):
+        node = index_ref[i]
+        known = of_ref[node]
+        fresh = known < 0
+        index = jnp.where(fresh, nodes, known)
+        of_ref[node] = index
+        index_ref[i] = index
+        node_ref[index] = node
+        count_ref[index] = jnp.where(fresh, 0, count_ref[index]) + 1
+        return nodes + fresh.astype(jnp.int32)
+
+    nodes = lax.fori_loop(0, taken, number, jnp.int32(0))
     size_ref[0] = taken
     size_ref[1] = nodes
     for a in range(UNROLL):
@@ -154,22 +157,33 @@
 def hidden_gates_kernel(
     node_ref,
     size_ref,
-    memory_ref,
-    gru_ref,
-    plain_ref,
+    memory_hbm,
+    gru_hbm,
+    plain_hbm,
     of_ref,
     previous_ref,
     gates_ref,
     kept_ref,
+    memory_ref,
+    gru_ref,
+    plain_ref,
     tiles_ref,
     rows_ref,
     made_ref,
     left_ref,
     sems,
 ):
+    loads = []
+    for source, target in ((memory_hbm, memory_ref), (plain_hbm, plain_ref), (gru_hbm, gru_ref)):
+        load = pltpu.make_async_copy(source, target, sems.at[3 + len(loads)])
+        load.start()
+        loads.append(load)
+    loads[0].wait()
+    loads[1].wait()
     left_ref[...] = jnp.where(of_ref[...] < 0, plain_ref[...].astype(jnp.float32), 0.0).astype(jnp.bfloat16)
     third = pltpu.make_async_copy(left_ref, kept_ref, sems.at[2])
     third.start()
+    loads[2].wait()
     steps = jnp.maximum(pl.cdiv(size_ref[1], TILE), 1)
     width = rows_ref.shape[1]
 
@@ -203,15 +217,22 @@
     third.wait()
 
 
-def fold_kernel(w2_ref, b2_ref, gru_ref, bias_ref, folded_ref, shift_ref):
-    folded_ref[...] = jnp.dot(w2_ref[...], gru_ref[...], preferred_element_type=jnp.float32).astype(jnp.bfloat16)
-    rest = jnp.broadcast_to(b2_ref[...], (SUB, b2_ref.shape[1]))
-    shift = bias_ref[...]
-    for i in range(3):
-        term = rest.astype(jnp.bfloat16)
-        shift = shift + jnp.dot(term, gru_ref[...], preferred_element_type=jnp.float32)[0:1, :]
-        rest = rest - term.astype(jnp.float32)
-    shift_ref[...] = shift
+def fold_kernel(w2_ref, b2_ref, gru_ref, bias_ref, folded_ref, shift_ref, left_ref):
+    hid = w2_ref.shape[0]
+
+    @pl.when(pl.program_id(0) == 0)
+    def _():
+        left_ref[:hid, :] = w2_ref[...]
+        first = b2_ref[...].astype(jnp.bfloat16).astype(jnp.float32)
+        rest = b2_ref[...] - first
+        second = rest.astype(jnp.bfloat16).astype(jnp.float32)
+        rows = lax.broadcasted_iota(jnp.int32, (2 * SUB, b2_ref.shape[1]), 0)
+        terms = jnp.where(rows == 0, first, jnp.where(rows == 1, second, jnp.where(rows == 2, rest - second, 0.0)))
+        left_ref[hid:, :] = terms.astype(jnp.bfloat16)
+
+    both = jnp.dot(left_ref[...], gru_ref[...], preferred_element_type=jnp.float32)
+    folded_ref[...] = both[:hid, :].astype(jnp.bfloat16)
+    shift_ref[...] = bias_ref[...] + jnp.sum(both[hid:, :], axis=0, keepdims=True)
 
 
 def message_kernel(
@@ -289,10 +310,10 @@
     kept_hbm,
     previous_hbm,
     gates_hbm,
-    gates_in_hbm,
-    candidate_in_hbm,
-    gates_bias_ref,
-    candidate_bias_ref,
+    left_in_hbm,
+    right_in_hbm,
+    left_bias_ref,
+    right_bias_ref,
     out_ref,
     final_ref,
     previous_ref,
@@ -310,14 +331,15 @@
     nodes = size_ref[1]
     steps = jnp.maximum(pl.cdiv(nodes, TILE), 1)
     half = width // 2
+    split = left_in_hbm.shape[1]
     first_tile = pl.ds(0, TILE)
     halves = []
     for h in range(2):
         loads = [(gates_hbm.at[first_tile, pl.ds(h * 3 * half, 3 * half)], gates_ref.at[:, pl.ds(h * 3 * half, 3 * half)])]
         for g in range(3):
-            cols = pl.ds(g * width + h * half, half)
-            source = gates_in_hbm.at[:, cols] if g < 2 else candidate_in_hbm.at[:, pl.ds(h * half, half)]
-            loads.append((source, gru_ref.at[:, cols]))
+            first = g * width + h * half
+            part = (left_in_hbm, right_in_hbm)[first // split]
+            loads.append((part.at[:, pl.ds(first % split, half)], gru_ref.at[:, pl.ds(first, half)]))
         if h == 0:
             loads.append((previous_hbm.at[first_tile], previous_ref))
         else:
@@ -361,7 +383,8 @@
         for g in range(3):
             cols = slice(g * width + j * COLS, g * width + (j + 1) * COLS)
             hid = gates_ref[:, (j * 3 + g) * COLS : (j * 3 + g + 1) * COLS].astype(jnp.float32)
-            bias = gates_bias_ref[:, cols] if g < 2 else candidate_bias_ref[:, j * COLS : (j + 1) * COLS]
+            first = g * width + j * COLS
+            bias = (left_bias_ref, right_bias_ref)[first // split][:, first % split : first % split + COLS]
             into = jnp.dot(aggregate_ref[...], gru_ref[:, cols], preferred_element_type=jnp.float32) + bias
             pre.append((into, hid))
         reset = jax.nn.sigmoid(pre[0][0] + pre[0][1])
@@ -468,7 +491,7 @@
         lambda *refs: answer_kernel(capacity, *refs),
         out_shape=(shape((slots, cells, LANES), bf16), shape((SUB, devices), i32)),
         in_specs=[VM, HBM],
-        out_specs=(HBM, VM),
+        out_specs=(HBM, HBM),
         scratch_shapes=[
             pltpu.VMEM((node_rows, cells, LANES), bf16),
             pltpu.VMEM((SUB, devices), i32),
@@ -511,14 +534,17 @@
             shape((padded, 3 * width), GATES),
             shape((node_rows, width), bf16),
         ),
-        in_specs=[SM, SM, VM, VM, VM, VM],
+        in_specs=[SM, SM, HBM, HBM, HBM, VM],
         out_specs=(HBM, HBM, HBM),
         scratch_shapes=[
+            pltpu.VMEM((node_rows, cells, LANES), bf16),
+            pltpu.VMEM((width, 3 * width), bf16),
+            pltpu.VMEM((node_rows, width), bf16),
             pltpu.VMEM((TILE * SUB, LANES), f32),
             pltpu.VMEM((TILE, width), bf16),
             pltpu.VMEM((TILE, 3 * width), GATES),
             pltpu.VMEM((node_rows, width), bf16),
-            pltpu.SemaphoreType.DMA((3,)),
+            pltpu.SemaphoreType.DMA((6,)),
         ],
         compiler_params=pltpu.CompilerParams(vmem_limit_bytes=WHOLE),
         cost_estimate=pl.CostEstimate(flops=4_000_000_000, bytes_accessed=20_000_000, transcendentals=0),
@@ -539,6 +565,7 @@
                 pl.BlockSpec((1, step), lambda i: (0, i + offset)),
             ],
             out_specs=(pl.BlockSpec((hid, step), lambda i: (0, i)), pl.BlockSpec((1, step), lambda i: (0, i))),
+            scratch_shapes=[pltpu.VMEM((hid + 2 * SUB, width), bf16)],
             compiler_params=pltpu.CompilerParams(vmem_limit_bytes=WHOLE),
             cost_estimate=pl.CostEstimate(
                 flops=2 * hid * width * (last - first), bytes_accessed=4 * width * (last - first), transcendentals=0
@@ -546,8 +573,9 @@
             name="fold",
         )(msg_w2, msg_b2.reshape(1, width), gru_in, gru_bias.reshape(1, 3 * width))
 
-    gates_in, gates_bias = fold(0, 2 * width)
-    returned, size, gates_in = lax.optimization_barrier((returned, size, gates_in))
+    split = 3 * width // 2
+    left_in, left_bias = fold(0, split)
+    returned, size, left_in = lax.optimization_barrier((returned, size, left_in))
     outgoing = pl.pallas_call(
         message_kernel,
         out_shape=shape((slots, cells, LANES), bf16),
@@ -565,7 +593,7 @@
         compiler_params=pltpu.CompilerParams(vmem_limit_bytes=MOST),
         name="message",
     )(place, returned, edge_feat, msg_w1, msg_b1.reshape(1, hid))
-    candidate_in, candidate_bias = fold(2 * width, 3 * width)
+    right_in, right_bias = fold(split, 3 * width)
     incoming = lax.all_to_all(
         outgoing.reshape(devices, capacity, cells, LANES), AXES, split_axis=0, concat_axis=0, tiled=True
     ).reshape(slots, cells, LANES)
@@ -599,10 +627,10 @@
         kept,
         previous,
         gates,
-        gates_in,
-        candidate_in,
-        gates_bias,
-        candidate_bias,
+        left_in,
+        right_in,
+        left_bias,
+        right_bias,
     )
 
 

time: 95.7 us -> 93.2 us (0.974)
  starting transfers between devices: 23.2 us -> 20.6 us
    all_to_all x1, waiting for transfers between devices: 2.39 us -> 6.14 us  [on_device(): lax.all_to_all(answers.reshape(devices, capacity, cells, LANES), AXES, sp...]
    all_to_all x1, waiting for transfers between devices: 6.71 us -> 3.87 us  [on_device(): lax.all_to_all(outgoing.reshape(devices, capacity, cells, LANES), AXES, s...]
    all_to_all x1, starting transfers between devices: 7.39 us -> 4.77 us  [on_device(): lax.all_to_all(outgoing.reshape(devices, capacity, cells, LANES), AXES, s...]
    pallas_call x1, Pallas kernels: 8.99 us -> 7.11 us  [on_device(): pl.pallas_call(lambda *refs: compact_kernel(capacity, padded, *refs), out...]
    pallas_call x1, Pallas kernels: 8.12 us -> 9.5 us  [on_device(): pl.pallas_call(hidden_gates_kernel, out_shape=(shape((padded, width), bf1...]
where the time goes in v6:
time: 93.2 us; the launch traced here: 92.7 us
  Pallas kernels  50.2 us (54%)
  starting transfers between devices  20.6 us (22%)
  waiting for transfers between devices  15.9 us (17%)
  local copies, waits for them, and re-layouts  5.78 us (6%)
    pallas_call x2, Pallas kernels, fold(): pl.pallas_call(fold_kernel, out_shape=(shape((hid, last - first), bf16),...  14.7 us
    all_to_all x1, starting transfers between devices, on_device(): lax.all_to_all(ids.reshape(devices, 1, LANES), AXES, split_axis=0, concat...  11.1 us
    pallas_call x1, Pallas kernels, on_device(): pl.pallas_call(hidden_gates_kernel, out_shape=(shape((padded, width), bf1...  9.5 us
    pallas_call x1, Pallas kernels, on_device(): pl.pallas_call(update_kernel, out_shape=shape((node_rows, width), bf16),...  8.04 us
    pallas_call x1, Pallas kernels, on_device(): pl.pallas_call(lambda *refs: compact_kernel(capacity, padded, *refs), out...  7.11 us
    all_to_all x1, waiting for transfers between devices, on_device(): lax.all_to_all(answers.reshape(devices, capacity, cells, LANES), AXES, sp...  6.14 us
    all_to_all x1, waiting for transfers between devices, on_device(): lax.all_to_all(ids.reshape(devices, 1, LANES), AXES, split_axis=0, concat...  5.94 us
    pallas_call x1, Pallas kernels, on_device(): pl.pallas_call(message_kernel, out_shape=shape((slots, cells, LANES), bf1...  5.57 us
  transfers between devices with their start and end apart: 3, of which 3 were waited for; matrix products, arithmetic and copies ran while one was open for 5% of the time, Pallas kernels for 34%

profile of v6, /device:TPU:0, one launch (start us, length us, event | category | flops | bytes accessed | tf_op | source)
XLA Modules:
  0.0 92.7 jit_solution(8278949812613018792)
XLA Ops:
  0.0 1.8 %plan.1 = (s32[128,128]{1,0:T(8,128)}, s32[2,256]{1,0:T(2,128)}) custom-call(s32[2,256]{1,0:T(2,128)} %bitcast.26, s32[2,256]{1,0:T(2,128)} %bitcast.27, s32[1,256]{1,0:T(1,128)} %bitcast.28), custom_call_target="tpu_custom_call" | custom-call | tf_op jit(solution)/shard_map/plan/pallas_call | solution.py:476
  1.8 11.1 %all-to-all-start = ((s32[128,1,128]{2,1,0:T(1,128)}), s32[128,1,128]{2,1,0:T(1,128)S(1)}, u32[]{:S(2)}, u32[]{:S(2)}) async-start(s32[128,1,128]{2,1,0:T(1,128)} %bitcast.25), calls=%async_computation | async-start | bytes 131072 | tf_op jit(solution)/shard_map/all_to_all | solution.py:485
  12.9 3.5 %copy.18 = bf16[128,8,8,128]{3,2,1,0:T(8,128)(2,1)} copy(bf16[128,8,8,128]{3,1,2,0:T(8,128)(2,1)} %bitcast.24) | data formatting | bytes 4194304
  16.4 5.9 %all-to-all-done = s32[128,1,128]{2,1,0:T(1,128)S(1)} async-done(((s32[128,1,128]{2,1,0:T(1,128)}), s32[128,1,128]{2,1,0:T(1,128)S(1)}, u32[]{:S(2)}, u32[]{:S(2)}) %all-to-all-start) | async-done | bytes 65568 | tf_op jit(solution)/shard_map/all_to_all | solution.py:485
  22.4 3.5 %answer.1 = (bf16[640,8,128]{2,1,0:T(8,128)(2,1)}, s32[8,128]{1,0:T(8,128)S(1)}) custom-call(s32[128,128]{1,0:T(8,128)S(1)} %bitcast.19, bf16[1024,8,128]{2,1,0:T(8,128)(2,1)} %bitcast.22), custom_call_target="tpu_custom_call" | custom-call | tf_op jit(solution)/shard_map/answer/pallas_call | solution.py:490
  25.9 4.7 %all-to-all-start.1 = ((bf16[128,5,8,128]{3,2,1,0:T(8,128)(2,1)}), bf16[128,5,8,128]{3,2,1,0:T(8,128)(2,1)S(1)}, u32[]{:S(2)}, u32[]{:S(2)}) async-start(bf16[128,5,8,128]{3,2,1,0:T(8,128)(2,1)} %bitcast.6), calls=%async_computation.1 | async-start | bytes 2621440 | tf_op jit(solution)/shard_map/all_to_all | solution.py:507
  30.6 7.3 %fold.2 = (bf16[1024,1536]{1,0:T(8,128)(2,1)}, f32[1,1536]{1,0:T(1,128)}) custom-call(bf16[1024,1024]{1,0:T(8,128)(2,1)} %w2_ref.3, f32[1,1024]{1,0:T(1,128)} %bitcast.31, bf16[1024,3072]{1,0:T(8,128)(2,1)} %gru_ref.3, f32[1,3072]{1,0:T(1,128)} %bitcast.29), custom_call_target="tpu_custom_call" | custom-call | flops 3221225472 | bytes 6291456 | tf_op jit(solution)/shard_map/fold/pallas_call | solution.py:557
  37.9 0.0 copy-start.1
  37.9 0.0 copy-start.4
  37.9 0.0 copy-start.5
  37.9 7.1 %compact.1 = (s32[1024]{0:T(1024)S(1)}, s32[1024]{0:T(1024)S(1)}, s32[1024]{0:T(1024)S(1)}, s32[1024]{0:T(1024)S(1)}, s32[1024]{0:T(1024)S(1)}, /*index=5*/s32[8]{0:T(128)S(1)}) custom-call(s32[8,128]{1,0:T(8,128)S(1)} %get-tuple-element.26.refs_0_), custom_call_target="tpu_custom_call" | custom-call | flops 4000000000 | bytes 20000000 | tf_op jit(solution)/shard_map/compact/pallas_call | solution.py:511
  45.0 0.0 copy-start.6
  45.1 0.6 copy-done.6
  45.6 0.0 copy-start.8
  45.6 0.6 copy-done.8
  46.2 6.1 %all-to-all-done.1 = bf16[128,5,8,128]{3,2,1,0:T(8,128)(2,1)S(1)} async-done(((bf16[128,5,8,128]{3,2,1,0:T(8,128)(2,1)}), bf16[128,5,8,128]{3,2,1,0:T(8,128)(2,1)S(1)}, u32[]{:S(2)}, u32[]{:S(2)}) %all-to-all-start.1) | async-done | bytes 1310752 | tf_op jit(solution)/shard_map/all_to_all | solution.py:507
  52.4 0.0 copy-done.1
  52.4 0.0 copy-done.4
  52.4 0.0 copy-done.5
  52.4 5.6 %message.1 = bf16[640,8,128]{2,1,0:T(8,128)(2,1)} custom-call(s32[2,256]{1,0:T(2,128)S(1)} %copy-done.5, bf16[640,8,128]{2,1,0:T(8,128)(2,1)S(1)} %bitcast.18, bf16[256,128]{1,0:T(8,128)(2,1)S(1)} %copy-done.1, bf16[2176,1024]{1,0:T(8,128)(2,1)} %w1_hbm.1, f32[1,1024]{1,0:T(1,128)S(1)} %bitcast.20), custom_call_target="tpu_custom_call" | custom-call | tf_op jit(solution)/shard_map/message/pallas_call | solution.py:579
  57.9 4.8 %all-to-all-start.2 = ((bf16[128,5,8,128]{3,2,1,0:T(8,128)(2,1)}), bf16[128,5,8,128]{3,2,1,0:T(8,128)(2,1)S(1)}, u32[]{:S(2)}, u32[]{:S(2)}) async-start(bf16[128,5,8,128]{3,2,1,0:T(8,128)(2,1)} %bitcast.11), calls=%async_computation.2 | async-start | bytes 2621440 | tf_op jit(solution)/shard_map/all_to_all | solution.py:597
  62.7 7.3 %fold.3 = (bf16[1024,1536]{1,0:T(8,128)(2,1)}, f32[1,1536]{1,0:T(1,128)}) custom-call(bf16[1024,1024]{1,0:T(8,128)(2,1)} %w2_ref.3, f32[1,1024]{1,0:T(1,128)} %bitcast.32, bf16[1024,3072]{1,0:T(8,128)(2,1)} %gru_ref.3, f32[1,3072]{1,0:T(1,128)} %bitcast.30), custom_call_target="tpu_custom_call" | custom-call | flops 3221225472 | bytes 6291456 | tf_op jit(solution)/shard_map/fold/pallas_call | solution.py:557
  70.1 1.0 %copy.17.of_ref = s32[1024,1]{1,0:T(8,128)} copy(s32[1024,1]{0,1:T(1,128)S(1)} %bitcast.21) | data formatting | bytes 8192 | tf_op jit(solution)/shard_map/reshape | solution.py:529
  71.1 0.0 copy-start
  71.1 0.0 copy-start.2
  71.1 0.0 copy-start.3
  71.1 0.0 copy-start.7
  71.1 9.5 %hidden_gates.1 = (bf16[768,1024]{1,0:T(8,128)(2,1)}, bf16[768,3072]{1,0:T(8,128)(2,1)}, bf16[1024,1024]{1,0:T(8,128)(2,1)}) custom-call(s32[1024]{0:T(1024)} %copy-done.8, s32[8]{0:T(128)} %copy-done.6, bf16[1024,8,128]{2,1,0:T(8,128)(2,1)} %bitcast.23, bf16[1024,3072]{1,0:T(8,128)(2,1)} %gru_hbm.1, bf16[1024,1024]{1,0:T(8,128)(2,1)} %plain_hbm.1, ...), custom_call_target="tpu_custom_call" | custom-call | flops 4000000000 | bytes 20000000 | tf_op jit(solution)/shard_map/hidden_gates/pallas_call | solution.py:530
  80.6 3.9 %all-to-all-done.2 = bf16[128,5,8,128]{3,2,1,0:T(8,128)(2,1)S(1)} async-done(((bf16[128,5,8,128]{3,2,1,0:T(8,128)(2,1)}), bf16[128,5,8,128]{3,2,1,0:T(8,128)(2,1)S(1)}, u32[]{:S(2)}, u32[]{:S(2)}) %all-to-all-start.2) | async-done | bytes 1310752 | tf_op jit(solution)/shard_map/all_to_all | solution.py:597
  84.5 0.0 copy-done
  84.5 0.0 copy-done.2
  84.5 0.0 copy-done.3
  84.5 0.0 copy-done.7
  84.5 8.0 %update.1 = bf16[1024,1024]{1,0:T(8,128)(2,1)} custom-call(s32[1024]{0:T(1024)S(1)} %get-tuple-element.27.slot_ref, s32[1024]{0:T(1024)S(1)} %get-tuple-element.28.index_ref, s32[1024]{0:T(1024)S(1)} %get-tuple-element.29.count_ref, s32[8]{0:T(128)S(1)} %copy-done.7, bf16[640,8,128]{2,1,0:T(8,128)(2,1)S(1)} %bitcast.17, s32[1024,1]{1,0:T(8,128)S(1)} %copy-done, ...), custom_call_target="tpu_custom_call" | custom-call | tf_op jit(solution)/shard_map/update/pallas_call | solution.py:601
Async XLA Ops:
  1.8 20.6 %all-to-all-start = ((s32[128,1,128]{2,1,0:T(1,128)}), s32[128,1,128]{2,1,0:T(1,128)S(1)}, u32[]{:S(2)}, u32[]{:S(2)}) async-start(s32[128,1,128]{2,1,0:T(1,128)} %bitcast.25), calls=%async_computation | async-start | bytes 131072 | tf_op jit(solution)/shard_map/all_to_all | solution.py:485
  25.9 26.4 %all-to-all-start.1 = ((bf16[128,5,8,128]{3,2,1,0:T(8,128)(2,1)}), bf16[128,5,8,128]{3,2,1,0:T(8,128)(2,1)S(1)}, u32[]{:S(2)}, u32[]{:S(2)}) async-start(bf16[128,5,8,128]{3,2,1,0:T(8,128)(2,1)} %bitcast.6), calls=%async_computation.1 | async-start | bytes 2621440 | tf_op jit(solution)/shard_map/all_to_all | solution.py:507
  37.9 14.5 %copy-start.1 = (bf16[256,128]{1,0:T(8,128)(2,1)S(1)}, bf16[256,128]{1,0:T(8,128)(2,1)}, u32[]{:S(2)}) copy-start(bf16[256,128]{1,0:T(8,128)(2,1)} %feat_ref.1) | copy-start | bytes 196612
  37.9 14.5 %copy-start.4 = (f32[1024]{0:T(1024)S(1)}, f32[1024]{0:T(1024)}, u32[]{:S(2)}) copy-start(f32[1024]{0:T(1024)} %param.18) | copy-start | bytes 12292
  37.9 14.5 %copy-start.5 = (s32[2,256]{1,0:T(2,128)S(1)}, s32[2,256]{1,0:T(2,128)}, u32[]{:S(2)}) copy-start(s32[2,256]{1,0:T(2,128)} %get-tuple-element.34.place_ref) | copy-start | bytes 6148
  45.0 0.6 copy-start.6
  45.6 0.6 copy-start.8
  57.9 26.5 %all-to-all-start.2 = ((bf16[128,5,8,128]{3,2,1,0:T(8,128)(2,1)}), bf16[128,5,8,128]{3,2,1,0:T(8,128)(2,1)S(1)}, u32[]{:S(2)}, u32[]{:S(2)}) async-start(bf16[128,5,8,128]{3,2,1,0:T(8,128)(2,1)} %bitcast.11), calls=%async_computation.2 | async-start | bytes 2621440 | tf_op jit(solution)/shard_map/all_to_all | solution.py:597
  71.1 13.4 %copy-start = (s32[1024,1]{1,0:T(8,128)S(1)}, s32[1024,1]{1,0:T(8,128)}, u32[]{:S(2)}) copy-start(s32[1024,1]{1,0:T(8,128)} %copy.17.of_ref) | copy-start | bytes 12292
  71.1 13.4 %copy-start.2 = (f32[1,1536]{1,0:T(1,128)S(1)}, f32[1,1536]{1,0:T(1,128)}, u32[]{:S(2)}) copy-start(f32[1,1536]{1,0:T(1,128)} %get-tuple-element.43.left_bias_ref) | copy-start | bytes 18436
  71.1 13.4 %copy-start.3 = (f32[1,1536]{1,0:T(1,128)S(1)}, f32[1,1536]{1,0:T(1,128)}, u32[]{:S(2)}) copy-start(f32[1,1536]{1,0:T(1,128)} %get-tuple-element.44.right_bias_ref) | copy-start | bytes 18436
  71.1 13.4 %copy-start.7 = (s32[8]{0:T(128)S(1)}, s32[8]{0:T(128)}, u32[]{:S(2)}) copy-start(s32[8]{0:T(128)} %copy-done.6) | copy-start | bytes 100

commit v7 on v6

--- a/solution.py
+++ b/solution.py
@@ -63,6 +63,7 @@
     codes_ref,
     memory_ref,
     turned_ref,
+    asked_ref,
     wanted_ref,
     rows_ref,
     memory_sem,
@@ -74,7 +75,8 @@
     memory_load.start()
     turned = jnp.transpose(ids_ref[...])[:SUB, :]
     turned_ref[...] = turned
-    load = pltpu.make_async_copy(turned_ref, wanted_ref, load_sem)
+    asked_ref[...] = turned & (ACTIVE - 1)
+    load = pltpu.make_async_copy(asked_ref, wanted_ref, load_sem)
     load.start()
     load.wait()
     keep = pltpu.make_async_copy(turned_ref, codes_ref, load_sem)
@@ -90,10 +92,10 @@
             for a in range(group):
                 p = q * part + i * group + a
                 for k in range(capacity):
-                    rows_ref[p * capacity + k] = memory_ref[wanted_ref[k, p] & (ACTIVE - 1)]
+                    rows_ref[p * capacity + k] = memory_ref[wanted_ref[k, p]]
             return carry
 
-        lax.fori_loop(0, part // group, step, 0)
+        lax.fori_loop(0, part // group, step, 0, unroll=True)
         here = pl.ds(q * part * capacity, part * capacity)
         send = pltpu.make_async_copy(rows_ref.at[here], out_ref.at[here], sems.at[q])
         send.start()
@@ -246,6 +248,7 @@
     tiles_ref,
     inputs_ref,
     partial_ref,
+    got_ref,
     sent_ref,
     sem,
     sems,
@@ -264,12 +267,11 @@
         def fetch(i, c):
             for a in range(group):
                 e = i * group + a
-                tiles_ref[pl.ds(pl.multiple_of(e * SUB, SUB), SUB), :] = rows_ref[place_ref[half, e]].astype(
-                    jnp.float32
-                )
+                got_ref[e] = rows_ref[place_ref[half, e]]
             return c
 
-        lax.fori_loop(0, events // group, fetch, 0)
+        lax.fori_loop(0, events // group, fetch, 0, unroll=True)
+        tiles_ref[...] = got_ref[...].astype(jnp.float32).reshape(events * SUB, LANES)
         inputs_ref[:, half * width : (half + 1) * width] = to_matrix(tiles_ref, 0, events)
     inputs_ref[:, 2 * width :] = feat_ref[...]
     loads[0].wait()
@@ -291,10 +293,11 @@
     def send(i, c):
         for a in range(group):
             e = i * group + a
-            sent_ref[place_ref[1, e]] = tiles_ref[pl.ds(pl.multiple_of(e * SUB, SUB), SUB), :].astype(jnp.bfloat16)
+            sent_ref[place_ref[1, e]] = got_ref[e]
         return c
 
-    lax.fori_loop(0, events // group, send, 0)
+    got_ref[...] = tiles_ref[...].reshape(events, SUB, LANES).astype(jnp.bfloat16)
+    lax.fori_loop(0, events // group, send, 0, unroll=True)
     leave = pltpu.make_async_copy(sent_ref, out_ref, sem)
     leave.start()
     leave.wait()
@@ -495,6 +498,7 @@
         scratch_shapes=[
             pltpu.VMEM((node_rows, cells, LANES), bf16),
             pltpu.VMEM((SUB, devices), i32),
+            pltpu.VMEM((SUB, devices), i32),
             pltpu.SMEM((SUB, devices), i32),
             pltpu.VMEM((slots, cells, LANES), bf16),
             pltpu.SemaphoreType.DMA,
@@ -586,6 +590,7 @@
             pltpu.VMEM((events * SUB, LANES), f32),
             pltpu.VMEM((events, msg_w1.shape[0]), bf16),
             pltpu.VMEM((events, hid), f32),
+            pltpu.VMEM((events, cells, LANES), bf16),
             pltpu.VMEM((slots, cells, LANES), bf16),
             pltpu.SemaphoreType.DMA,
             pltpu.SemaphoreType.DMA((2,)),

time: 93.2 us -> 92.1 us (0.988)
  Pallas kernels: 50.2 us -> 49.2 us
where the time goes in v7:
time: 92.1 us; the launch traced here: 91.4 us
  Pallas kernels  49.2 us (53%)
  starting transfers between devices  20.4 us (22%)
  waiting for transfers between devices  15.7 us (17%)
  local copies, waits for them, and re-layouts  5.78 us (6%)
    pallas_call x2, Pallas kernels, fold(): pl.pallas_call(fold_kernel, out_shape=(shape((hid, last - first), bf16),...  14.7 us
    all_to_all x1, starting transfers between devices, on_device(): lax.all_to_all(ids.reshape(devices, 1, LANES), AXES, split_axis=0, concat...  11.1 us
    pallas_call x1, Pallas kernels, on_device(): pl.pallas_call(hidden_gates_kernel, out_shape=(shape((padded, width), bf1...  9.49 us
    pallas_call x1, Pallas kernels, on_device(): pl.pallas_call(update_kernel, out_shape=shape((node_rows, width), bf16),...  8.04 us
    pallas_call x1, Pallas kernels, on_device(): pl.pallas_call(lambda *refs: compact_kernel(capacity, padded, *refs), out...  7.33 us
    all_to_all x1, waiting for transfers between devices, on_device(): lax.all_to_all(ids.reshape(devices, 1, LANES), AXES, split_axis=0, concat...  5.94 us
    all_to_all x1, waiting for transfers between devices, on_device(): lax.all_to_all(answers.reshape(devices, capacity, cells, LANES), AXES, sp...  5.93 us
    pallas_call x1, Pallas kernels, on_device(): pl.pallas_call(message_kernel, out_shape=shape((slots, cells, LANES), bf1...  5.06 us
  transfers between devices with their start and end apart: 3, of which 3 were waited for; matrix products, arithmetic and copies ran while one was open for 5% of the time, Pallas kernels for 34%

profile of v7, /device:TPU:0, one launch (start us, length us, event | category | flops | bytes accessed | tf_op | source)
XLA Modules:
  0.0 91.4 jit_solution(3251380046266221978)
XLA Ops:
  0.0 1.8 %plan.1 = (s32[128,128]{1,0:T(8,128)}, s32[2,256]{1,0:T(2,128)}) custom-call(s32[2,256]{1,0:T(2,128)} %bitcast.26, s32[2,256]{1,0:T(2,128)} %bitcast.27, s32[1,256]{1,0:T(1,128)} %bitcast.28), custom_call_target="tpu_custom_call" | custom-call | tf_op jit(solution)/shard_map/plan/pallas_call | solution.py:479
  1.8 11.1 %all-to-all-start = ((s32[128,1,128]{2,1,0:T(1,128)}), s32[128,1,128]{2,1,0:T(1,128)S(1)}, u32[]{:S(2)}, u32[]{:S(2)}) async-start(s32[128,1,128]{2,1,0:T(1,128)} %bitcast.25), calls=%async_computation | async-start | bytes 131072 | tf_op jit(solution)/shard_map/all_to_all | solution.py:488
  12.9 3.5 %copy.18 = bf16[128,8,8,128]{3,2,1,0:T(8,128)(2,1)} copy(bf16[128,8,8,128]{3,1,2,0:T(8,128)(2,1)} %bitcast.24) | data formatting | bytes 4194304
  16.4 5.9 %all-to-all-done = s32[128,1,128]{2,1,0:T(1,128)S(1)} async-done(((s32[128,1,128]{2,1,0:T(1,128)}), s32[128,1,128]{2,1,0:T(1,128)S(1)}, u32[]{:S(2)}, u32[]{:S(2)}) %all-to-all-start) | async-done | bytes 65568 | tf_op jit(solution)/shard_map/all_to_all | solution.py:488
  22.4 2.9 %answer.1 = (bf16[640,8,128]{2,1,0:T(8,128)(2,1)}, s32[8,128]{1,0:T(8,128)S(1)}) custom-call(s32[128,128]{1,0:T(8,128)S(1)} %bitcast.19, bf16[1024,8,128]{2,1,0:T(8,128)(2,1)} %bitcast.22), custom_call_target="tpu_custom_call" | custom-call | tf_op jit(solution)/shard_map/answer/pallas_call | solution.py:493
  25.3 4.7 %all-to-all-start.1 = ((bf16[128,5,8,128]{3,2,1,0:T(8,128)(2,1)}), bf16[128,5,8,128]{3,2,1,0:T(8,128)(2,1)S(1)}, u32[]{:S(2)}, u32[]{:S(2)}) async-start(bf16[128,5,8,128]{3,2,1,0:T(8,128)(2,1)} %bitcast.6), calls=%async_computation.1 | async-start | bytes 2621440 | tf_op jit(solution)/shard_map/all_to_all | solution.py:511
  29.9 7.3 %fold.2 = (bf16[1024,1536]{1,0:T(8,128)(2,1)}, f32[1,1536]{1,0:T(1,128)}) custom-call(bf16[1024,1024]{1,0:T(8,128)(2,1)} %w2_ref.3, f32[1,1024]{1,0:T(1,128)} %bitcast.31, bf16[1024,3072]{1,0:T(8,128)(2,1)} %gru_ref.3, f32[1,3072]{1,0:T(1,128)} %bitcast.29), custom_call_target="tpu_custom_call" | custom-call | flops 3221225472 | bytes 6291456 | tf_op jit(solution)/shard_map/fold/pallas_call | solution.py:561
  37.3 0.0 copy-start.1
  37.3 0.0 copy-start.4
  37.3 0.0 copy-start.5
  37.3 7.3 %compact.1 = (s32[1024]{0:T(1024)S(1)}, s32[1024]{0:T(1024)S(1)}, s32[1024]{0:T(1024)S(1)}, s32[1024]{0:T(1024)S(1)}, s32[1024]{0:T(1024)S(1)}, /*index=5*/s32[8]{0:T(128)S(1)}) custom-call(s32[8,128]{1,0:T(8,128)S(1)} %get-tuple-element.26.refs_0_), custom_call_target="tpu_custom_call" | custom-call | flops 4000000000 | bytes 20000000 | tf_op jit(solution)/shard_map/compact/pallas_call | solution.py:515
  44.6 0.0 copy-start.6
  44.6 0.6 copy-done.6
  45.2 0.0 copy-start.8
  45.2 0.6 copy-done.8
  45.8 5.9 %all-to-all-done.1 = bf16[128,5,8,128]{3,2,1,0:T(8,128)(2,1)S(1)} async-done(((bf16[128,5,8,128]{3,2,1,0:T(8,128)(2,1)}), bf16[128,5,8,128]{3,2,1,0:T(8,128)(2,1)S(1)}, u32[]{:S(2)}, u32[]{:S(2)}) %all-to-all-start.1) | async-done | bytes 1310752 | tf_op jit(solution)/shard_map/all_to_all | solution.py:511
  51.7 0.0 copy-done.1
  51.7 0.0 copy-done.4
  51.7 0.0 copy-done.5
  51.7 5.1 %message.1 = bf16[640,8,128]{2,1,0:T(8,128)(2,1)} custom-call(s32[2,256]{1,0:T(2,128)S(1)} %copy-done.5, bf16[640,8,128]{2,1,0:T(8,128)(2,1)S(1)} %bitcast.18, bf16[256,128]{1,0:T(8,128)(2,1)S(1)} %copy-done.1, bf16[2176,1024]{1,0:T(8,128)(2,1)} %w1_hbm.1, f32[1,1024]{1,0:T(1,128)S(1)} %bitcast.20), custom_call_target="tpu_custom_call" | custom-call | tf_op jit(solution)/shard_map/message/pallas_call | solution.py:583
  56.8 4.7 %all-to-all-start.2 = ((bf16[128,5,8,128]{3,2,1,0:T(8,128)(2,1)}), bf16[128,5,8,128]{3,2,1,0:T(8,128)(2,1)S(1)}, u32[]{:S(2)}, u32[]{:S(2)}) async-start(bf16[128,5,8,128]{3,2,1,0:T(8,128)(2,1)} %bitcast.11), calls=%async_computation.2 | async-start | bytes 2621440 | tf_op jit(solution)/shard_map/all_to_all | solution.py:602
  61.5 7.3 %fold.3 = (bf16[1024,1536]{1,0:T(8,128)(2,1)}, f32[1,1536]{1,0:T(1,128)}) custom-call(bf16[1024,1024]{1,0:T(8,128)(2,1)} %w2_ref.3, f32[1,1024]{1,0:T(1,128)} %bitcast.32, bf16[1024,3072]{1,0:T(8,128)(2,1)} %gru_ref.3, f32[1,3072]{1,0:T(1,128)} %bitcast.30), custom_call_target="tpu_custom_call" | custom-call | flops 3221225472 | bytes 6291456 | tf_op jit(solution)/shard_map/fold/pallas_call | solution.py:561
  68.8 1.0 %copy.17.of_ref = s32[1024,1]{1,0:T(8,128)} copy(s32[1024,1]{0,1:T(1,128)S(1)} %bitcast.21) | data formatting | bytes 8192 | tf_op jit(solution)/shard_map/reshape | solution.py:533
  69.8 0.0 copy-start
  69.8 0.0 copy-start.2
  69.8 0.0 copy-start.3
  69.8 0.0 copy-start.7
  69.8 9.5 %hidden_gates.1 = (bf16[768,1024]{1,0:T(8,128)(2,1)}, bf16[768,3072]{1,0:T(8,128)(2,1)}, bf16[1024,1024]{1,0:T(8,128)(2,1)}) custom-call(s32[1024]{0:T(1024)} %copy-done.8, s32[8]{0:T(128)} %copy-done.6, bf16[1024,8,128]{2,1,0:T(8,128)(2,1)} %bitcast.23, bf16[1024,3072]{1,0:T(8,128)(2,1)} %gru_hbm.1, bf16[1024,1024]{1,0:T(8,128)(2,1)} %plain_hbm.1, ...), custom_call_target="tpu_custom_call" | custom-call | flops 4000000000 | bytes 20000000 | tf_op jit(solution)/shard_map/hidden_gates/pallas_call | solution.py:534
  79.3 3.9 %all-to-all-done.2 = bf16[128,5,8,128]{3,2,1,0:T(8,128)(2,1)S(1)} async-done(((bf16[128,5,8,128]{3,2,1,0:T(8,128)(2,1)}), bf16[128,5,8,128]{3,2,1,0:T(8,128)(2,1)S(1)}, u32[]{:S(2)}, u32[]{:S(2)}) %all-to-all-start.2) | async-done | bytes 1310752 | tf_op jit(solution)/shard_map/all_to_all | solution.py:602
  83.2 0.0 copy-done
  83.2 0.0 copy-done.2
  83.2 0.0 copy-done.3
  83.2 0.0 copy-done.7
  83.2 8.0 %update.1 = bf16[1024,1024]{1,0:T(8,128)(2,1)} custom-call(s32[1024]{0:T(1024)S(1)} %get-tuple-element.27.slot_ref, s32[1024]{0:T(1024)S(1)} %get-tuple-element.28.index_ref, s32[1024]{0:T(1024)S(1)} %get-tuple-element.29.count_ref, s32[8]{0:T(128)S(1)} %copy-done.7, bf16[640,8,128]{2,1,0:T(8,128)(2,1)S(1)} %bitcast.17, s32[1024,1]{1,0:T(8,128)S(1)} %copy-done, ...), custom_call_target="tpu_custom_call" | custom-call | tf_op jit(solution)/shard_map/update/pallas_call | solution.py:606
Async XLA Ops:
  1.8 20.6 %all-to-all-start = ((s32[128,1,128]{2,1,0:T(1,128)}), s32[128,1,128]{2,1,0:T(1,128)S(1)}, u32[]{:S(2)}, u32[]{:S(2)}) async-start(s32[128,1,128]{2,1,0:T(1,128)} %bitcast.25), calls=%async_computation | async-start | bytes 131072 | tf_op jit(solution)/shard_map/all_to_all | solution.py:488
  25.3 26.4 %all-to-all-start.1 = ((bf16[128,5,8,128]{3,2,1,0:T(8,128)(2,1)}), bf16[128,5,8,128]{3,2,1,0:T(8,128)(2,1)S(1)}, u32[]{:S(2)}, u32[]{:S(2)}) async-start(bf16[128,5,8,128]{3,2,1,0:T(8,128)(2,1)} %bitcast.6), calls=%async_computation.1 | async-start | bytes 2621440 | tf_op jit(solution)/shard_map/all_to_all | solution.py:511
  37.3 14.5 %copy-start.1 = (bf16[256,128]{1,0:T(8,128)(2,1)S(1)}, bf16[256,128]{1,0:T(8,128)(2,1)}, u32[]{:S(2)}) copy-start(bf16[256,128]{1,0:T(8,128)(2,1)} %feat_ref.1) | copy-start | bytes 196612
  37.3 14.5 %copy-start.4 = (f32[1024]{0:T(1024)S(1)}, f32[1024]{0:T(1024)}, u32[]{:S(2)}) copy-start(f32[1024]{0:T(1024)} %param.18) | copy-start | bytes 12292
  37.3 14.5 %copy-start.5 = (s32[2,256]{1,0:T(2,128)S(1)}, s32[2,256]{1,0:T(2,128)}, u32[]{:S(2)}) copy-start(s32[2,256]{1,0:T(2,128)} %get-tuple-element.34.place_ref) | copy-start | bytes 6148
  44.6 0.6 copy-start.6
  45.2 0.6 copy-start.8
  56.8 26.4 %all-to-all-start.2 = ((bf16[128,5,8,128]{3,2,1,0:T(8,128)(2,1)}), bf16[128,5,8,128]{3,2,1,0:T(8,128)(2,1)S(1)}, u32[]{:S(2)}, u32[]{:S(2)}) async-start(bf16[128,5,8,128]{3,2,1,0:T(8,128)(2,1)} %bitcast.11), calls=%async_computation.2 | async-start | bytes 2621440 | tf_op jit(solution)/shard_map/all_to_all | solution.py:602
  69.8 13.4 %copy-start = (s32[1024,1]{1,0:T(8,128)S(1)}, s32[1024,1]{1,0:T(8,128)}, u32[]{:S(2)}) copy-start(s32[1024,1]{1,0:T(8,128)} %copy.17.of_ref) | copy-start | bytes 12292
  69.8 13.4 %copy-start.2 = (f32[1,1536]{1,0:T(1,128)S(1)}, f32[1,1536]{1,0:T(1,128)}, u32[]{:S(2)}) copy-start(f32[1,1536]{1,0:T(1,128)} %get-tuple-element.43.left_bias_ref) | copy-start | bytes 18436
  69.8 13.4 %copy-start.3 = (f32[1,1536]{1,0:T(1,128)S(1)}, f32[1,1536]{1,0:T(1,128)}, u32[]{:S(2)}) copy-start(f32[1,1536]{1,0:T(1,128)} %get-tuple-element.44.right_bias_ref) | copy-start | bytes 18436
  69.8 13.4 %copy-start.7 = (s32[8]{0:T(128)S(1)}, s32[8]{0:T(128)}, u32[]{:S(2)}) copy-start(s32[8]{0:T(128)} %copy-done.6) | copy-start | bytes 100

commit v8 on v7

--- a/solution.py
+++ b/solution.py
@@ -159,33 +159,22 @@
 def hidden_gates_kernel(
     node_ref,
     size_ref,
-    memory_hbm,
-    gru_hbm,
-    plain_hbm,
+    memory_ref,
+    gru_ref,
+    plain_ref,
     of_ref,
     previous_ref,
     gates_ref,
     kept_ref,
-    memory_ref,
-    gru_ref,
-    plain_ref,
     tiles_ref,
     rows_ref,
     made_ref,
     left_ref,
     sems,
 ):
-    loads = []
-    for source, target in ((memory_hbm, memory_ref), (plain_hbm, plain_ref), (gru_hbm, gru_ref)):
-        load = pltpu.make_async_copy(source, target, sems.at[3 + len(loads)])
-        load.start()
-        loads.append(load)
-    loads[0].wait()
-    loads[1].wait()
     left_ref[...] = jnp.where(of_ref[...] < 0, plain_ref[...].astype(jnp.float32), 0.0).astype(jnp.bfloat16)
     third = pltpu.make_async_copy(left_ref, kept_ref, sems.at[2])
     third.start()
-    loads[2].wait()
     steps = jnp.maximum(pl.cdiv(size_ref[1], TILE), 1)
     width = rows_ref.shape[1]
 
@@ -341,8 +330,8 @@
         loads = [(gates_hbm.at[first_tile, pl.ds(h * 3 * half, 3 * half)], gates_ref.at[:, pl.ds(h * 3 * half, 3 * half)])]
         for g in range(3):
             first = g * width + h * half
-            part = (left_in_hbm, right_in_hbm)[first // split]
-            loads.append((part.at[:, pl.ds(first % split, half)], gru_ref.at[:, pl.ds(first, half)]))
+            part, at = (left_in_hbm, first) if first < split else (right_in_hbm, first - split)
+            loads.append((part.at[:, pl.ds(at, half)], gru_ref.at[:, pl.ds(first, half)]))
         if h == 0:
             loads.append((previous_hbm.at[first_tile], previous_ref))
         else:
@@ -387,7 +376,8 @@
             cols = slice(g * width + j * COLS, g * width + (j + 1) * COLS)
             hid = gates_ref[:, (j * 3 + g) * COLS : (j * 3 + g + 1) * COLS].astype(jnp.float32)
             first = g * width + j * COLS
-            bias = (left_bias_ref, right_bias_ref)[first // split][:, first % split : first % split + COLS]
+            part, at = (left_bias_ref, first) if first < split else (right_bias_ref, first - split)
+            bias = part[:, at : at + COLS]
             into = jnp.dot(aggregate_ref[...], gru_ref[:, cols], preferred_element_type=jnp.float32) + bias
             pre.append((into, hid))
         reset = jax.nn.sigmoid(pre[0][0] + pre[0][1])
@@ -538,17 +528,14 @@
             shape((padded, 3 * width), GATES),
             shape((node_rows, width), bf16),
         ),
-        in_specs=[SM, SM, HBM, HBM, HBM, VM],
+        in_specs=[SM, SM, VM, VM, VM, VM],
         out_specs=(HBM, HBM, HBM),
         scratch_shapes=[
-            pltpu.VMEM((node_rows, cells, LANES), bf16),
-            pltpu.VMEM((width, 3 * width), bf16),
-            pltpu.VMEM((node_rows, width), bf16),
             pltpu.VMEM((TILE * SUB, LANES), f32),
             pltpu.VMEM((TILE, width), bf16),
             pltpu.VMEM((TILE, 3 * width), GATES),
             pltpu.VMEM((node_rows, width), bf16),
-            pltpu.SemaphoreType.DMA((6,)),
+            pltpu.SemaphoreType.DMA((3,)),
         ],
         compiler_params=pltpu.CompilerParams(vmem_limit_bytes=WHOLE),
         cost_estimate=pl.CostEstimate(flops=4_000_000_000, bytes_accessed=20_000_000, transcendentals=0),
@@ -577,7 +564,7 @@
             name="fold",
         )(msg_w2, msg_b2.reshape(1, width), gru_in, gru_bias.reshape(1, 3 * width))
 
-    split = 3 * width // 2
+    split = width
     left_in, left_bias = fold(0, split)
     returned, size, left_in = lax.optimization_barrier((returned, size, left_in))
     outgoing = pl.pallas_call(

time: 92.1 us -> 91.9 us (level)
  waiting for transfers between devices: 15.7 us -> 17.7 us
  Pallas kernels: 49.2 us -> 47.3 us
    all_to_all x1, waiting for transfers between devices: 5.93 us -> 7.91 us  [on_device(): lax.all_to_all(answers.reshape(devices, capacity, cells, LANES), AXES, sp...]
    pallas_call x1, Pallas kernels: 9.49 us -> 8.13 us  [on_device(): pl.pallas_call(hidden_gates_kernel, out_shape=(shape((padded, width), bf1...]
  transfers between devices with their start and end apart: 3 -> 3, of which waited for: 3 -> 3; matrix products, arithmetic and copies ran while one was open for 5% -> 5% of each run, Pallas kernels for 34% -> 32%
where the time goes in v8:
time: 91.9 us; the launch traced here: 91.4 us
  Pallas kernels  47.3 us (51%)
  starting transfers between devices  20.4 us (22%)
  waiting for transfers between devices  17.7 us (19%)
  local copies, waits for them, and re-layouts  5.78 us (6%)
    pallas_call x2, Pallas kernels, fold(): pl.pallas_call(fold_kernel, out_shape=(shape((hid, last - first), bf16),...  14.5 us
    all_to_all x1, starting transfers between devices, on_device(): lax.all_to_all(ids.reshape(devices, 1, LANES), AXES, split_axis=0, concat...  11.1 us
    pallas_call x1, Pallas kernels, on_device(): pl.pallas_call(hidden_gates_kernel, out_shape=(shape((padded, width), bf1...  8.13 us
    pallas_call x1, Pallas kernels, on_device(): pl.pallas_call(update_kernel, out_shape=shape((node_rows, width), bf16),...  8.03 us
    all_to_all x1, waiting for transfers between devices, on_device(): lax.all_to_all(answers.reshape(devices, capacity, cells, LANES), AXES, sp...  7.91 us
    pallas_call x1, Pallas kernels, on_device(): pl.pallas_call(lambda *refs: compact_kernel(capacity, padded, *refs), out...  6.93 us
    all_to_all x1, waiting for transfers between devices, on_device(): lax.all_to_all(ids.reshape(devices, 1, LANES), AXES, split_axis=0, concat...  5.94 us
    pallas_call x1, Pallas kernels, on_device(): pl.pallas_call(message_kernel, out_shape=shape((slots, cells, LANES), bf1...  5.06 us
  transfers between devices with their start and end apart: 3, of which 3 were waited for; matrix products, arithmetic and copies ran while one was open for 5% of the time, Pallas kernels for 32%

profile of v8, /device:TPU:0, one launch (start us, length us, event | category | flops | bytes accessed | tf_op | source)
XLA Modules:
  0.0 91.4 jit_solution(17692553016380230178)
XLA Ops:
  0.0 1.8 %plan.1 = (s32[128,128]{1,0:T(8,128)}, s32[2,256]{1,0:T(2,128)}) custom-call(s32[2,256]{1,0:T(2,128)} %bitcast.30, s32[2,256]{1,0:T(2,128)} %bitcast.31, s32[1,256]{1,0:T(1,128)} %bitcast.32), custom_call_target="tpu_custom_call" | custom-call | tf_op jit(solution)/shard_map/plan/pallas_call | solution.py:469
  1.8 11.1 %all-to-all-start = ((s32[128,1,128]{2,1,0:T(1,128)}), s32[128,1,128]{2,1,0:T(1,128)S(1)}, u32[]{:S(2)}, u32[]{:S(2)}) async-start(s32[128,1,128]{2,1,0:T(1,128)} %bitcast.25), calls=%async_computation | async-start | bytes 131072 | tf_op jit(solution)/shard_map/all_to_all | solution.py:478
  12.9 3.5 %copy.18 = bf16[128,8,8,128]{3,2,1,0:T(8,128)(2,1)} copy(bf16[128,8,8,128]{3,1,2,0:T(8,128)(2,1)} %bitcast.24) | data formatting | bytes 4194304
  16.4 5.9 %all-to-all-done = s32[128,1,128]{2,1,0:T(1,128)S(1)} async-done(((s32[128,1,128]{2,1,0:T(1,128)}), s32[128,1,128]{2,1,0:T(1,128)S(1)}, u32[]{:S(2)}, u32[]{:S(2)}) %all-to-all-start) | async-done | bytes 65568 | tf_op jit(solution)/shard_map/all_to_all | solution.py:478
  22.4 2.9 %answer.1 = (bf16[640,8,128]{2,1,0:T(8,128)(2,1)}, s32[8,128]{1,0:T(8,128)S(1)}) custom-call(s32[128,128]{1,0:T(8,128)S(1)} %bitcast.19, bf16[1024,8,128]{2,1,0:T(8,128)(2,1)} %bitcast.22), custom_call_target="tpu_custom_call" | custom-call | tf_op jit(solution)/shard_map/answer/pallas_call | solution.py:483
  25.3 4.7 %all-to-all-start.1 = ((bf16[128,5,8,128]{3,2,1,0:T(8,128)(2,1)}), bf16[128,5,8,128]{3,2,1,0:T(8,128)(2,1)S(1)}, u32[]{:S(2)}, u32[]{:S(2)}) async-start(bf16[128,5,8,128]{3,2,1,0:T(8,128)(2,1)} %bitcast.6), calls=%async_computation.1 | async-start | bytes 2621440 | tf_op jit(solution)/shard_map/all_to_all | solution.py:501
  29.9 5.7 %fold.2 = (bf16[1024,1024]{1,0:T(8,128)(2,1)}, f32[1,1024]{1,0:T(1,128)}) custom-call(bf16[1024,1024]{1,0:T(8,128)(2,1)} %w2_ref.3, f32[1,1024]{1,0:T(1,128)} %bitcast.28, bf16[1024,3072]{1,0:T(8,128)(2,1)} %gru_ref.5, f32[1,3072]{1,0:T(1,128)} %bitcast.26), custom_call_target="tpu_custom_call" | custom-call | flops 2147483648 | bytes 4194304 | tf_op jit(solution)/shard_map/fold/pallas_call | solution.py:548
  35.7 0.0 copy-start.1
  35.7 0.0 copy-start.3
  35.7 0.0 copy-start.5
  35.7 6.9 %compact.1 = (s32[1024]{0:T(1024)S(1)}, s32[1024]{0:T(1024)S(1)}, s32[1024]{0:T(1024)S(1)}, s32[1024]{0:T(1024)S(1)}, s32[1024]{0:T(1024)S(1)}, /*index=5*/s32[8]{0:T(128)S(1)}) custom-call(s32[8,128]{1,0:T(8,128)S(1)} %get-tuple-element.26.refs_0_), custom_call_target="tpu_custom_call" | custom-call | flops 4000000000 | bytes 20000000 | tf_op jit(solution)/shard_map/compact/pallas_call | solution.py:505
  42.6 0.0 copy-start.6
  42.6 0.6 copy-done.6
  43.2 0.0 copy-start.8
  43.2 0.6 copy-done.8
  43.8 7.9 %all-to-all-done.1 = bf16[128,5,8,128]{3,2,1,0:T(8,128)(2,1)S(1)} async-done(((bf16[128,5,8,128]{3,2,1,0:T(8,128)(2,1)}), bf16[128,5,8,128]{3,2,1,0:T(8,128)(2,1)S(1)}, u32[]{:S(2)}, u32[]{:S(2)}) %all-to-all-start.1) | async-done | bytes 1310752 | tf_op jit(solution)/shard_map/all_to_all | solution.py:501
  51.7 0.0 copy-done.1
  51.7 0.0 copy-done.3
  51.7 0.0 copy-done.5
  51.7 5.1 %message.1 = bf16[640,8,128]{2,1,0:T(8,128)(2,1)} custom-call(s32[2,256]{1,0:T(2,128)S(1)} %copy-done.5, bf16[640,8,128]{2,1,0:T(8,128)(2,1)S(1)} %bitcast.18, bf16[256,128]{1,0:T(8,128)(2,1)S(1)} %copy-done.1, bf16[2176,1024]{1,0:T(8,128)(2,1)} %w1_hbm.1, f32[1,1024]{1,0:T(1,128)S(1)} %bitcast.20), custom_call_target="tpu_custom_call" | custom-call | tf_op jit(solution)/shard_map/message/pallas_call | solution.py:570
  56.8 4.7 %all-to-all-start.2 = ((bf16[128,5,8,128]{3,2,1,0:T(8,128)(2,1)}), bf16[128,5,8,128]{3,2,1,0:T(8,128)(2,1)S(1)}, u32[]{:S(2)}, u32[]{:S(2)}) async-start(bf16[128,5,8,128]{3,2,1,0:T(8,128)(2,1)} %bitcast.11), calls=%async_computation.2 | async-start | bytes 2621440 | tf_op jit(solution)/shard_map/all_to_all | solution.py:589
  61.5 8.7 %fold.3 = (bf16[1024,2048]{1,0:T(8,128)(2,1)}, f32[1,2048]{1,0:T(1,128)}) custom-call(bf16[1024,1024]{1,0:T(8,128)(2,1)} %w2_ref.3, f32[1,1024]{1,0:T(1,128)} %bitcast.29, bf16[1024,3072]{1,0:T(8,128)(2,1)} %gru_ref.5, f32[1,3072]{1,0:T(1,128)} %bitcast.27), custom_call_target="tpu_custom_call" | custom-call | flops 4294967296 | bytes 8388608 | tf_op jit(solution)/shard_map/fold/pallas_call | solution.py:548
  70.2 1.0 %copy.17.of_ref = s32[1024,1]{1,0:T(8,128)} copy(s32[1024,1]{0,1:T(1,128)S(1)} %bitcast.21) | data formatting | bytes 8192 | tf_op jit(solution)/shard_map/reshape | solution.py:523
  71.2 0.0 copy-start
  71.2 0.0 copy-start.2
  71.2 0.0 copy-start.4
  71.2 0.0 copy-start.7
  71.3 8.1 %hidden_gates.1 = (bf16[768,1024]{1,0:T(8,128)(2,1)}, bf16[768,3072]{1,0:T(8,128)(2,1)}, bf16[1024,1024]{1,0:T(8,128)(2,1)}) custom-call(s32[1024]{0:T(1024)} %copy-done.8, s32[8]{0:T(128)} %copy-done.6, bf16[1024,8,128]{2,1,0:T(8,128)(2,1)} %bitcast.23, bf16[1024,3072]{1,0:T(8,128)(2,1)} %gru_ref.4, bf16[1024,1024]{1,0:T(8,128)(2,1)} %plain_ref.1, ...), custom_call_target="tpu_custom_call" | custom-call | flops 4000000000 | bytes 20000000 | tf_op jit(solution)/shard_map/hidden_gates/pallas_call | solution.py:524
  79.4 3.8 %all-to-all-done.2 = bf16[128,5,8,128]{3,2,1,0:T(8,128)(2,1)S(1)} async-done(((bf16[128,5,8,128]{3,2,1,0:T(8,128)(2,1)}), bf16[128,5,8,128]{3,2,1,0:T(8,128)(2,1)S(1)}, u32[]{:S(2)}, u32[]{:S(2)}) %all-to-all-start.2) | async-done | bytes 1310752 | tf_op jit(solution)/shard_map/all_to_all | solution.py:589
  83.2 0.0 copy-done
  83.2 0.0 copy-done.2
  83.2 0.0 copy-done.4
  83.2 0.0 copy-done.7
  83.2 8.0 %update.1 = bf16[1024,1024]{1,0:T(8,128)(2,1)} custom-call(s32[1024]{0:T(1024)S(1)} %get-tuple-element.27.slot_ref, s32[1024]{0:T(1024)S(1)} %get-tuple-element.28.index_ref, s32[1024]{0:T(1024)S(1)} %get-tuple-element.29.count_ref, s32[8]{0:T(128)S(1)} %copy-done.7, bf16[640,8,128]{2,1,0:T(8,128)(2,1)S(1)} %bitcast.17, s32[1024,1]{1,0:T(8,128)S(1)} %copy-done, ...), custom_call_target="tpu_custom_call" | custom-call | tf_op jit(solution)/shard_map/update/pallas_call | solution.py:593
Async XLA Ops:
  1.8 20.6 %all-to-all-start = ((s32[128,1,128]{2,1,0:T(1,128)}), s32[128,1,128]{2,1,0:T(1,128)S(1)}, u32[]{:S(2)}, u32[]{:S(2)}) async-start(s32[128,1,128]{2,1,0:T(1,128)} %bitcast.25), calls=%async_computation | async-start | bytes 131072 | tf_op jit(solution)/shard_map/all_to_all | solution.py:478
  25.3 26.4 %all-to-all-start.1 = ((bf16[128,5,8,128]{3,2,1,0:T(8,128)(2,1)}), bf16[128,5,8,128]{3,2,1,0:T(8,128)(2,1)S(1)}, u32[]{:S(2)}, u32[]{:S(2)}) async-start(bf16[128,5,8,128]{3,2,1,0:T(8,128)(2,1)} %bitcast.6), calls=%async_computation.1 | async-start | bytes 2621440 | tf_op jit(solution)/shard_map/all_to_all | solution.py:501
  35.7 16.0 %copy-start.1 = (bf16[256,128]{1,0:T(8,128)(2,1)S(1)}, bf16[256,128]{1,0:T(8,128)(2,1)}, u32[]{:S(2)}) copy-start(bf16[256,128]{1,0:T(8,128)(2,1)} %feat_ref.1) | copy-start | bytes 196612
  35.7 16.0 %copy-start.3 = (f32[1024]{0:T(1024)S(1)}, f32[1024]{0:T(1024)}, u32[]{:S(2)}) copy-start(f32[1024]{0:T(1024)} %param.18) | copy-start | bytes 12292
  35.7 16.0 %copy-start.5 = (s32[2,256]{1,0:T(2,128)S(1)}, s32[2,256]{1,0:T(2,128)}, u32[]{:S(2)}) copy-start(s32[2,256]{1,0:T(2,128)} %get-tuple-element.34.place_ref) | copy-start | bytes 6148
  42.6 0.6 copy-start.6
  43.2 0.6 copy-start.8
  56.8 26.4 %all-to-all-start.2 = ((bf16[128,5,8,128]{3,2,1,0:T(8,128)(2,1)}), bf16[128,5,8,128]{3,2,1,0:T(8,128)(2,1)S(1)}, u32[]{:S(2)}, u32[]{:S(2)}) async-start(bf16[128,5,8,128]{3,2,1,0:T(8,128)(2,1)} %bitcast.11), calls=%async_computation.2 | async-start | bytes 2621440 | tf_op jit(solution)/shard_map/all_to_all | solution.py:589
  71.2 12.0 %copy-start = (s32[1024,1]{1,0:T(8,128)S(1)}, s32[1024,1]{1,0:T(8,128)}, u32[]{:S(2)}) copy-start(s32[1024,1]{1,0:T(8,128)} %copy.17.of_ref) | copy-start | bytes 12292
  71.2 12.0 %copy-start.2 = (f32[1,2048]{1,0:T(1,128)S(1)}, f32[1,2048]{1,0:T(1,128)}, u32[]{:S(2)}) copy-start(f32[1,2048]{1,0:T(1,128)} %get-tuple-element.44.right_bias_ref) | copy-start | bytes 24580
  71.2 12.0 %copy-start.4 = (f32[1,1024]{1,0:T(1,128)S(1)}, f32[1,1024]{1,0:T(1,128)}, u32[]{:S(2)}) copy-start(f32[1,1024]{1,0:T(1,128)} %get-tuple-element.43.left_bias_ref) | copy-start | bytes 12292
  71.2 12.0 %copy-start.7 = (s32[8]{0:T(128)S(1)}, s32[8]{0:T(128)}, u32[]{:S(2)}) copy-start(s32[8]{0:T(128)} %copy-done.6) | copy-start | bytes 100

commit v9 on v8

--- a/solution.py
+++ b/solution.py
@@ -17,7 +17,8 @@
 MIB = 1 << 20
 WHOLE = 58 * MIB
 MOST = 51 * MIB
-ANSWER = 51968 * 1024
+MESSAGE = 48 * MIB
+ANSWER = 48 * MIB
 
 VM = pl.BlockSpec(memory_space=pltpu.VMEM)
 SM = pl.BlockSpec(memory_space=pltpu.SMEM)
@@ -58,21 +59,17 @@
 def answer_kernel(
     capacity,
     ids_ref,
-    memory_hbm,
+    memory_ref,
     out_ref,
     codes_ref,
-    memory_ref,
     turned_ref,
     asked_ref,
     wanted_ref,
     rows_ref,
-    memory_sem,
     load_sem,
     sems,
 ):
     devices = ids_ref.shape[0]
-    memory_load = pltpu.make_async_copy(memory_hbm, memory_ref, memory_sem)
-    memory_load.start()
     turned = jnp.transpose(ids_ref[...])[:SUB, :]
     turned_ref[...] = turned
     asked_ref[...] = turned & (ACTIVE - 1)
@@ -81,7 +78,6 @@
     load.wait()
     keep = pltpu.make_async_copy(turned_ref, codes_ref, load_sem)
     keep.start()
-    memory_load.wait()
     group = 8
     chunks = sems.shape[0]
     part = devices // chunks
@@ -230,6 +226,7 @@
     place_ref,
     rows_ref,
     feat_ref,
+    w1_first_ref,
     w1_hbm,
     b1_ref,
     out_ref,
@@ -240,17 +237,12 @@
     got_ref,
     sent_ref,
     sem,
-    sems,
 ):
     events = feat_ref.shape[0]
-    depth, hid = w1_ref.shape
-    width = (depth - feat_ref.shape[1]) // 2
+    width, hid = w1_first_ref.shape
     group = 16
-    loads = []
-    for i, rows in enumerate((pl.ds(0, width), pl.ds(width, depth - width))):
-        load = pltpu.make_async_copy(w1_hbm.at[rows], w1_ref.at[rows], sems.at[i])
-        load.start()
-        loads.append(load)
+    load = pltpu.make_async_copy(w1_hbm.at[pl.ds(width, w1_ref.shape[0])], w1_ref, sem)
+    load.start()
     for half in range(2):
 
         def fetch(i, c):
@@ -263,17 +255,16 @@
         tiles_ref[...] = got_ref[...].astype(jnp.float32).reshape(events * SUB, LANES)
         inputs_ref[:, half * width : (half + 1) * width] = to_matrix(tiles_ref, 0, events)
     inputs_ref[:, 2 * width :] = feat_ref[...]
-    loads[0].wait()
     for j in range(hid // COLS):
         cols = slice(j * COLS, (j + 1) * COLS)
         partial_ref[:, cols] = (
-            jnp.dot(inputs_ref[:, :width], w1_ref[:width, cols], preferred_element_type=jnp.float32) + b1_ref[:, cols]
+            jnp.dot(inputs_ref[:, :width], w1_first_ref[:, cols], preferred_element_type=jnp.float32) + b1_ref[:, cols]
         )
-    loads[1].wait()
+    load.wait()
     for j in range(hid // COLS):
         cols = slice(j * COLS, (j + 1) * COLS)
         h = partial_ref[:, cols] + jnp.dot(
-            inputs_ref[:, width:], w1_ref[width:, cols], preferred_element_type=jnp.float32
+            inputs_ref[:, width:], w1_ref[:, cols], preferred_element_type=jnp.float32
         )
         h = jnp.maximum(h, 0.0)
         for c in range(COLS // LANES):
@@ -482,16 +473,14 @@
 
     answers, codes = pl.pallas_call(
         lambda *refs: answer_kernel(capacity, *refs),
-        out_shape=(shape((slots, cells, LANES), bf16), shape((SUB, devices), i32)),
-        in_specs=[VM, HBM],
+        out_shape=(pltpu.HBM((slots, cells, LANES), bf16), pltpu.HBM((SUB, devices), i32)),
+        in_specs=[VM, VM],
         out_specs=(HBM, HBM),
         scratch_shapes=[
-            pltpu.VMEM((node_rows, cells, LANES), bf16),
             pltpu.VMEM((SUB, devices), i32),
             pltpu.VMEM((SUB, devices), i32),
             pltpu.SMEM((SUB, devices), i32),
             pltpu.VMEM((slots, cells, LANES), bf16),
-            pltpu.SemaphoreType.DMA,
             pltpu.SemaphoreType.DMA,
             pltpu.SemaphoreType.DMA((4,)),
         ],
@@ -569,22 +558,21 @@
     returned, size, left_in = lax.optimization_barrier((returned, size, left_in))
     outgoing = pl.pallas_call(
         message_kernel,
-        out_shape=shape((slots, cells, LANES), bf16),
-        in_specs=[SM, VM, VM, HBM, VM],
+        out_shape=pltpu.HBM((slots, cells, LANES), bf16),
+        in_specs=[SM, VM, VM, VM, HBM, VM],
         out_specs=HBM,
         scratch_shapes=[
-            pltpu.VMEM(msg_w1.shape, bf16),
+            pltpu.VMEM((msg_w1.shape[0] - width, hid), bf16),
             pltpu.VMEM((events * SUB, LANES), f32),
             pltpu.VMEM((events, msg_w1.shape[0]), bf16),
             pltpu.VMEM((events, hid), f32),
             pltpu.VMEM((events, cells, LANES), bf16),
             pltpu.VMEM((slots, cells, LANES), bf16),
             pltpu.SemaphoreType.DMA,
-            pltpu.SemaphoreType.DMA((2,)),
         ],
-        compiler_params=pltpu.CompilerParams(vmem_limit_bytes=MOST),
+        compiler_params=pltpu.CompilerParams(vmem_limit_bytes=MESSAGE),
         name="message",
-    )(place, returned, edge_feat, msg_w1, msg_b1.reshape(1, hid))
+    )(place, returned, edge_feat, msg_w1[:width], msg_w1, msg_b1.reshape(1, hid))
     right_in, right_bias = fold(split, 3 * width)
     incoming = lax.all_to_all(
         outgoing.reshape(devices, capacity, cells, LANES), AXES, split_axis=0, concat_axis=0, tiled=True

time: 91.9 us -> 91.2 us (level)
  waiting for transfers between devices: 17.7 us -> 16.5 us
    all_to_all x1, waiting for transfers between devices: 7.91 us -> 5.4 us  [on_device(): lax.all_to_all(answers.reshape(devices, capacity, cells, LANES), AXES, sp...]
    slice x0 -> x1, local copies, waits for them, and re-layouts: none -> 1.76 us  [on_device(): msg_w1[:width]]
    unnamed x19 -> x23, local copies, waits for them, and re-layouts: 4.74 us -> 3.35 us
    all_to_all x1, waiting for transfers between devices: 5.94 us -> 7.24 us  [on_device(): lax.all_to_all(ids.reshape(devices, 1, LANES), AXES, split_axis=0, concat...]
    pallas_call x2, Pallas kernels: 7.95 us -> 6.92 us  [the longest x1 4.97 us: on_device(): pl.pallas_call(message_kernel, out_shape=pltpu.HBM((slots, cells, LANES),...]
  transfers between devices with their start and end apart: 3 -> 3, of which waited for: 3 -> 3; matrix products, arithmetic and copies ran while one was open for 5% -> 6% of each run, Pallas kernels for 32% -> 33%
where the time goes in v9:
time: 91.2 us; the launch traced here: 90.9 us
  Pallas kernels  47 us (52%)
  starting transfers between devices  20.9 us (23%)
  waiting for transfers between devices  16.5 us (18%)
  local copies, waits for them, and re-layouts  6.17 us (7%)
    pallas_call x2, Pallas kernels, fold(): pl.pallas_call(fold_kernel, out_shape=(shape((hid, last - first), bf16),...  14.5 us
    all_to_all x1, starting transfers between devices, on_device(): lax.all_to_all(ids.reshape(devices, 1, LANES), AXES, split_axis=0, concat...  11.1 us
    pallas_call x1, Pallas kernels, on_device(): pl.pallas_call(hidden_gates_kernel, out_shape=(shape((padded, width), bf1...  8.12 us
    pallas_call x1, Pallas kernels, on_device(): pl.pallas_call(update_kernel, out_shape=shape((node_rows, width), bf16),...  8.03 us
    pallas_call x1, Pallas kernels, on_device(): pl.pallas_call(lambda *refs: compact_kernel(capacity, padded, *refs), out...  7.71 us
    all_to_all x1, waiting for transfers between devices, on_device(): lax.all_to_all(ids.reshape(devices, 1, LANES), AXES, split_axis=0, concat...  7.24 us
    all_to_all x1, waiting for transfers between devices, on_device(): lax.all_to_all(answers.reshape(devices, capacity, cells, LANES), AXES, sp...  5.4 us
    all_to_all x1, starting transfers between devices, on_device(): lax.all_to_all(outgoing.reshape(devices, capacity, cells, LANES), AXES, s...  5.14 us
  transfers between devices with their start and end apart: 3, of which 3 were waited for; matrix products, arithmetic and copies ran while one was open for 6% of the time, Pallas kernels for 33%

profile of v9, /device:TPU:0, one launch (start us, length us, event | category | flops | bytes accessed | tf_op | source)
XLA Modules:
  0.0 90.9 jit_solution(2594117852063342322)
XLA Ops:
  0.0 1.8 %plan.1 = (s32[128,128]{1,0:T(8,128)}, s32[2,256]{1,0:T(2,128)}) custom-call(s32[2,256]{1,0:T(2,128)} %bitcast.32, s32[2,256]{1,0:T(2,128)} %bitcast.33, s32[1,256]{1,0:T(1,128)} %bitcast.34), custom_call_target="tpu_custom_call" | custom-call | tf_op jit(solution)/shard_map/plan/pallas_call | solution.py:460
  1.8 11.1 %all-to-all-start = ((s32[128,1,128]{2,1,0:T(1,128)}), s32[128,1,128]{2,1,0:T(1,128)S(1)}, u32[]{:S(2)}, u32[]{:S(2)}) async-start(s32[128,1,128]{2,1,0:T(1,128)} %bitcast.27), calls=%async_computation | async-start | bytes 131072 | tf_op jit(solution)/shard_map/all_to_all | solution.py:469
  12.9 2.2 %copy.18 = bf16[128,8,8,128]{3,2,1,0:T(8,128)(2,1)S(1)} copy(bf16[128,8,8,128]{3,1,2,0:T(8,128)(2,1)} %bitcast.25) | data formatting | bytes 4194304
  15.1 0.0 copy-start
  15.1 7.2 %all-to-all-done = s32[128,1,128]{2,1,0:T(1,128)S(1)} async-done(((s32[128,1,128]{2,1,0:T(1,128)}), s32[128,1,128]{2,1,0:T(1,128)S(1)}, u32[]{:S(2)}, u32[]{:S(2)}) %all-to-all-start) | async-done | bytes 65568 | tf_op jit(solution)/shard_map/all_to_all | solution.py:469
  22.4 1.9 %answer.1 = (bf16[640,8,128]{2,1,0:T(8,128)(2,1)}, s32[8,128]{1,0:T(8,128)}) custom-call(s32[128,128]{1,0:T(8,128)S(1)} %bitcast.21, bf16[1024,8,128]{2,1,0:T(8,128)(2,1)S(1)} %bitcast.17), custom_call_target="tpu_custom_call" | custom-call | tf_op jit(solution)/shard_map/answer/pallas_call | solution.py:474
  24.3 0.0 copy-done
  24.4 4.7 %all-to-all-start.1 = ((bf16[128,5,8,128]{3,2,1,0:T(8,128)(2,1)}), bf16[128,5,8,128]{3,2,1,0:T(8,128)(2,1)S(1)}, u32[]{:S(2)}, u32[]{:S(2)}) async-start(bf16[128,5,8,128]{3,2,1,0:T(8,128)(2,1)} %bitcast.26), calls=%async_computation.1 | async-start | bytes 2621440 | tf_op jit(solution)/shard_map/all_to_all | solution.py:490
  29.0 1.8 %slice.3.w1_first_ref = bf16[1024,1024]{1,0:T(8,128)(2,1)S(1)} slice(bf16[2176,1024]{1,0:T(8,128)(2,1)} %w1_hbm.1), slice={[0:1024], [0:1024]} | slice | bytes 4194304 | tf_op jit(solution)/shard_map/slice | solution.py:575
  30.8 0.0 copy-start.9
  30.8 5.7 %fold.2 = (bf16[1024,1024]{1,0:T(8,128)(2,1)}, f32[1,1024]{1,0:T(1,128)}) custom-call(bf16[1024,1024]{1,0:T(8,128)(2,1)} %w2_ref.3, f32[1,1024]{1,0:T(1,128)} %bitcast.30, bf16[1024,3072]{1,0:T(8,128)(2,1)} %gru_ref.5, f32[1,3072]{1,0:T(1,128)} %bitcast.28), custom_call_target="tpu_custom_call" | custom-call | flops 2147483648 | bytes 4194304 | tf_op jit(solution)/shard_map/fold/pallas_call | solution.py:537
  36.5 0.0 copy-done.9
  36.5 0.0 copy-start.2
  36.5 0.0 copy-start.4
  36.5 0.0 copy-start.6
  36.6 7.7 %compact.1 = (s32[1024]{0:T(1024)S(1)}, s32[1024]{0:T(1024)S(1)}, s32[1024]{0:T(1024)S(1)}, s32[1024]{0:T(1024)S(1)}, s32[1024]{0:T(1024)S(1)}, /*index=5*/s32[8]{0:T(128)S(1)}) custom-call(s32[8,128]{1,0:T(8,128)S(1)} %copy-done.9), custom_call_target="tpu_custom_call" | custom-call | flops 4000000000 | bytes 20000000 | tf_op jit(solution)/shard_map/compact/pallas_call | solution.py:494
  44.3 0.0 copy-start.7
  44.3 0.5 copy-done.7
  44.8 0.0 copy-start.10
  44.8 0.6 copy-done.10
  45.4 5.4 %all-to-all-done.1 = bf16[128,5,8,128]{3,2,1,0:T(8,128)(2,1)S(1)} async-done(((bf16[128,5,8,128]{3,2,1,0:T(8,128)(2,1)}), bf16[128,5,8,128]{3,2,1,0:T(8,128)(2,1)S(1)}, u32[]{:S(2)}, u32[]{:S(2)}) %all-to-all-start.1) | async-done | bytes 1310752 | tf_op jit(solution)/shard_map/all_to_all | solution.py:490
  50.8 0.0 copy-done.2
  50.8 0.0 copy-done.4
  50.8 0.0 copy-done.6
  50.8 5.0 %message.1 = bf16[640,8,128]{2,1,0:T(8,128)(2,1)} custom-call(s32[2,256]{1,0:T(2,128)S(1)} %copy-done.6, bf16[640,8,128]{2,1,0:T(8,128)(2,1)S(1)} %bitcast.20, bf16[256,128]{1,0:T(8,128)(2,1)S(1)} %copy-done.2, bf16[1024,1024]{1,0:T(8,128)(2,1)S(1)} %slice.3.w1_first_ref, bf16[2176,1024]{1,0:T(8,128)(2,1)} %w1_hbm.1, f32[1,1024]{1,0:T(1,128)S(1)} %bitcast.22), custom_call_target="tpu_custom_call" | custom-call | tf_op jit(solution)/shard_map/message/pallas_call | solution.py:559
  55.8 5.1 %all-to-all-start.2 = ((bf16[128,5,8,128]{3,2,1,0:T(8,128)(2,1)}), bf16[128,5,8,128]{3,2,1,0:T(8,128)(2,1)S(1)}, u32[]{:S(2)}, u32[]{:S(2)}) async-start(bf16[128,5,8,128]{3,2,1,0:T(8,128)(2,1)} %bitcast.24), calls=%async_computation.2 | async-start | bytes 2621440 | tf_op jit(solution)/shard_map/all_to_all | solution.py:577
  60.9 8.7 %fold.3 = (bf16[1024,2048]{1,0:T(8,128)(2,1)}, f32[1,2048]{1,0:T(1,128)}) custom-call(bf16[1024,1024]{1,0:T(8,128)(2,1)} %w2_ref.3, f32[1,1024]{1,0:T(1,128)} %bitcast.31, bf16[1024,3072]{1,0:T(8,128)(2,1)} %gru_ref.5, f32[1,3072]{1,0:T(1,128)} %bitcast.29), custom_call_target="tpu_custom_call" | custom-call | flops 4294967296 | bytes 8388608 | tf_op jit(solution)/shard_map/fold/pallas_call | solution.py:537
  69.7 1.1 %copy.17.of_ref = s32[1024,1]{1,0:T(8,128)} copy(s32[1024,1]{0,1:T(1,128)S(1)} %bitcast.23) | data formatting | bytes 8192 | tf_op jit(solution)/shard_map/reshape | solution.py:512
  70.7 0.0 copy-start.1
  70.7 0.0 copy-start.3
  70.7 0.0 copy-start.5
  70.7 0.0 copy-start.8
  70.7 8.1 %hidden_gates.1 = (bf16[768,1024]{1,0:T(8,128)(2,1)}, bf16[768,3072]{1,0:T(8,128)(2,1)}, bf16[1024,1024]{1,0:T(8,128)(2,1)}) custom-call(s32[1024]{0:T(1024)} %copy-done.10, s32[8]{0:T(128)} %copy-done.7, bf16[1024,8,128]{2,1,0:T(8,128)(2,1)} %bitcast.18, bf16[1024,3072]{1,0:T(8,128)(2,1)} %gru_ref.4, bf16[1024,1024]{1,0:T(8,128)(2,1)} %plain_ref.1, ...), custom_call_target="tpu_custom_call" | custom-call | flops 4000000000 | bytes 20000000 | tf_op jit(solution)/shard_map/hidden_gates/pallas_call | solution.py:513
  78.8 3.8 %all-to-all-done.2 = bf16[128,5,8,128]{3,2,1,0:T(8,128)(2,1)S(1)} async-done(((bf16[128,5,8,128]{3,2,1,0:T(8,128)(2,1)}), bf16[128,5,8,128]{3,2,1,0:T(8,128)(2,1)S(1)}, u32[]{:S(2)}, u32[]{:S(2)}) %all-to-all-start.2) | async-done | bytes 1310752 | tf_op jit(solution)/shard_map/all_to_all | solution.py:577
  82.7 0.0 copy-done.1
  82.7 0.0 copy-done.3
  82.7 0.0 copy-done.5
  82.7 0.0 copy-done.8
  82.7 8.0 %update.1 = bf16[1024,1024]{1,0:T(8,128)(2,1)} custom-call(s32[1024]{0:T(1024)S(1)} %get-tuple-element.27.slot_ref, s32[1024]{0:T(1024)S(1)} %get-tuple-element.28.index_ref, s32[1024]{0:T(1024)S(1)} %get-tuple-element.29.count_ref, s32[8]{0:T(128)S(1)} %copy-done.8, bf16[640,8,128]{2,1,0:T(8,128)(2,1)S(1)} %bitcast.19, s32[1024,1]{1,0:T(8,128)S(1)} %copy-done.1, ...), custom_call_target="tpu_custom_call" | custom-call | tf_op jit(solution)/shard_map/update/pallas_call | solution.py:581
Async XLA Ops:
  1.8 20.6 %all-to-all-start = ((s32[128,1,128]{2,1,0:T(1,128)}), s32[128,1,128]{2,1,0:T(1,128)S(1)}, u32[]{:S(2)}, u32[]{:S(2)}) async-start(s32[128,1,128]{2,1,0:T(1,128)} %bitcast.27), calls=%async_computation | async-start | bytes 131072 | tf_op jit(solution)/shard_map/all_to_all | solution.py:469
  15.1 9.2 %copy-start = (bf16[128,8,8,128]{3,2,1,0:T(8,128)(2,1)}, bf16[128,8,8,128]{3,2,1,0:T(8,128)(2,1)S(1)}, u32[]{:S(2)}) copy-start(bf16[128,8,8,128]{3,2,1,0:T(8,128)(2,1)S(1)} %copy.18) | copy-start | bytes 6291460
  24.4 26.4 %all-to-all-start.1 = ((bf16[128,5,8,128]{3,2,1,0:T(8,128)(2,1)}), bf16[128,5,8,128]{3,2,1,0:T(8,128)(2,1)S(1)}, u32[]{:S(2)}, u32[]{:S(2)}) async-start(bf16[128,5,8,128]{3,2,1,0:T(8,128)(2,1)} %bitcast.26), calls=%async_computation.1 | async-start | bytes 2621440 | tf_op jit(solution)/shard_map/all_to_all | solution.py:490
  30.8 5.7 %copy-start.9 = (s32[8,128]{1,0:T(8,128)S(1)}, s32[8,128]{1,0:T(8,128)}, u32[]{:S(2)}) copy-start(s32[8,128]{1,0:T(8,128)} %get-tuple-element.26.refs_0_) | copy-start | bytes 12292
  36.5 14.3 %copy-start.2 = (bf16[256,128]{1,0:T(8,128)(2,1)S(1)}, bf16[256,128]{1,0:T(8,128)(2,1)}, u32[]{:S(2)}) copy-start(bf16[256,128]{1,0:T(8,128)(2,1)} %feat_ref.1) | copy-start | bytes 196612
  36.5 14.3 %copy-start.4 = (f32[1024]{0:T(1024)S(1)}, f32[1024]{0:T(1024)}, u32[]{:S(2)}) copy-start(f32[1024]{0:T(1024)} %param.18) | copy-start | bytes 12292
  36.5 14.2 %copy-start.6 = (s32[2,256]{1,0:T(2,128)S(1)}, s32[2,256]{1,0:T(2,128)}, u32[]{:S(2)}) copy-start(s32[2,256]{1,0:T(2,128)} %get-tuple-element.34.place_ref) | copy-start | bytes 6148
  44.3 0.5 copy-start.7
  44.8 0.6 copy-start.10
  55.8 26.9 %all-to-all-start.2 = ((bf16[128,5,8,128]{3,2,1,0:T(8,128)(2,1)}), bf16[128,5,8,128]{3,2,1,0:T(8,128)(2,1)S(1)}, u32[]{:S(2)}, u32[]{:S(2)}) async-start(bf16[128,5,8,128]{3,2,1,0:T(8,128)(2,1)} %bitcast.24), calls=%async_computation.2 | async-start | bytes 2621440 | tf_op jit(solution)/shard_map/all_to_all | solution.py:577
  70.7 12.0 %copy-start.1 = (s32[1024,1]{1,0:T(8,128)S(1)}, s32[1024,1]{1,0:T(8,128)}, u32[]{:S(2)}) copy-start(s32[1024,1]{1,0:T(8,128)} %copy.17.of_ref) | copy-start | bytes 12292
  70.7 12.0 %copy-start.3 = (f32[1,2048]{1,0:T(1,128)S(1)}, f32[1,2048]{1,0:T(1,128)}, u32[]{:S(2)}) copy-start(f32[1,2048]{1,0:T(1,128)} %get-tuple-element.44.right_bias_ref) | copy-start | bytes 24580
  70.7 12.0 %copy-start.5 = (f32[1,1024]{1,0:T(1,128)S(1)}, f32[1,1024]{1,0:T(1,128)}, u32[]{:S(2)}) copy-start(f32[1,1024]{1,0:T(1,128)} %get-tuple-element.43.left_bias_ref) | copy-start | bytes 12292
  70.7 12.0 %copy-start.8 = (s32[8]{0:T(128)S(1)}, s32[8]{0:T(128)}, u32[]{:S(2)}) copy-start(s32[8]{0:T(128)} %copy-done.7) | copy-start | bytes 100

commit v10 on v9

--- a/solution.py
+++ b/solution.py
@@ -18,6 +18,7 @@
 WHOLE = 58 * MIB
 MOST = 51 * MIB
 MESSAGE = 48 * MIB
+SMALL = 48 * MIB
 ANSWER = 48 * MIB
 
 VM = pl.BlockSpec(memory_space=pltpu.VMEM)
@@ -293,7 +294,7 @@
     kept_hbm,
     previous_hbm,
     gates_hbm,
-    left_in_hbm,
+    left_in_ref,
     right_in_hbm,
     left_bias_ref,
     right_bias_ref,
@@ -314,15 +315,14 @@
     nodes = size_ref[1]
     steps = jnp.maximum(pl.cdiv(nodes, TILE), 1)
     half = width // 2
-    split = left_in_hbm.shape[1]
+    split = left_in_ref.shape[1]
     first_tile = pl.ds(0, TILE)
     halves = []
     for h in range(2):
         loads = [(gates_hbm.at[first_tile, pl.ds(h * 3 * half, 3 * half)], gates_ref.at[:, pl.ds(h * 3 * half, 3 * half)])]
-        for g in range(3):
-            first = g * width + h * half
-            part, at = (left_in_hbm, first) if first < split else (right_in_hbm, first - split)
-            loads.append((part.at[:, pl.ds(at, half)], gru_ref.at[:, pl.ds(first, half)]))
+        for g in range(1, 3):
+            cols = pl.ds(g * width + h * half - split, half)
+            loads.append((right_in_hbm.at[:, cols], gru_ref.at[:, cols]))
         if h == 0:
             loads.append((previous_hbm.at[first_tile], previous_ref))
         else:
@@ -364,12 +364,12 @@
     def renew(j):
         pre = []
         for g in range(3):
-            cols = slice(g * width + j * COLS, g * width + (j + 1) * COLS)
             hid = gates_ref[:, (j * 3 + g) * COLS : (j * 3 + g + 1) * COLS].astype(jnp.float32)
             first = g * width + j * COLS
             part, at = (left_bias_ref, first) if first < split else (right_bias_ref, first - split)
             bias = part[:, at : at + COLS]
-            into = jnp.dot(aggregate_ref[...], gru_ref[:, cols], preferred_element_type=jnp.float32) + bias
+            weight = (left_in_ref if first < split else gru_ref)[:, at : at + COLS]
+            into = jnp.dot(aggregate_ref[...], weight, preferred_element_type=jnp.float32) + bias
             pre.append((into, hid))
         reset = jax.nn.sigmoid(pre[0][0] + pre[0][1])
         update = jax.nn.sigmoid(pre[1][0] + pre[1][1])
@@ -580,14 +580,14 @@
 
     return pl.pallas_call(
         update_kernel,
-        out_shape=shape((node_rows, width), bf16),
-        in_specs=[SM, SM, SM, SM, VM, VM, HBM, HBM, HBM, HBM, HBM, VM, VM],
+        out_shape=pltpu.HBM((node_rows, width), bf16),
+        in_specs=[SM, SM, SM, SM, VM, VM, HBM, HBM, HBM, VM, HBM, VM, VM],
         out_specs=HBM,
         scratch_shapes=[
             pltpu.VMEM((node_rows, width), bf16),
             pltpu.VMEM((TILE, width), bf16),
             pltpu.VMEM((TILE, 3 * width), GATES),
-            pltpu.VMEM((width, 3 * width), bf16),
+            pltpu.VMEM((width, 2 * width), bf16),
             pltpu.VMEM(((padded + 1) * SUB, LANES), f32),
             pltpu.VMEM(((padded + 1) * SUB, LANES), f32),
             pltpu.VMEM((TILE, width), bf16),
@@ -595,7 +595,7 @@
             pltpu.SemaphoreType.DMA((2, 5)),
             pltpu.SemaphoreType.DMA((2,)),
         ],
-        compiler_params=pltpu.CompilerParams(vmem_limit_bytes=MOST),
+        compiler_params=pltpu.CompilerParams(vmem_limit_bytes=SMALL),
         name="update",
     )(
         slot,

time: 91.2 us -> 94 us (1.031)
  local copies, waits for them, and re-layouts: 6.17 us -> 9.16 us
    unnamed x23 -> x27, local copies, waits for them, and re-layouts: 3.35 us -> 6.37 us
  transfers between devices with their start and end apart: 3 -> 3, of which waited for: 3 -> 3; matrix products, arithmetic and copies ran while one was open for 6% -> 5% of each run, Pallas kernels for 33% -> 32%
where the time goes in v10:
time: 94 us; the launch traced here: 93.4 us
  Pallas kernels  46.2 us (49%)
  starting transfers between devices  20.8 us (22%)
  waiting for transfers between devices  17 us (18%)
  local copies, waits for them, and re-layouts  9.16 us (10%)
    pallas_call x2, Pallas kernels, fold(): pl.pallas_call(fold_kernel, out_shape=(shape((hid, last - first), bf16),...  14.5 us
    all_to_all x1, starting transfers between devices, on_device(): lax.all_to_all(ids.reshape(devices, 1, LANES), AXES, split_axis=0, concat...  11.1 us
    pallas_call x1, Pallas kernels, on_device(): pl.pallas_call(hidden_gates_kernel, out_shape=(shape((padded, width), bf1...  8.11 us
    pallas_call x1, Pallas kernels, on_device(): pl.pallas_call(update_kernel, out_shape=pltpu.HBM((node_rows, width), bf1...  7.64 us
    all_to_all x1, waiting for transfers between devices, on_device(): lax.all_to_all(ids.reshape(devices, 1, LANES), AXES, split_axis=0, concat...  7.25 us
    pallas_call x1, Pallas kernels, on_device(): pl.pallas_call(lambda *refs: compact_kernel(capacity, padded, *refs), out...  7.23 us
    unnamed x27, local copies, waits for them, and re-layouts  6.37 us
    all_to_all x1, waiting for transfers between devices, on_device(): lax.all_to_all(answers.reshape(devices, capacity, cells, LANES), AXES, sp...  5.85 us
  transfers between devices with their start and end apart: 3, of which 3 were waited for; matrix products, arithmetic and copies ran while one was open for 5% of the time, Pallas kernels for 32%

profile of v10, /device:TPU:0, one launch (start us, length us, event | category | flops | bytes accessed | tf_op | source)
XLA Modules:
  0.0 93.4 jit_solution(16920817303110570635)
XLA Ops:
  0.0 1.8 %plan.1 = (s32[128,128]{1,0:T(8,128)}, s32[2,256]{1,0:T(2,128)}) custom-call(s32[2,256]{1,0:T(2,128)} %bitcast.32, s32[2,256]{1,0:T(2,128)} %bitcast.33, s32[1,256]{1,0:T(1,128)} %bitcast.34), custom_call_target="tpu_custom_call" | custom-call | tf_op jit(solution)/shard_map/plan/pallas_call | solution.py:460
  1.8 11.1 %all-to-all-start = ((s32[128,1,128]{2,1,0:T(1,128)}), s32[128,1,128]{2,1,0:T(1,128)S(1)}, u32[]{:S(2)}, u32[]{:S(2)}) async-start(s32[128,1,128]{2,1,0:T(1,128)} %bitcast.27), calls=%async_computation | async-start | bytes 131072 | tf_op jit(solution)/shard_map/all_to_all | solution.py:469
  12.9 2.2 %copy.18 = bf16[128,8,8,128]{3,2,1,0:T(8,128)(2,1)S(1)} copy(bf16[128,8,8,128]{3,1,2,0:T(8,128)(2,1)} %bitcast.25) | data formatting | bytes 4194304
  15.1 0.0 copy-start
  15.1 7.3 %all-to-all-done = s32[128,1,128]{2,1,0:T(1,128)S(1)} async-done(((s32[128,1,128]{2,1,0:T(1,128)}), s32[128,1,128]{2,1,0:T(1,128)S(1)}, u32[]{:S(2)}, u32[]{:S(2)}) %all-to-all-start) | async-done | bytes 65568 | tf_op jit(solution)/shard_map/all_to_all | solution.py:469
  22.4 2.0 %answer.1 = (bf16[640,8,128]{2,1,0:T(8,128)(2,1)}, s32[8,128]{1,0:T(8,128)}) custom-call(s32[128,128]{1,0:T(8,128)S(1)} %bitcast.21, bf16[1024,8,128]{2,1,0:T(8,128)(2,1)S(1)} %bitcast.17), custom_call_target="tpu_custom_call" | custom-call | tf_op jit(solution)/shard_map/answer/pallas_call | solution.py:474
  24.4 0.0 copy-done
  24.4 4.7 %all-to-all-start.1 = ((bf16[128,5,8,128]{3,2,1,0:T(8,128)(2,1)}), bf16[128,5,8,128]{3,2,1,0:T(8,128)(2,1)S(1)}, u32[]{:S(2)}, u32[]{:S(2)}) async-start(bf16[128,5,8,128]{3,2,1,0:T(8,128)(2,1)} %bitcast.26), calls=%async_computation.1 | async-start | bytes 2621440 | tf_op jit(solution)/shard_map/all_to_all | solution.py:490
  29.0 1.8 %slice.3.w1_first_ref = bf16[1024,1024]{1,0:T(8,128)(2,1)S(1)} slice(bf16[2176,1024]{1,0:T(8,128)(2,1)} %w1_hbm.1), slice={[0:1024], [0:1024]} | slice | bytes 4194304 | tf_op jit(solution)/shard_map/slice | solution.py:575
  30.8 0.0 copy-start.11
  30.8 5.7 %fold.2 = (bf16[1024,1024]{1,0:T(8,128)(2,1)}, f32[1,1024]{1,0:T(1,128)}) custom-call(bf16[1024,1024]{1,0:T(8,128)(2,1)} %w2_ref.3, f32[1,1024]{1,0:T(1,128)} %bitcast.30, bf16[1024,3072]{1,0:T(8,128)(2,1)} %gru_ref.5, f32[1,3072]{1,0:T(1,128)} %bitcast.28), custom_call_target="tpu_custom_call" | custom-call | flops 2147483648 | bytes 4194304 | tf_op jit(solution)/shard_map/fold/pallas_call | solution.py:537
  36.6 0.0 copy-done.11
  36.6 0.0 copy-start.4
  36.6 0.0 copy-start.6
  36.6 0.0 copy-start.8
  36.6 7.2 %compact.1 = (s32[1024]{0:T(1024)S(1)}, s32[1024]{0:T(1024)S(1)}, s32[1024]{0:T(1024)S(1)}, s32[1024]{0:T(1024)S(1)}, s32[1024]{0:T(1024)S(1)}, /*index=5*/s32[8]{0:T(128)S(1)}) custom-call(s32[8,128]{1,0:T(8,128)S(1)} %copy-done.11), custom_call_target="tpu_custom_call" | custom-call | flops 4000000000 | bytes 20000000 | tf_op jit(solution)/shard_map/compact/pallas_call | solution.py:494
  43.8 0.0 copy-start.9
  43.8 0.5 copy-done.9
  44.4 0.0 copy-start.12
  44.4 0.6 copy-done.12
  45.0 5.8 %all-to-all-done.1 = bf16[128,5,8,128]{3,2,1,0:T(8,128)(2,1)S(1)} async-done(((bf16[128,5,8,128]{3,2,1,0:T(8,128)(2,1)}), bf16[128,5,8,128]{3,2,1,0:T(8,128)(2,1)S(1)}, u32[]{:S(2)}, u32[]{:S(2)}) %all-to-all-start.1) | async-done | bytes 1310752 | tf_op jit(solution)/shard_map/all_to_all | solution.py:490
  50.8 0.0 copy-done.4
  50.8 0.0 copy-done.6
  50.8 0.0 copy-done.8
  50.8 5.0 %message.1 = bf16[640,8,128]{2,1,0:T(8,128)(2,1)} custom-call(s32[2,256]{1,0:T(2,128)S(1)} %copy-done.8, bf16[640,8,128]{2,1,0:T(8,128)(2,1)S(1)} %bitcast.20, bf16[256,128]{1,0:T(8,128)(2,1)S(1)} %copy-done.4, bf16[1024,1024]{1,0:T(8,128)(2,1)S(1)} %slice.3.w1_first_ref, bf16[2176,1024]{1,0:T(8,128)(2,1)} %w1_hbm.1, f32[1,1024]{1,0:T(1,128)S(1)} %bitcast.22), custom_call_target="tpu_custom_call" | custom-call | tf_op jit(solution)/shard_map/message/pallas_call | solution.py:559
  55.8 5.0 %all-to-all-start.2 = ((bf16[128,5,8,128]{3,2,1,0:T(8,128)(2,1)}), bf16[128,5,8,128]{3,2,1,0:T(8,128)(2,1)S(1)}, u32[]{:S(2)}, u32[]{:S(2)}) async-start(bf16[128,5,8,128]{3,2,1,0:T(8,128)(2,1)} %bitcast.24), calls=%async_computation.2 | async-start | bytes 2621440 | tf_op jit(solution)/shard_map/all_to_all | solution.py:577
  60.8 8.7 %fold.3 = (bf16[1024,2048]{1,0:T(8,128)(2,1)}, f32[1,2048]{1,0:T(1,128)}) custom-call(bf16[1024,1024]{1,0:T(8,128)(2,1)} %w2_ref.3, f32[1,1024]{1,0:T(1,128)} %bitcast.31, bf16[1024,3072]{1,0:T(8,128)(2,1)} %gru_ref.5, f32[1,3072]{1,0:T(1,128)} %bitcast.29), custom_call_target="tpu_custom_call" | custom-call | flops 4294967296 | bytes 8388608 | tf_op jit(solution)/shard_map/fold/pallas_call | solution.py:537
  69.6 1.0 %copy.17.of_ref = s32[1024,1]{1,0:T(8,128)} copy(s32[1024,1]{0,1:T(1,128)S(1)} %bitcast.23) | data formatting | bytes 8192 | tf_op jit(solution)/shard_map/reshape | solution.py:512
  70.6 0.0 copy-start.2
  70.6 0.0 copy-start.5
  70.6 0.0 copy-start.7
  70.6 0.0 copy-start.10
  70.6 8.1 %hidden_gates.1 = (bf16[768,1024]{1,0:T(8,128)(2,1)}, bf16[768,3072]{1,0:T(8,128)(2,1)}, bf16[1024,1024]{1,0:T(8,128)(2,1)}) custom-call(s32[1024]{0:T(1024)} %copy-done.12, s32[8]{0:T(128)} %copy-done.9, bf16[1024,8,128]{2,1,0:T(8,128)(2,1)} %bitcast.18, bf16[1024,3072]{1,0:T(8,128)(2,1)} %gru_ref.4, bf16[1024,1024]{1,0:T(8,128)(2,1)} %plain_ref.1, ...), custom_call_target="tpu_custom_call" | custom-call | flops 4000000000 | bytes 20000000 | tf_op jit(solution)/shard_map/hidden_gates/pallas_call | solution.py:513
  78.7 3.9 %all-to-all-done.2 = bf16[128,5,8,128]{3,2,1,0:T(8,128)(2,1)S(1)} async-done(((bf16[128,5,8,128]{3,2,1,0:T(8,128)(2,1)}), bf16[128,5,8,128]{3,2,1,0:T(8,128)(2,1)S(1)}, u32[]{:S(2)}, u32[]{:S(2)}) %all-to-all-start.2) | async-done | bytes 1310752 | tf_op jit(solution)/shard_map/all_to_all | solution.py:577
  82.6 0.0 copy-done.2
  82.6 0.0 copy-done.5
  82.6 0.0 copy-done.7
  82.6 0.0 copy-done.10
  82.6 0.0 copy-start.1
  82.6 1.6 %copy-done.1 = bf16[1024,1024]{1,0:T(8,128)(2,1)S(1)} copy-done((bf16[1024,1024]{1,0:T(8,128)(2,1)S(1)}, bf16[1024,1024]{1,0:T(8,128)(2,1)}, u32[]{:S(2)}) %copy-start.1) | copy-done | bytes 2097176
  84.2 0.0 copy-start.3
  84.2 1.4 %copy-done.3 = bf16[768,1024]{1,0:T(8,128)(2,1)S(1)} copy-done((bf16[768,1024]{1,0:T(8,128)(2,1)S(1)}, bf16[768,1024]{1,0:T(8,128)(2,1)}, u32[]{:S(2)}) %copy-start.3) | copy-done | bytes 1572888
  85.6 7.6 %update.1 = bf16[1024,1024]{1,0:T(8,128)(2,1)} custom-call(s32[1024]{0:T(1024)S(1)} %get-tuple-element.27.slot_ref, s32[1024]{0:T(1024)S(1)} %get-tuple-element.28.index_ref, s32[1024]{0:T(1024)S(1)} %get-tuple-element.29.count_ref, s32[8]{0:T(128)S(1)} %copy-done.10, bf16[640,8,128]{2,1,0:T(8,128)(2,1)S(1)} %bitcast.19, s32[1024,1]{1,0:T(8,128)S(1)} %copy-done.2, ...), custom_call_target="tpu_custom_call" | custom-call | tf_op jit(solution)/shard_map/update/pallas_call | solution.py:581
Async XLA Ops:
  1.8 20.6 %all-to-all-start = ((s32[128,1,128]{2,1,0:T(1,128)}), s32[128,1,128]{2,1,0:T(1,128)S(1)}, u32[]{:S(2)}, u32[]{:S(2)}) async-start(s32[128,1,128]{2,1,0:T(1,128)} %bitcast.27), calls=%async_computation | async-start | bytes 131072 | tf_op jit(solution)/shard_map/all_to_all | solution.py:469
  15.1 9.2 %copy-start = (bf16[128,8,8,128]{3,2,1,0:T(8,128)(2,1)}, bf16[128,8,8,128]{3,2,1,0:T(8,128)(2,1)S(1)}, u32[]{:S(2)}) copy-start(bf16[128,8,8,128]{3,2,1,0:T(8,128)(2,1)S(1)} %copy.18) | copy-start | bytes 6291460
  24.4 26.4 %all-to-all-start.1 = ((bf16[128,5,8,128]{3,2,1,0:T(8,128)(2,1)}), bf16[128,5,8,128]{3,2,1,0:T(8,128)(2,1)S(1)}, u32[]{:S(2)}, u32[]{:S(2)}) async-start(bf16[128,5,8,128]{3,2,1,0:T(8,128)(2,1)} %bitcast.26), calls=%async_computation.1 | async-start | bytes 2621440 | tf_op jit(solution)/shard_map/all_to_all | solution.py:490
  30.8 5.8 %copy-start.11 = (s32[8,128]{1,0:T(8,128)S(1)}, s32[8,128]{1,0:T(8,128)}, u32[]{:S(2)}) copy-start(s32[8,128]{1,0:T(8,128)} %get-tuple-element.26.refs_0_) | copy-start | bytes 12292
  36.6 14.2 %copy-start.4 = (bf16[256,128]{1,0:T(8,128)(2,1)S(1)}, bf16[256,128]{1,0:T(8,128)(2,1)}, u32[]{:S(2)}) copy-start(bf16[256,128]{1,0:T(8,128)(2,1)} %feat_ref.1) | copy-start | bytes 196612
  36.6 14.2 %copy-start.6 = (f32[1024]{0:T(1024)S(1)}, f32[1024]{0:T(1024)}, u32[]{:S(2)}) copy-start(f32[1024]{0:T(1024)} %param.18) | copy-start | bytes 12292
  36.6 14.2 %copy-start.8 = (s32[2,256]{1,0:T(2,128)S(1)}, s32[2,256]{1,0:T(2,128)}, u32[]{:S(2)}) copy-start(s32[2,256]{1,0:T(2,128)} %get-tuple-element.34.place_ref) | copy-start | bytes 6148
  43.8 0.5 copy-start.9
  44.4 0.6 copy-start.12
  55.8 26.8 %all-to-all-start.2 = ((bf16[128,5,8,128]{3,2,1,0:T(8,128)(2,1)}), bf16[128,5,8,128]{3,2,1,0:T(8,128)(2,1)S(1)}, u32[]{:S(2)}, u32[]{:S(2)}) async-start(bf16[128,5,8,128]{3,2,1,0:T(8,128)(2,1)} %bitcast.24), calls=%async_computation.2 | async-start | bytes 2621440 | tf_op jit(solution)/shard_map/all_to_all | solution.py:577
  70.6 12.0 %copy-start.2 = (s32[1024,1]{1,0:T(8,128)S(1)}, s32[1024,1]{1,0:T(8,128)}, u32[]{:S(2)}) copy-start(s32[1024,1]{1,0:T(8,128)} %copy.17.of_ref) | copy-start | bytes 12292
  70.6 12.0 %copy-start.5 = (f32[1,2048]{1,0:T(1,128)S(1)}, f32[1,2048]{1,0:T(1,128)}, u32[]{:S(2)}) copy-start(f32[1,2048]{1,0:T(1,128)} %get-tuple-element.44.right_bias_ref) | copy-start | bytes 24580
  70.6 12.0 %copy-start.7 = (f32[1,1024]{1,0:T(1,128)S(1)}, f32[1,1024]{1,0:T(1,128)}, u32[]{:S(2)}) copy-start(f32[1,1024]{1,0:T(1,128)} %get-tuple-element.43.left_bias_ref) | copy-start | bytes 12292
  70.6 12.0 %copy-start.10 = (s32[8]{0:T(128)S(1)}, s32[8]{0:T(128)}, u32[]{:S(2)}) copy-start(s32[8]{0:T(128)} %copy-done.9) | copy-start | bytes 100
  82.6 1.6 %copy-start.1 = (bf16[1024,1024]{1,0:T(8,128)(2,1)S(1)}, bf16[1024,1024]{1,0:T(8,128)(2,1)}, u32[]{:S(2)}) copy-start(bf16[1024,1024]{1,0:T(8,128)(2,1)} %get-tuple-element.38.kept_hbm) | copy-start | bytes 6291460
  84.2 1.4 %copy-start.3 = (bf16[768,1024]{1,0:T(8,128)(2,1)S(1)}, bf16[768,1024]{1,0:T(8,128)(2,1)}, u32[]{:S(2)}) copy-start(bf16[768,1024]{1,0:T(8,128)(2,1)} %get-tuple-element.39.previous_hbm) | copy-start | bytes 4718596

commit v11 on v9

--- a/solution.py
+++ b/solution.py
@@ -482,7 +482,7 @@
             pltpu.SMEM((SUB, devices), i32),
             pltpu.VMEM((slots, cells, LANES), bf16),
             pltpu.SemaphoreType.DMA,
-            pltpu.SemaphoreType.DMA((4,)),
+            pltpu.SemaphoreType.DMA((8,)),
         ],
         compiler_params=pltpu.CompilerParams(vmem_limit_bytes=ANSWER),
         name="answer",

time: 91.2 us -> 91.4 us (level)
  no operation moved by 1% of the time
where the time goes in v11:
time: 91.4 us; the launch traced here: 90.9 us
  Pallas kernels  46.4 us (51%)
  starting transfers between devices  21 us (23%)
  waiting for transfers between devices  17 us (19%)
  local copies, waits for them, and re-layouts  6.17 us (7%)
    pallas_call x2, Pallas kernels, fold(): pl.pallas_call(fold_kernel, out_shape=(shape((hid, last - first), bf16),...  14.5 us
    all_to_all x1, starting transfers between devices, on_device(): lax.all_to_all(ids.reshape(devices, 1, LANES), AXES, split_axis=0, concat...  11.1 us
    pallas_call x1, Pallas kernels, on_device(): pl.pallas_call(hidden_gates_kernel, out_shape=(shape((padded, width), bf1...  8.12 us
    pallas_call x1, Pallas kernels, on_device(): pl.pallas_call(update_kernel, out_shape=shape((node_rows, width), bf16),...  8.03 us
    all_to_all x1, waiting for transfers between devices, on_device(): lax.all_to_all(ids.reshape(devices, 1, LANES), AXES, split_axis=0, concat...  7.24 us
    pallas_call x1, Pallas kernels, on_device(): pl.pallas_call(lambda *refs: compact_kernel(capacity, padded, *refs), out...  7.18 us
    all_to_all x1, waiting for transfers between devices, on_device(): lax.all_to_all(answers.reshape(devices, capacity, cells, LANES), AXES, sp...  5.93 us
    all_to_all x1, starting transfers between devices, on_device(): lax.all_to_all(outgoing.reshape(devices, capacity, cells, LANES), AXES, s...  5.2 us
  transfers between devices with their start and end apart: 3, of which 3 were waited for; matrix products, arithmetic and copies ran while one was open for 6% of the time, Pallas kernels for 33%

profile of v11, /device:TPU:0, one launch (start us, length us, event | category | flops | bytes accessed | tf_op | source)
XLA Modules:
  0.0 90.9 jit_solution(11789468735584065111)
XLA Ops:
  0.0 1.8 %plan.1 = (s32[128,128]{1,0:T(8,128)}, s32[2,256]{1,0:T(2,128)}) custom-call(s32[2,256]{1,0:T(2,128)} %bitcast.32, s32[2,256]{1,0:T(2,128)} %bitcast.33, s32[1,256]{1,0:T(1,128)} %bitcast.34), custom_call_target="tpu_custom_call" | custom-call | tf_op jit(solution)/shard_map/plan/pallas_call | solution.py:460
  1.8 11.1 %all-to-all-start = ((s32[128,1,128]{2,1,0:T(1,128)}), s32[128,1,128]{2,1,0:T(1,128)S(1)}, u32[]{:S(2)}, u32[]{:S(2)}) async-start(s32[128,1,128]{2,1,0:T(1,128)} %bitcast.27), calls=%async_computation | async-start | bytes 131072 | tf_op jit(solution)/shard_map/all_to_all | solution.py:469
  12.9 2.2 %copy.18 = bf16[128,8,8,128]{3,2,1,0:T(8,128)(2,1)S(1)} copy(bf16[128,8,8,128]{3,1,2,0:T(8,128)(2,1)} %bitcast.25) | data formatting | bytes 4194304
  15.1 0.0 copy-start
  15.1 7.2 %all-to-all-done = s32[128,1,128]{2,1,0:T(1,128)S(1)} async-done(((s32[128,1,128]{2,1,0:T(1,128)}), s32[128,1,128]{2,1,0:T(1,128)S(1)}, u32[]{:S(2)}, u32[]{:S(2)}) %all-to-all-start) | async-done | bytes 65568 | tf_op jit(solution)/shard_map/all_to_all | solution.py:469
  22.4 1.9 %answer.1 = (bf16[640,8,128]{2,1,0:T(8,128)(2,1)}, s32[8,128]{1,0:T(8,128)}) custom-call(s32[128,128]{1,0:T(8,128)S(1)} %bitcast.21, bf16[1024,8,128]{2,1,0:T(8,128)(2,1)S(1)} %bitcast.17), custom_call_target="tpu_custom_call" | custom-call | tf_op jit(solution)/shard_map/answer/pallas_call | solution.py:474
  24.3 0.0 copy-done
  24.3 4.7 %all-to-all-start.1 = ((bf16[128,5,8,128]{3,2,1,0:T(8,128)(2,1)}), bf16[128,5,8,128]{3,2,1,0:T(8,128)(2,1)S(1)}, u32[]{:S(2)}, u32[]{:S(2)}) async-start(bf16[128,5,8,128]{3,2,1,0:T(8,128)(2,1)} %bitcast.26), calls=%async_computation.1 | async-start | bytes 2621440 | tf_op jit(solution)/shard_map/all_to_all | solution.py:490
  29.0 1.8 %slice.3.w1_first_ref = bf16[1024,1024]{1,0:T(8,128)(2,1)S(1)} slice(bf16[2176,1024]{1,0:T(8,128)(2,1)} %w1_hbm.1), slice={[0:1024], [0:1024]} | slice | bytes 4194304 | tf_op jit(solution)/shard_map/slice | solution.py:575
  30.8 0.0 copy-start.9
  30.8 5.7 %fold.2 = (bf16[1024,1024]{1,0:T(8,128)(2,1)}, f32[1,1024]{1,0:T(1,128)}) custom-call(bf16[1024,1024]{1,0:T(8,128)(2,1)} %w2_ref.3, f32[1,1024]{1,0:T(1,128)} %bitcast.30, bf16[1024,3072]{1,0:T(8,128)(2,1)} %gru_ref.5, f32[1,3072]{1,0:T(1,128)} %bitcast.28), custom_call_target="tpu_custom_call" | custom-call | flops 2147483648 | bytes 4194304 | tf_op jit(solution)/shard_map/fold/pallas_call | solution.py:537
  36.5 0.0 copy-done.9
  36.5 0.0 copy-start.2
  36.5 0.0 copy-start.4
  36.5 0.0 copy-start.6
  36.5 7.2 %compact.1 = (s32[1024]{0:T(1024)S(1)}, s32[1024]{0:T(1024)S(1)}, s32[1024]{0:T(1024)S(1)}, s32[1024]{0:T(1024)S(1)}, s32[1024]{0:T(1024)S(1)}, /*index=5*/s32[8]{0:T(128)S(1)}) custom-call(s32[8,128]{1,0:T(8,128)S(1)} %copy-done.9), custom_call_target="tpu_custom_call" | custom-call | flops 4000000000 | bytes 20000000 | tf_op jit(solution)/shard_map/compact/pallas_call | solution.py:494
  43.7 0.0 copy-start.7
  43.7 0.5 copy-done.7
  44.2 0.0 copy-start.10
  44.2 0.6 copy-done.10
  44.8 5.9 %all-to-all-done.1 = bf16[128,5,8,128]{3,2,1,0:T(8,128)(2,1)S(1)} async-done(((bf16[128,5,8,128]{3,2,1,0:T(8,128)(2,1)}), bf16[128,5,8,128]{3,2,1,0:T(8,128)(2,1)S(1)}, u32[]{:S(2)}, u32[]{:S(2)}) %all-to-all-start.1) | async-done | bytes 1310752 | tf_op jit(solution)/shard_map/all_to_all | solution.py:490
  50.8 0.0 copy-done.2
  50.8 0.0 copy-done.4
  50.8 0.0 copy-done.6
  50.8 5.0 %message.1 = bf16[640,8,128]{2,1,0:T(8,128)(2,1)} custom-call(s32[2,256]{1,0:T(2,128)S(1)} %copy-done.6, bf16[640,8,128]{2,1,0:T(8,128)(2,1)S(1)} %bitcast.20, bf16[256,128]{1,0:T(8,128)(2,1)S(1)} %copy-done.2, bf16[1024,1024]{1,0:T(8,128)(2,1)S(1)} %slice.3.w1_first_ref, bf16[2176,1024]{1,0:T(8,128)(2,1)} %w1_hbm.1, f32[1,1024]{1,0:T(1,128)S(1)} %bitcast.22), custom_call_target="tpu_custom_call" | custom-call | tf_op jit(solution)/shard_map/message/pallas_call | solution.py:559
  55.7 5.2 %all-to-all-start.2 = ((bf16[128,5,8,128]{3,2,1,0:T(8,128)(2,1)}), bf16[128,5,8,128]{3,2,1,0:T(8,128)(2,1)S(1)}, u32[]{:S(2)}, u32[]{:S(2)}) async-start(bf16[128,5,8,128]{3,2,1,0:T(8,128)(2,1)} %bitcast.24), calls=%async_computation.2 | async-start | bytes 2621440 | tf_op jit(solution)/shard_map/all_to_all | solution.py:577
  61.0 8.7 %fold.3 = (bf16[1024,2048]{1,0:T(8,128)(2,1)}, f32[1,2048]{1,0:T(1,128)}) custom-call(bf16[1024,1024]{1,0:T(8,128)(2,1)} %w2_ref.3, f32[1,1024]{1,0:T(1,128)} %bitcast.31, bf16[1024,3072]{1,0:T(8,128)(2,1)} %gru_ref.5, f32[1,3072]{1,0:T(1,128)} %bitcast.29), custom_call_target="tpu_custom_call" | custom-call | flops 4294967296 | bytes 8388608 | tf_op jit(solution)/shard_map/fold/pallas_call | solution.py:537
  69.7 1.1 %copy.17.of_ref = s32[1024,1]{1,0:T(8,128)} copy(s32[1024,1]{0,1:T(1,128)S(1)} %bitcast.23) | data formatting | bytes 8192 | tf_op jit(solution)/shard_map/reshape | solution.py:512
  70.7 0.0 copy-start.1
  70.7 0.0 copy-start.3
  70.7 0.0 copy-start.5
  70.8 0.0 copy-start.8
  70.8 8.1 %hidden_gates.1 = (bf16[768,1024]{1,0:T(8,128)(2,1)}, bf16[768,3072]{1,0:T(8,128)(2,1)}, bf16[1024,1024]{1,0:T(8,128)(2,1)}) custom-call(s32[1024]{0:T(1024)} %copy-done.10, s32[8]{0:T(128)} %copy-done.7, bf16[1024,8,128]{2,1,0:T(8,128)(2,1)} %bitcast.18, bf16[1024,3072]{1,0:T(8,128)(2,1)} %gru_ref.4, bf16[1024,1024]{1,0:T(8,128)(2,1)} %plain_ref.1, ...), custom_call_target="tpu_custom_call" | custom-call | flops 4000000000 | bytes 20000000 | tf_op jit(solution)/shard_map/hidden_gates/pallas_call | solution.py:513
  78.9 3.8 %all-to-all-done.2 = bf16[128,5,8,128]{3,2,1,0:T(8,128)(2,1)S(1)} async-done(((bf16[128,5,8,128]{3,2,1,0:T(8,128)(2,1)}), bf16[128,5,8,128]{3,2,1,0:T(8,128)(2,1)S(1)}, u32[]{:S(2)}, u32[]{:S(2)}) %all-to-all-start.2) | async-done | bytes 1310752 | tf_op jit(solution)/shard_map/all_to_all | solution.py:577
  82.7 0.0 copy-done.1
  82.7 0.0 copy-done.3
  82.7 0.0 copy-done.5
  82.7 0.0 copy-done.8
  82.7 8.0 %update.1 = bf16[1024,1024]{1,0:T(8,128)(2,1)} custom-call(s32[1024]{0:T(1024)S(1)} %get-tuple-element.27.slot_ref, s32[1024]{0:T(1024)S(1)} %get-tuple-element.28.index_ref, s32[1024]{0:T(1024)S(1)} %get-tuple-element.29.count_ref, s32[8]{0:T(128)S(1)} %copy-done.8, bf16[640,8,128]{2,1,0:T(8,128)(2,1)S(1)} %bitcast.19, s32[1024,1]{1,0:T(8,128)S(1)} %copy-done.1, ...), custom_call_target="tpu_custom_call" | custom-call | tf_op jit(solution)/shard_map/update/pallas_call | solution.py:581
Async XLA Ops:
  1.8 20.6 %all-to-all-start = ((s32[128,1,128]{2,1,0:T(1,128)}), s32[128,1,128]{2,1,0:T(1,128)S(1)}, u32[]{:S(2)}, u32[]{:S(2)}) async-start(s32[128,1,128]{2,1,0:T(1,128)} %bitcast.27), calls=%async_computation | async-start | bytes 131072 | tf_op jit(solution)/shard_map/all_to_all | solution.py:469
  15.1 9.2 %copy-start = (bf16[128,8,8,128]{3,2,1,0:T(8,128)(2,1)}, bf16[128,8,8,128]{3,2,1,0:T(8,128)(2,1)S(1)}, u32[]{:S(2)}) copy-start(bf16[128,8,8,128]{3,2,1,0:T(8,128)(2,1)S(1)} %copy.18) | copy-start | bytes 6291460
  24.3 26.4 %all-to-all-start.1 = ((bf16[128,5,8,128]{3,2,1,0:T(8,128)(2,1)}), bf16[128,5,8,128]{3,2,1,0:T(8,128)(2,1)S(1)}, u32[]{:S(2)}, u32[]{:S(2)}) async-start(bf16[128,5,8,128]{3,2,1,0:T(8,128)(2,1)} %bitcast.26), calls=%async_computation.1 | async-start | bytes 2621440 | tf_op jit(solution)/shard_map/all_to_all | solution.py:490
  30.8 5.7 %copy-start.9 = (s32[8,128]{1,0:T(8,128)S(1)}, s32[8,128]{1,0:T(8,128)}, u32[]{:S(2)}) copy-start(s32[8,128]{1,0:T(8,128)} %get-tuple-element.26.refs_0_) | copy-start | bytes 12292
  36.5 14.3 %copy-start.2 = (bf16[256,128]{1,0:T(8,128)(2,1)S(1)}, bf16[256,128]{1,0:T(8,128)(2,1)}, u32[]{:S(2)}) copy-start(bf16[256,128]{1,0:T(8,128)(2,1)} %feat_ref.1) | copy-start | bytes 196612
  36.5 14.3 %copy-start.4 = (f32[1024]{0:T(1024)S(1)}, f32[1024]{0:T(1024)}, u32[]{:S(2)}) copy-start(f32[1024]{0:T(1024)} %param.18) | copy-start | bytes 12292
  36.5 14.2 %copy-start.6 = (s32[2,256]{1,0:T(2,128)S(1)}, s32[2,256]{1,0:T(2,128)}, u32[]{:S(2)}) copy-start(s32[2,256]{1,0:T(2,128)} %get-tuple-element.34.place_ref) | copy-start | bytes 6148
  43.7 0.5 copy-start.7
  44.2 0.6 copy-start.10
  55.7 27.0 %all-to-all-start.2 = ((bf16[128,5,8,128]{3,2,1,0:T(8,128)(2,1)}), bf16[128,5,8,128]{3,2,1,0:T(8,128)(2,1)S(1)}, u32[]{:S(2)}, u32[]{:S(2)}) async-start(bf16[128,5,8,128]{3,2,1,0:T(8,128)(2,1)} %bitcast.24), calls=%async_computation.2 | async-start | bytes 2621440 | tf_op jit(solution)/shard_map/all_to_all | solution.py:577
  70.7 12.0 %copy-start.1 = (s32[1024,1]{1,0:T(8,128)S(1)}, s32[1024,1]{1,0:T(8,128)}, u32[]{:S(2)}) copy-start(s32[1024,1]{1,0:T(8,128)} %copy.17.of_ref) | copy-start | bytes 12292
  70.7 12.0 %copy-start.3 = (f32[1,2048]{1,0:T(1,128)S(1)}, f32[1,2048]{1,0:T(1,128)}, u32[]{:S(2)}) copy-start(f32[1,2048]{1,0:T(1,128)} %get-tuple-element.44.right_bias_ref) | copy-start | bytes 24580
  70.7 12.0 %copy-start.5 = (f32[1,1024]{1,0:T(1,128)S(1)}, f32[1,1024]{1,0:T(1,128)}, u32[]{:S(2)}) copy-start(f32[1,1024]{1,0:T(1,128)} %get-tuple-element.43.left_bias_ref) | copy-start | bytes 12292
  70.8 12.0 %copy-start.8 = (s32[8]{0:T(128)S(1)}, s32[8]{0:T(128)}, u32[]{:S(2)}) copy-start(s32[8]{0:T(128)} %copy-done.7) | copy-start | bytes 100
